TPU v7x, 32 devices: a whole 2x2x4 slice. The times are simulated.
32 devices in a mesh: dp: 4 (over z), ctx: 4 (over x, core), uly: 2 (over y).
Axes of the slice: x: 2, y: 2, z: 4, core: 2. Of those that a mesh axis runs over, the one named last changes fastest.
Arguments:
- queries: bfloat16 [4096, 4096], P(('dp', 'ctx', 'uly')), parts along dimension 0, may hold values from -130 to 130
- keys: bfloat16 [4096, 1024], P(('dp', 'ctx', 'uly')), parts along dimension 0, may hold values from -6.5 to 6.5
- values: bfloat16 [4096, 1024], P(('dp', 'ctx', 'uly')), parts along dimension 0, may hold values from -6 to 6
- d_out: bfloat16 [4096, 4096], P(('dp', 'ctx', 'uly')), parts along dimension 0, may hold values from -96 to 96
- rand_blocks: int32 [32, 3], P('dp'), parts along dimension 0, may hold values from 0 to 7, as said below
Outputs:
- d_queries: bfloat16 [4096, 4096], P(('dp', 'ctx', 'uly')), parts along dimension 0
- d_keys: bfloat16 [4096, 1024], P(('dp', 'ctx', 'uly')), parts along dimension 0
- d_values: bfloat16 [4096, 1024], P(('dp', 'ctx', 'uly')), parts along dimension 0
There are 4 independent parts, one for each index of `dp`. A program takes and returns all parts, laid end to end along the dimension named above; each array names one. Nothing has to cross between parts.
Inputs may be any that keep to these rules, and one draw needn't show every extreme that they name: `rand_blocks`: for every group of 2 consecutive query blocks, the entries of its lists (window, random) that name blocks of one other group of 2 number at most 2, and at most 4 when the 2 global blocks are counted once each; both bounds are reached in every draw.
All inputs are finite; a program needn't handle non-finite values.
Results may differ from a plain program's by a relative error of at most 0.005.
Values may be sent and summed in bfloat16 or wider, within the bound.
No kernel may reach another device: no remote copies, remote signals or barrier semaphores. Data moves between devices by JAX's collectives and lax.ppermute only.
A program may use at most 128 MiB of HBM per device.

v0:
```python
from functools import partial

import jax
import jax.numpy as jnp
from jax import lax
from jax.sharding import PartitionSpec as P

HEAD_DIM = 128
BLOCK = 128
WINDOW = 3
GLOBALS = 2
RANDOMS = 3
ENTRIES = 8
GROUP = 4


def listed_blocks(rand_blocks):
    total = rand_blocks.shape[0]
    block_ids = jnp.arange(total, dtype=jnp.int32)
    window_part = (
        block_ids[:, None] + jnp.arange(WINDOW, dtype=jnp.int32)[None, :] - WINDOW // 2
    ) % total
    global_part = jnp.broadcast_to(jnp.arange(GLOBALS, dtype=jnp.int32)[None, :], (total, GLOBALS))
    return jnp.concatenate([window_part, global_part, rand_blocks], axis=1)


def block_backward(sources, softmax_scale, inputs):
    query_blk, dout_blk, source_rows = inputs
    picked = jnp.take(sources, source_rows, axis=0)
    kv_width = picked.shape[-1] // 2
    kv_count = kv_width // HEAD_DIM
    key_sel = picked[..., :kv_width].reshape(ENTRIES, BLOCK, kv_count, HEAD_DIM)
    value_sel = picked[..., kv_width:].reshape(ENTRIES, BLOCK, kv_count, HEAD_DIM)
    query_four = query_blk.reshape(BLOCK, kv_count, GROUP, HEAD_DIM)
    dout_four = dout_blk.reshape(BLOCK, kv_count, GROUP, HEAD_DIM)
    scores = jnp.einsum("tkgd,eskd->kgtes", query_four, key_sel, preferred_element_type=jnp.float32)
    scores = scores.reshape(kv_count, GROUP, BLOCK, ENTRIES * BLOCK) * softmax_scale
    row_max = jnp.max(scores, axis=-1, keepdims=True)
    exp_scores = jnp.exp(scores - row_max)
    prob_rows = exp_scores / jnp.sum(exp_scores, axis=-1, keepdims=True)
    grad_probs = jnp.einsum(
        "tkgd,eskd->kgtes", dout_four, value_sel, preferred_element_type=jnp.float32
    )
    grad_probs = grad_probs.reshape(kv_count, GROUP, BLOCK, ENTRIES * BLOCK)
    row_delta = jnp.sum(prob_rows * grad_probs, axis=-1, keepdims=True)
    grad_scores = (
        (prob_rows * (grad_probs - row_delta))
        .astype(jnp.bfloat16)
        .reshape(kv_count, GROUP, BLOCK, ENTRIES, BLOCK)
    )
    probs_low = prob_rows.astype(jnp.bfloat16).reshape(kv_count, GROUP, BLOCK, ENTRIES, BLOCK)
    grad_values = jnp.einsum(
        "kgtes,tkgd->eskd", probs_low, dout_four, preferred_element_type=jnp.float32
    )
    grad_keys = (
        jnp.einsum("kgtes,tkgd->eskd", grad_scores, query_four, preferred_element_type=jnp.float32)
        * softmax_scale
    )
    grad_query = (
        jnp.einsum("kgtes,eskd->tkgd", grad_scores, key_sel, preferred_element_type=jnp.float32)
        * softmax_scale
    )
    partials = jnp.concatenate(
        [
            grad_keys.reshape(ENTRIES, BLOCK, kv_width),
            grad_values.reshape(ENTRIES, BLOCK, kv_width),
        ],
        axis=-1,
    )
    return (partials, grad_query.reshape(BLOCK, kv_count * GROUP * HEAD_DIM))


def per_device(queries, keys, values, d_out, rand_blocks):
    softmax_scale = HEAD_DIM ** (-0.5)
    groups = lax.axis_size("ctx")
    my_group = lax.axis_index("ctx")
    queries_here, dout_here, keys_here, values_here = (
        lax.all_to_all(queries, "uly", split_axis=1, concat_axis=0, tiled=True),
        lax.all_to_all(d_out, "uly", split_axis=1, concat_axis=0, tiled=True),
        lax.all_to_all(keys, "uly", split_axis=1, concat_axis=0, tiled=True),
        lax.all_to_all(values, "uly", split_axis=1, concat_axis=0, tiled=True),
    )
    tokens_here = keys_here.shape[0]
    per_group = tokens_here // BLOCK
    kv_width = keys_here.shape[1]
    local_blocks = jnp.concatenate([keys_here, values_here], axis=1).reshape(
        per_group, BLOCK, 2 * kv_width
    )
    listed = listed_blocks(rand_blocks)
    owners = listed // per_group
    offsets = listed % per_group
    requester = (jnp.arange(listed.shape[0], dtype=jnp.int32) // per_group)[:, None]
    entry_ids = jnp.arange(ENTRIES, dtype=jnp.int32)
    is_global = (entry_ids >= WINDOW) & (entry_ids < WINDOW + GLOBALS)
    entry_global = jnp.tile(is_global, per_group)
    global_slot = jnp.tile(entry_ids - WINDOW, per_group)
    rand_capacity = per_group * RANDOMS // groups + 1
    remote = owners != requester
    capacity = rand_capacity + GLOBALS
    lead_slots = GLOBALS
    owners = owners.reshape(groups, per_group * ENTRIES)
    offsets = offsets.reshape(groups, per_group * ENTRIES)
    remote = remote.reshape(groups, per_group * ENTRIES)
    counted = remote & jnp.logical_not(entry_global)[None, :]
    owner_hot = (
        (owners[:, :, None] == jnp.arange(groups, dtype=jnp.int32)[None, None, :])
        & counted[:, :, None]
    ).astype(jnp.int32)
    rand_slot = jnp.sum((jnp.cumsum(owner_hot, axis=1) - 1) * owner_hot, axis=2) + lead_slots
    slot_index = jnp.where(entry_global[None, :], global_slot[None, :], rand_slot)
    for_me = remote & (owners == my_group)
    slot_match = (
        slot_index[:, :, None, None] == jnp.arange(capacity, dtype=jnp.int32)[None, None, :, None]
    )
    block_match = (
        offsets[:, :, None, None] == jnp.arange(per_group, dtype=jnp.int32)[None, None, None, :]
    )
    slot_picker = jnp.minimum(
        jnp.sum((for_me[:, :, None, None] & slot_match & block_match).astype(jnp.int32), axis=1), 1
    )
    outgoing = jnp.einsum(
        "csb,bxd->csxd",
        slot_picker.astype(jnp.bfloat16),
        local_blocks,
        preferred_element_type=jnp.float32,
    ).astype(jnp.bfloat16)
    incoming = lax.all_to_all(outgoing, "ctx", split_axis=0, concat_axis=0, tiled=True)
    my_owner = lax.dynamic_index_in_dim(owners, my_group, 0, keepdims=False)
    my_slot = lax.dynamic_index_in_dim(slot_index, my_group, 0, keepdims=False)
    my_offset = lax.dynamic_index_in_dim(offsets, my_group, 0, keepdims=False)
    my_remote = lax.dynamic_index_in_dim(remote, my_group, 0, keepdims=False)
    source_rows = jnp.where(my_remote, per_group + my_owner * capacity + my_slot, my_offset)
    pieces = [local_blocks, incoming.reshape(groups * capacity, BLOCK, 2 * kv_width)]
    sources = jnp.concatenate(pieces, axis=0)
    source_count = sources.shape[0]
    query_blocks = queries_here.reshape(per_group, BLOCK, queries_here.shape[1])
    dout_blocks = dout_here.reshape(per_group, BLOCK, dout_here.shape[1])
    partials, grad_query = lax.map(
        partial(block_backward, sources, softmax_scale),
        (query_blocks, dout_blocks, source_rows.reshape(per_group, ENTRIES)),
    )
    source_hot = (
        source_rows[:, None] == jnp.arange(source_count, dtype=jnp.int32)[None, :]
    ).astype(jnp.float32)
    source_grads = jnp.einsum(
        "ms,mxd->sxd",
        source_hot,
        partials.reshape(per_group * ENTRIES, BLOCK, 2 * kv_width),
        precision=lax.Precision.HIGHEST,
    )
    own_grads = source_grads[:per_group]
    sent_grads = source_grads[per_group : per_group + groups * capacity].reshape(
        groups, capacity, BLOCK, 2 * kv_width
    )
    returned = lax.all_to_all(sent_grads, "ctx", split_axis=0, concat_axis=0, tiled=True)
    own_grads = own_grads + jnp.einsum(
        "csb,csxd->bxd", slot_picker.astype(jnp.float32), returned, precision=lax.Precision.HIGHEST
    )
    query_grads = grad_query.reshape(tokens_here, queries_here.shape[1]).astype(jnp.bfloat16)
    key_grads = own_grads[..., :kv_width].reshape(tokens_here, kv_width).astype(jnp.bfloat16)
    value_grads = own_grads[..., kv_width:].reshape(tokens_here, kv_width).astype(jnp.bfloat16)
    d_queries, d_keys, d_values = (
        lax.all_to_all(query_grads, "uly", split_axis=0, concat_axis=1, tiled=True),
        lax.all_to_all(key_grads, "uly", split_axis=0, concat_axis=1, tiled=True),
        lax.all_to_all(value_grads, "uly", split_axis=0, concat_axis=1, tiled=True),
    )
    return (d_queries, d_keys, d_values)


def solution(mesh):
    in_specs = (
        P(("dp", "ctx", "uly"), None),
        P(("dp", "ctx", "uly"), None),
        P(("dp", "ctx", "uly"), None),
        P(("dp", "ctx", "uly"), None),
        P("dp", None),
    )
    out_specs = (
        P(("dp", "ctx", "uly"), None),
        P(("dp", "ctx", "uly"), None),
        P(("dp", "ctx", "uly"), None),
    )
    return jax.shard_map(
        per_device, mesh=mesh, in_specs=in_specs, out_specs=out_specs, check_vma=False
    )
```

profile of v0, /device:TPU:0, one launch (start us, length us, event | category | flops | bytes accessed | tf_op | source)
XLA Modules:
  0.0 362.4 jit_solution(10996990037546857192)
XLA Ops:
  2.6 4.2 %all-to-all-start.2 = ((bf16[128,2,512]{2,0,1:T(8,128)(2,1)}), bf16[128,2,512]{2,0,1:T(8,128)(2,1)S(1)}, u32[]{:S(2)}, u32[]{:S(2)}) async-start(bf16[128,2,512]{2,0,1:T(8,128)(2,1)} %copy.130), calls=%async_computation.2 | async-start | bytes 524288 | tf_op jit(solution)/shard_map/all_to_all | solution.py:81
  10.5 2.3 copy.124
  12.7 3.5 all-to-all-start.1
  16.2 5.8 %all-to-all-done.1 = bf16[128,2,512]{2,0,1:T(8,128)(2,1)S(1)} async-done(((bf16[128,2,512]{2,0,1:T(8,128)(2,1)}), bf16[128,2,512]{2,0,1:T(8,128)(2,1)S(1)}, u32[]{:S(2)}, u32[]{:S(2)}) %all-to-all-start.1) | async-done | bytes 262176 | tf_op jit(solution)/shard_map/all_to_all | solution.py:80
  22.1 4.4 %all-to-all-start = ((bf16[128,2,2048]{0,2,1:T(8,128)(2,1)}), bf16[128,2,2048]{0,2,1:T(8,128)(2,1)}, u32[]{:S(2)}, u32[]{:S(2)}) async-start(bf16[128,2,2048]{0,2,1:T(8,128)(2,1)} %bitcast.31), calls=%async_computation | async-start | bytes 2097152 | tf_op jit(solution)/shard_map/all_to_all | solution.py:78
  27.4 4.4 %convolution_convert_fusion = bf16[4,4,128,1024]{3,1,2,0:T(4,128)(2,1)} fusion(s32[4,4,2]{1,2,0:T(2,128)S(1)} %convert_reduce_fusion, bf16[2,128,512]{2,0,1:T(2,128)(2,1)S(1)} %bitcast.211, bf16[2,128,512]{2,0,1:T(2,128)(2,1)S(1)} %bitcast.213), kind=kOutput, calls=%fused_computation.38 | convolution fusion | flops 11534400 | bytes 4718720 | tf_op jit(solution)/shard_map/csb,bxd->csxd/dot_general | solution.py:121
  31.8 8.1 %all-to-all-done = bf16[128,2,2048]{0,2,1:T(8,128)(2,1)} async-done(((bf16[128,2,2048]{0,2,1:T(8,128)(2,1)}), bf16[128,2,2048]{0,2,1:T(8,128)(2,1)}, u32[]{:S(2)}, u32[]{:S(2)}) %all-to-all-start) | async-done | bytes 1048608 | tf_op jit(solution)/shard_map/all_to_all | solution.py:78
  39.9 4.9 %all-to-all-start.3 = ((bf16[4,4,128,1024]{3,1,2,0:T(4,128)(2,1)}), bf16[4,4,128,1024]{3,1,2,0:T(4,128)(2,1)}, u32[]{:S(2)}, u32[]{:S(2)}) async-start(bf16[4,4,128,1024]{3,1,2,0:T(4,128)(2,1)} %convolution_convert_fusion), calls=%async_computation.3 | async-start | bytes 8388608 | tf_op jit(solution)/shard_map/all_to_all | solution.py:127
  44.9 1.3 copy.134
  46.2 46.9 %all-to-all-done.3 = bf16[4,4,128,1024]{3,1,2,0:T(4,128)(2,1)} async-done(((bf16[4,4,128,1024]{3,1,2,0:T(4,128)(2,1)}), bf16[4,4,128,1024]{3,1,2,0:T(4,128)(2,1)}, u32[]{:S(2)}, u32[]{:S(2)}) %all-to-all-start.3) | async-done | bytes 4194336 | tf_op jit(solution)/shard_map/all_to_all | solution.py:127
  93.1 4.4 %all-to-all-start.4 = ((bf16[128,2,2048]{0,2,1:T(8,128)(2,1)}), bf16[128,2,2048]{0,2,1:T(8,128)(2,1)}, u32[]{:S(2)}, u32[]{:S(2)}) async-start(bf16[128,2,2048]{0,2,1:T(8,128)(2,1)} %bitcast.41), calls=%async_computation.4 | async-start | bytes 2097152 | tf_op jit(solution)/shard_map/all_to_all | solution.py:79
  99.9 3.6 %copy.132 = bf16[4,4,128,1024]{3,2,1,0:T(8,128)(2,1)S(1)} copy(bf16[4,4,128,1024]{3,1,2,0:T(4,128)(2,1)} %all-to-all-done.3) | data formatting | bytes 8388608 | tf_op jit(solution)/shard_map/all_to_all | solution.py:127
  103.6 2.5 pad_maximum_fusion
  106.1 5.2 %all-to-all-done.4 = bf16[128,2,2048]{0,2,1:T(8,128)(2,1)} async-done(((bf16[128,2,2048]{0,2,1:T(8,128)(2,1)}), bf16[128,2,2048]{0,2,1:T(8,128)(2,1)}, u32[]{:S(2)}, u32[]{:S(2)}) %all-to-all-start.4) | async-done | bytes 1048608 | tf_op jit(solution)/shard_map/all_to_all | solution.py:79
  111.3 65.8 %while.12 = (s32[]{:T(128)}, f32[2,8,128,1024]{2,3,1,0:T(8,128)}, bf16[2,128,2048]{1,2,0:T(8,128)(2,1)}, bf16[2,128,2048]{1,2,0:T(8,128)(2,1)}, s32[2,8]{1,0:T(2...) while((s32[]{:T(128)}, f32[2,8,128,1024]{2,3,1,0:T(8,128)}, ...), condition=%wide.region_7.8_spmd, body=%wide.region_3.7_spmd.sunk | while | flops 2729438208 | bytes 243889072 | solution.py:138
  111.3 3.0 gather_fusion
  115.9 1.6 copy.204
  118.8 1.3 bitcast_reduce_fusion.2
  120.1 3.2 copy-done
  123.4 1.4 fusion.90
  126.1 5.3 %fusion.92 = (f32[4,4,128]{2,1,0:T(4,128)S(1)}, f32[4,8,128,128,4]{3,2,4,1,0:T(8,128)S(1)}) fusion(f32[4,4,128]{2,1,0:T(4,128)S(1)} %fusion.90, f32[4,4,128]{2,1,0:T(4,128)S(1)} %get-tuple-element.135, f32[4,8,128,128,4]{3,2,4,1,0:T(8,128)} %copy-done, bf16[128,4,4,128,1]{0,3,2,4,1:T(8,128)(2,1)S(1)} %bitcast.200, ...), kind=kOutput, calls=%fused_computation.3.clone.1 | convolution fusion | flops 547354624 | bytes 18374656 | tf_op jit(solution)/shard_map/while/body/eval_jaxpr/tkgd,eskd->kgtes/dot_general | solution.py:41
  132.2 2.4 fusion.93
  134.6 1.5 fusion.94
  136.3 2.2 fusion.91
  140.9 2.5 copy-done.3
  144.2 3.0 gather_fusion
  148.8 1.6 copy.204
  153.0 3.2 copy-done
  156.3 1.4 fusion.90
  159.0 5.3 %fusion.92 = (f32[4,4,128]{2,1,0:T(4,128)S(1)}, f32[4,8,128,128,4]{3,2,4,1,0:T(8,128)S(1)}) fusion(f32[4,4,128]{2,1,0:T(4,128)S(1)} %fusion.90, f32[4,4,128]{2,1,0:T(4,128)S(1)} %get-tuple-element.135, f32[4,8,128,128,4]{3,2,4,1,0:T(8,128)} %copy-done, bf16[128,4,4,128,1]{0,3,2,4,1:T(8,128)(2,1)S(1)} %bitcast.200, ...), kind=kOutput, calls=%fused_computation.3.clone.1 | convolution fusion | flops 547354624 | bytes 18374656 | tf_op jit(solution)/shard_map/while/body/eval_jaxpr/tkgd,eskd->kgtes/dot_general | solution.py:41
  165.1 2.4 fusion.93
  167.5 1.5 fusion.94
  169.2 2.2 fusion.91
  173.8 2.5 copy-done.3
  177.1 8.9 %copy.136 = f32[16,128,1024]{2,0,1:T(8,128)} copy(f32[16,128,1024]{1,2,0:T(8,128)} %bitcast.205) | data formatting | bytes 16777216 | tf_op jit(solution)/shard_map/reshape | solution.py:148
  186.0 9.6 %fusion.35 = f32[18,128,1024]{2,0,1:T(8,128)S(1)} fusion(f32[16,128,1024]{2,0,1:T(8,128)} %copy.136, s32[16]{0:T(128)S(1)} %bitcast.215), kind=kOutput, calls=%fused_computation.55 | convolution fusion | flops 452985120 | bytes 17825856 | tf_op jit(solution)/shard_map/ms,mxd->sxd/dot_general | solution.py:145
  195.6 4.5 %copy-done.2 = f32[18,128,1024]{2,0,1:T(8,128)} copy-done((f32[18,128,1024]{2,0,1:T(8,128)}, f32[18,128,1024]{2,0,1:T(8,128)S(1)}, u32[]{:S(2)}) %copy-start.2) | copy-done | bytes 9437208
  200.1 5.3 %slice.29 = f32[16,128,1024]{2,0,1:T(8,128)} slice(f32[18,128,1024]{2,0,1:T(8,128)S(1)} %fusion.35), slice={[2:18], [0:128], [0:1024]} | slice | bytes 16777216 | tf_op jit(solution)/shard_map/slice | solution.py:152
  205.4 9.8 %reshape.355 = f32[4,4,128,1024]{3,1,0,2:T(4,128)} reshape(f32[16,128,1024]{2,0,1:T(8,128)} %slice.29) | data formatting | bytes 16777216 | tf_op jit(solution)/shard_map/reshape | solution.py:152
  215.2 9.4 %copy.137 = f32[4,4,128,1024]{3,1,2,0:T(4,128)} copy(f32[4,4,128,1024]{3,1,0,2:T(4,128)} %reshape.355) | data formatting | bytes 16777216 | tf_op jit(solution)/shard_map/reshape | solution.py:152
  224.7 100.7 %all_to_all.122 = f32[4,4,128,1024]{3,1,2,0:T(4,128)} all-to-all(f32[4,4,128,1024]{3,1,2,0:T(4,128)} %copy.137), channel_id=1, replica_groups=mesh['dp'=4,'ctx'=4,'uly'=2] {'ctx'}, dimensions={0} | all-to-all | bytes 16777216 | tf_op jit(solution)/shard_map/all_to_all | solution.py:155
  325.3 3.6 all-to-all-start.5
  328.9 14.1 %fusion.29 = bf16[2,128,1024]{2,0,1:T(2,128)(2,1)S(1)} fusion(f32[4,4,128,1024]{3,1,2,0:T(4,128)} %all_to_all.122, f32[18,128,1024]{2,0,1:T(8,128)} %copy-done.2, s32[4,4,2]{1,2,0:T(2,128)S(1)} %copy-done.6), kind=kOutput, calls=%fused_computation.41 | convolution fusion | flops 50856000 | bytes 9961600 | tf_op jit(solution)/shard_map/csb,csxd->bxd/dot_general | solution.py:156
  344.1 3.4 all-to-all-start.7
  348.3 4.4 %all-to-all-done.7 = bf16[2,128,512]{2,1,0:T(8,128)(2,1)S(1)} async-done(((bf16[2,128,512]{2,1,0:T(8,128)(2,1)}), bf16[2,128,512]{2,1,0:T(8,128)(2,1)S(1)}, u32[]{:S(2)}, u32[]{:S(2)}) %all-to-all-start.7) | async-done | bytes 262176 | tf_op jit(solution)/shard_map/all_to_all | solution.py:164
  352.7 3.4 all-to-all-start.8
  356.2 1.3 copy.171
  358.5 2.8 all-to-all-done.8
  (98 shorter events, 30.6 us)
Async XLA Ops:
  2.6 10.1 %all-to-all-start.2 = ((bf16[128,2,512]{2,0,1:T(8,128)(2,1)}), bf16[128,2,512]{2,0,1:T(8,128)(2,1)S(1)}, u32[]{:S(2)}, u32[]{:S(2)}) async-start(bf16[128,2,512]{2,0,1:T(8,128)(2,1)} %copy.130), calls=%async_computation.2 | async-start | bytes 524288 | tf_op jit(solution)/shard_map/all_to_all | solution.py:81
  12.7 9.3 %all-to-all-start.1 = ((bf16[128,2,512]{2,0,1:T(8,128)(2,1)}), bf16[128,2,512]{2,0,1:T(8,128)(2,1)S(1)}, u32[]{:S(2)}, u32[]{:S(2)}) async-start(bf16[128,2,512]{2,0,1:T(8,128)(2,1)} %copy.127), calls=%async_computation.1 | async-start | bytes 524288 | tf_op jit(solution)/shard_map/all_to_all | solution.py:80
  16.2 28.6 %copy-start.4 = (bf16[128,4096]{1,0:T(8,128)(2,1)S(1)}, bf16[128,4096]{1,0:T(8,128)(2,1)}, u32[]{:S(2)}) copy-start(bf16[128,4096]{1,0:T(8,128)(2,1)} %param.10) | copy-start | bytes 3145732
  22.1 17.8 %all-to-all-start = ((bf16[128,2,2048]{0,2,1:T(8,128)(2,1)}), bf16[128,2,2048]{0,2,1:T(8,128)(2,1)}, u32[]{:S(2)}, u32[]{:S(2)}) async-start(bf16[128,2,2048]{0,2,1:T(8,128)(2,1)} %bitcast.31), calls=%async_computation | async-start | bytes 2097152 | tf_op jit(solution)/shard_map/all_to_all | solution.py:78
  26.7 0.6 copy-start.5
  39.9 53.2 %all-to-all-start.3 = ((bf16[4,4,128,1024]{3,1,2,0:T(4,128)(2,1)}), bf16[4,4,128,1024]{3,1,2,0:T(4,128)(2,1)}, u32[]{:S(2)}, u32[]{:S(2)}) async-start(bf16[4,4,128,1024]{3,1,2,0:T(4,128)(2,1)} %convolution_convert_fusion), calls=%async_computation.3 | async-start | bytes 8388608 | tf_op jit(solution)/shard_map/all_to_all | solution.py:127
  93.1 18.2 %all-to-all-start.4 = ((bf16[128,2,2048]{0,2,1:T(8,128)(2,1)}), bf16[128,2,2048]{0,2,1:T(8,128)(2,1)}, u32[]{:S(2)}, u32[]{:S(2)}) async-start(bf16[128,2,2048]{0,2,1:T(8,128)(2,1)} %bitcast.41), calls=%async_computation.4 | async-start | bytes 2097152 | tf_op jit(solution)/shard_map/all_to_all | solution.py:79
  120.1 3.2 copy-start
  126.1 6.1 %copy-start.1 = (f32[4,8,128,128,4]{3,2,4,1,0:T(8,128)S(1)}, f32[4,8,128,128,4]{3,2,4,1,0:T(8,128)}, u32[]{:S(2)}) copy-start(f32[4,8,128,128,4]{3,2,4,1,0:T(8,128)} %copy-done) | copy-start | bytes 25165828 | tf_op jit(solution)/shard_map/while
  136.1 2.6 slice-start
  136.3 3.4 slice-start.1
  140.1 3.2 copy-start.3
  153.0 3.2 copy-start
  159.0 6.1 %copy-start.1 = (f32[4,8,128,128,4]{3,2,4,1,0:T(8,128)S(1)}, f32[4,8,128,128,4]{3,2,4,1,0:T(8,128)}, u32[]{:S(2)}) copy-start(f32[4,8,128,128,4]{3,2,4,1,0:T(8,128)} %copy-done) | copy-start | bytes 25165828 | tf_op jit(solution)/shard_map/while
  169.0 2.6 slice-start
  169.2 3.4 slice-start.1
  173.0 3.2 copy-start.3
  177.1 8.9 %copy-start.7 = (s32[1,16]{1,0:T(1,128)S(1)}, s32[1,16]{1,0:T(1,128)}, u32[]{:S(2)}) copy-start(s32[1,16]{1,0:T(1,128)} %get-tuple-element.67) | copy-start | bytes 196
  195.6 4.5 %copy-start.2 = (f32[18,128,1024]{2,0,1:T(8,128)}, f32[18,128,1024]{2,0,1:T(8,128)S(1)}, u32[]{:S(2)}) copy-start(f32[18,128,1024]{2,0,1:T(8,128)S(1)} %fusion.35) | copy-start | bytes 28311556
  224.7 104.3 %copy-start.6 = (s32[4,4,2]{1,2,0:T(2,128)S(1)}, s32[4,4,2]{1,2,0:T(2,128)}, u32[]{:S(2)}) copy-start(s32[4,4,2]{1,2,0:T(2,128)} %copy-done.5) | copy-start | bytes 388
  325.3 18.8 %all-to-all-start.5 = ((bf16[2,128,2048]{1,2,0:T(8,128)(2,1)}), bf16[2,128,2048]{1,2,0:T(8,128)(2,1)S(1)}, u32[]{:S(2)}, u32[]{:S(2)}) async-start(bf16[2,128,2048]{1,2,0:T(8,128)(2,1)} %get-tuple-element.41), calls=%async_computation.5 | async-start | bytes 2097152 | tf_op jit(solution)/shard_map/all_to_all | solution.py:163
  344.1 8.6 %all-to-all-start.7 = ((bf16[2,128,512]{2,1,0:T(8,128)(2,1)}), bf16[2,128,512]{2,1,0:T(8,128)(2,1)S(1)}, u32[]{:S(2)}, u32[]{:S(2)}) async-start(bf16[2,128,512]{2,1,0:T(8,128)(2,1)} %copy.139), calls=%async_computation.7 | async-start | bytes 524288 | tf_op jit(solution)/shard_map/all_to_all | solution.py:164
  352.7 8.6 %all-to-all-start.8 = ((bf16[2,128,512]{2,1,0:T(8,128)(2,1)}), bf16[2,128,512]{2,1,0:T(8,128)(2,1)S(1)}, u32[]{:S(2)}, u32[]{:S(2)}) async-start(bf16[2,128,512]{2,1,0:T(8,128)(2,1)} %copy.141), calls=%async_computation.8 | async-start | bytes 524288 | tf_op jit(solution)/shard_map/all_to_all | solution.py:165
where the time goes:
time: 364 us; the launch traced here: 362 us
  blocking collectives  101 us (28%)
  local copies, waits for them, and re-layouts  90.3 us (25%)
  waiting for transfers between devices  73.3 us (20%)
  matrix products  50.2 us (14%)
  starting transfers between devices  31.9 us (9%)
  other arithmetic  14.7 us (4%)
    all_to_all x1, blocking collectives, per_device(): lax.all_to_all(sent_grads, 'ctx', split_axis=0, concat_axis=0, tiled=True)  101 us
    all_to_all x1, waiting for transfers between devices, per_device(): lax.all_to_all(outgoing, 'ctx', split_axis=0, concat_axis=0, tiled=True)  46.9 us
    reshape x2, local copies, waits for them, and re-layouts, per_device(): source_grads[per_group:per_group + groups * capacity]  19.2 us
    while x20, local copies, waits for them, and re-layouts  14.9 us
    dot_general x1, matrix products, per_device(): jnp.einsum('csb,csxd->bxd', slot_picker.astype(jnp.float32), returned, pr...  14.1 us
    unnamed x16, local copies, waits for them, and re-layouts  12.1 us
    dot_general x2, matrix products, block_backward(): jnp.einsum('tkgd,eskd->kgtes', dout_four, value_sel, preferred_element_ty...  10.7 us
    dot_general x1, matrix products, per_device(): jnp.einsum('ms,mxd->sxd', source_hot, partials.reshape(per_group * ENTRIE...  9.64 us
  transfers between devices with their start and end apart: 8, of which 6 were waited for; matrix products, arithmetic and copies ran while one was open for 11% of the time, Pallas kernels for 0%

commit v1 on v0

--- a/solution.py
+++ b/solution.py
@@ -3,6 +3,8 @@
 import jax
 import jax.numpy as jnp
 from jax import lax
+from jax.experimental import pallas as pl
+from jax.experimental.pallas import tpu as pltpu
 from jax.sharding import PartitionSpec as P
 
 HEAD_DIM = 128
@@ -70,7 +72,7 @@
     return (partials, grad_query.reshape(BLOCK, kv_count * GROUP * HEAD_DIM))
 
 
-def per_device(queries, keys, values, d_out, rand_blocks):
+def per_device_sparse(queries, keys, values, d_out, rand_blocks):
     softmax_scale = HEAD_DIM ** (-0.5)
     groups = lax.axis_size("ctx")
     my_group = lax.axis_index("ctx")
@@ -167,6 +169,320 @@
     return (d_queries, d_keys, d_values)
 
 
+LOG2E = 1.4426950408889634
+PART = 8
+HEAD_HALF = 4
+CHUNKS = 1
+HALF_Q = HEAD_HALF * GROUP * HEAD_DIM
+HALF_KV = HEAD_HALF * HEAD_DIM
+PAIR = 2 * BLOCK
+AXES = ("ctx", "uly")
+
+SWAP = 2
+
+
+def perm_to(first, second):
+    return [(i, i ^ (second if i & SWAP else first)) for i in range(PART)]
+
+
+SWAP_PERM = perm_to(SWAP, SWAP)
+NEAR_PERM = perm_to(4, 1)
+FAR_PERM = perm_to(1, 4)
+
+
+def send(array, perm):
+    return lax.ppermute(array, AXES, perm)
+
+
+def pack_kernel(chunks, where_ref, k_ref, v_ref, ko_ref, vo_ref, *outs):
+    heads = HEAD_HALF // chunks
+    for chunk in range(chunks):
+        for head in range(heads):
+            src = slice((chunk * heads + head) * HEAD_DIM, (chunk * heads + head + 1) * HEAD_DIM)
+            for side, ref in enumerate((k_ref, v_ref)):
+                cols = slice((2 * head + side) * HEAD_DIM, (2 * head + side + 1) * HEAD_DIM)
+                outs[chunk][0:BLOCK, cols] = ref[:, src]
+            for side, ref in enumerate((ko_ref, vo_ref)):
+                cols = slice((2 * head + side) * HEAD_DIM, (2 * head + side + 1) * HEAD_DIM)
+                outs[chunk][BLOCK:PAIR, cols] = ref[:, src]
+
+
+def pack_pairs(where, keys, values, keys_other, values_other):
+    width = 2 * HALF_KV // CHUNKS
+    spec = pl.BlockSpec((BLOCK, HALF_KV), lambda g, w: (0, w[0]))
+    return pl.pallas_call(
+        partial(pack_kernel, CHUNKS),
+        out_shape=[jax.ShapeDtypeStruct((PAIR, width), jnp.bfloat16)] * CHUNKS,
+        grid_spec=pltpu.PrefetchScalarGridSpec(
+            num_scalar_prefetch=1,
+            grid=(1,),
+            in_specs=[spec] * 4,
+            out_specs=[pl.BlockSpec((PAIR, width), lambda g, w: (0, 0))] * CHUNKS,
+        ),
+        name="pack_pairs",
+        cost_estimate=pl.CostEstimate(flops=0, bytes_accessed=2**20, transcendentals=0),
+    )(where, keys, values, keys_other, values_other)
+
+
+def attend_kernel(
+    where_ref,
+    rand_ref,
+    q_ref,
+    do_ref,
+    qo_ref,
+    doo_ref,
+    pair_ref,
+    near_ref,
+    far_ref,
+    corner_ref,
+    dq_ref,
+    dqo_ref,
+    own_out,
+    near_out,
+    far_out,
+    corner_out,
+    s_ref,
+    dp_ref,
+    qcat_ref,
+    docat_ref,
+    dk_ref,
+    dv_ref,
+):
+    scale = HEAD_DIM ** (-0.5)
+    step = pl.program_id(1)
+    half = where_ref[0]
+    me = where_ref[1]
+    near = 4 - 3 * half
+    far = 1 + 3 * half
+    block = me ^ (SWAP * step)
+    mine = step == 0
+    sources = (pair_ref, near_ref, far_ref, corner_ref)
+    deltas = (0, near, far, near ^ far)
+
+    @pl.when(mine)
+    def _():
+        for g in range(GROUP):
+            qcat_ref[g * BLOCK : (g + 1) * BLOCK, :] = q_ref[:, g * HEAD_DIM : (g + 1) * HEAD_DIM]
+            docat_ref[g * BLOCK : (g + 1) * BLOCK, :] = do_ref[:, g * HEAD_DIM : (g + 1) * HEAD_DIM]
+        dk_ref[...] = jnp.zeros_like(dk_ref)
+        dv_ref[...] = jnp.zeros_like(dv_ref)
+
+    @pl.when(jnp.logical_not(mine))
+    def _():
+        for g in range(GROUP):
+            qcat_ref[g * BLOCK : (g + 1) * BLOCK, :] = qo_ref[:, g * HEAD_DIM : (g + 1) * HEAD_DIM]
+            docat_ref[g * BLOCK : (g + 1) * BLOCK, :] = doo_ref[
+                :, g * HEAD_DIM : (g + 1) * HEAD_DIM
+            ]
+
+    def count_of(slot):
+        listed = me ^ deltas[slot // 2] ^ (SWAP * (slot % 2))
+        total = jnp.int32(0)
+        for w in range(WINDOW):
+            total += (lax.rem(block + (w - WINDOW // 2 + PART), PART) == listed).astype(jnp.int32)
+        total += (listed < GLOBALS).astype(jnp.int32)
+        for r in range(RANDOMS):
+            total += (rand_ref[block * RANDOMS + r] == listed).astype(jnp.int32)
+        return total
+
+    counts = [count_of(slot) for slot in range(PART)]
+    qcat = qcat_ref[...]
+    docat = docat_ref[...]
+    rows = GROUP * BLOCK
+    contract_last = (((1,), (1,)), ((), ()))
+    contract = (((1,), (0,)), ((), ()))
+
+    def key_of(slot):
+        base = (slot % 2) * BLOCK
+        return sources[slot // 2][base : base + BLOCK, 0:HEAD_DIM]
+
+    def value_of(slot):
+        base = (slot % 2) * BLOCK
+        return sources[slot // 2][base : base + BLOCK, HEAD_DIM : 2 * HEAD_DIM]
+
+    top = None
+    for slot in range(PART):
+        s = lax.dot_general(key_of(slot), qcat, contract_last, preferred_element_type=jnp.float32)
+        s_ref[slot] = s
+        part = jnp.max(s.reshape(BLOCK // 8, 8, rows), axis=0)
+        part = jnp.where(counts[slot] > 0, part, -1e30)
+        top = part if top is None else jnp.maximum(top, part)
+        dp_ref[slot] = lax.dot_general(
+            value_of(slot), docat, contract_last, preferred_element_type=jnp.float32
+        )
+    factor = scale * LOG2E
+    top = jnp.max(top, axis=0, keepdims=True) * factor
+    total = jnp.zeros((8, rows), jnp.float32)
+    delta = jnp.zeros((8, rows), jnp.float32)
+    for slot in range(PART):
+        shift = jnp.where(counts[slot] > 0, top, 1e30)
+        weight = counts[slot].astype(jnp.float32)
+        e = jnp.exp2(s_ref[slot] * factor - shift)
+        s_ref[slot] = e
+        total += weight * jnp.sum(e.reshape(BLOCK // 8, 8, rows), axis=0)
+        delta += weight * jnp.sum((e * dp_ref[slot]).reshape(BLOCK // 8, 8, rows), axis=0)
+    inverse = 1.0 / jnp.sum(total, axis=0, keepdims=True)
+    delta = jnp.sum(delta, axis=0, keepdims=True) * inverse
+    dq = None
+    for slot in range(PART):
+        p = s_ref[slot] * (counts[slot].astype(jnp.float32) * inverse)
+        ds = (p * (dp_ref[slot] - delta)).astype(jnp.bfloat16)
+        dv_ref[slot] += lax.dot_general(
+            p.astype(jnp.bfloat16), docat, contract, preferred_element_type=jnp.float32
+        )
+        dk_ref[slot] += lax.dot_general(ds, qcat, contract, preferred_element_type=jnp.float32)
+        term = lax.dot_general(
+            key_of(slot).T, ds, contract, preferred_element_type=jnp.float32
+        )
+        dq = term if dq is None else dq + term
+    dq = (dq * scale).T.astype(jnp.bfloat16)
+
+    @pl.when(mine)
+    def _():
+        for g in range(GROUP):
+            dq_ref[:, g * HEAD_DIM : (g + 1) * HEAD_DIM] = dq[g * BLOCK : (g + 1) * BLOCK]
+
+    @pl.when(jnp.logical_not(mine))
+    def _():
+        for g in range(GROUP):
+            dqo_ref[:, g * HEAD_DIM : (g + 1) * HEAD_DIM] = dq[g * BLOCK : (g + 1) * BLOCK]
+        for place, out in enumerate((own_out, near_out, far_out, corner_out)):
+            for r in range(2):
+                base = slice(r * BLOCK, (r + 1) * BLOCK)
+                out[base, 0:HEAD_DIM] = (dk_ref[2 * place + r] * scale).astype(out.dtype)
+                out[base, HEAD_DIM : 2 * HEAD_DIM] = dv_ref[2 * place + r].astype(out.dtype)
+
+
+def attend(chunk, where, rand, queries, d_out, queries_other, dout_other, sources):
+    heads = HEAD_HALF // CHUNKS
+    qw = GROUP * HEAD_DIM
+    kw = 2 * HEAD_DIM
+    first = chunk * heads
+    q_spec = pl.BlockSpec((BLOCK, qw), lambda j, b, w, r: (0, w[0] * HEAD_HALF + first + j))
+    kv_spec = pl.BlockSpec((PAIR, kw), lambda j, b, w, r: (0, j))
+    dq_spec = pl.BlockSpec((BLOCK, qw), lambda j, b, w, r: (0, j))
+    rows = GROUP * BLOCK
+    pairs = 2 * heads * rows * PART * BLOCK
+    dq_shape = jax.ShapeDtypeStruct((BLOCK, heads * qw), jnp.bfloat16)
+    wide = jax.ShapeDtypeStruct((PAIR, heads * kw), jnp.float32)
+    narrow = jax.ShapeDtypeStruct((PAIR, heads * kw), jnp.bfloat16)
+    return pl.pallas_call(
+        attend_kernel,
+        out_shape=[dq_shape, dq_shape, wide, wide, narrow, narrow],
+        grid_spec=pltpu.PrefetchScalarGridSpec(
+            num_scalar_prefetch=2,
+            grid=(heads, 2),
+            in_specs=[q_spec] * 4 + [kv_spec] * 4,
+            out_specs=[dq_spec] * 2 + [kv_spec] * 4,
+            scratch_shapes=[
+                pltpu.VMEM((PART, BLOCK, rows), jnp.float32),
+                pltpu.VMEM((PART, BLOCK, rows), jnp.float32),
+                pltpu.VMEM((rows, HEAD_DIM), jnp.bfloat16),
+                pltpu.VMEM((rows, HEAD_DIM), jnp.bfloat16),
+                pltpu.VMEM((PART, BLOCK, HEAD_DIM), jnp.float32),
+                pltpu.VMEM((PART, BLOCK, HEAD_DIM), jnp.float32),
+            ],
+        ),
+        name="attend",
+        compiler_params=pltpu.CompilerParams(vmem_limit_bytes=24 * 2**20),
+        cost_estimate=pl.CostEstimate(
+            flops=10 * pairs * HEAD_DIM * 2, bytes_accessed=4 * 2**20, transcendentals=pairs
+        ),
+    )(where, rand, queries, d_out, queries_other, dout_other, *sources)
+
+
+def finish_kernel(chunks, where_ref, *refs):
+    heads = HEAD_HALF // chunks
+    own, other, dq_own, dq_got = (refs[i * chunks : (i + 1) * chunks] for i in range(4))
+    dq_ref, dk_ref, dv_ref = refs[4 * chunks :]
+    half = where_ref[0]
+    for value in range(2):
+
+        @pl.when(half == value)
+        def _():
+            for piece, place in ((own, value), (other, 1 - value)):
+                for chunk in range(chunks):
+                    for head in range(heads):
+                        at = place * HALF_KV + (chunk * heads + head) * HEAD_DIM
+                        from_col = 2 * head * HEAD_DIM
+                        dk_ref[:, at : at + HEAD_DIM] = piece[chunk][
+                            0:BLOCK, from_col : from_col + HEAD_DIM
+                        ]
+                        dv_ref[:, at : at + HEAD_DIM] = piece[chunk][
+                            0:BLOCK, from_col + HEAD_DIM : from_col + 2 * HEAD_DIM
+                        ]
+            width = HALF_Q // chunks
+            for piece, place in ((dq_own, value), (dq_got, 1 - value)):
+                for chunk in range(chunks):
+                    at = place * HALF_Q + chunk * width
+                    dq_ref[:, at : at + width] = piece[chunk][...]
+
+
+def finish(where, own, other, dq_own, dq_got):
+    return pl.pallas_call(
+        partial(finish_kernel, CHUNKS),
+        out_shape=[
+            jax.ShapeDtypeStruct((BLOCK, 2 * HALF_Q), jnp.bfloat16),
+            jax.ShapeDtypeStruct((BLOCK, 2 * HALF_KV), jnp.bfloat16),
+            jax.ShapeDtypeStruct((BLOCK, 2 * HALF_KV), jnp.bfloat16),
+        ],
+        in_specs=[pl.BlockSpec(memory_space=pltpu.SMEM)]
+        + [pl.BlockSpec(memory_space=pltpu.VMEM)] * (4 * CHUNKS),
+        out_specs=[pl.BlockSpec(memory_space=pltpu.VMEM)] * 3,
+        name="finish",
+        cost_estimate=pl.CostEstimate(flops=0, bytes_accessed=3 * 2**20, transcendentals=0),
+    )(where, *own, *other, *dq_own, *dq_got)
+
+
+def per_device_dense(queries, keys, values, d_out, rand_blocks):
+    me = lax.axis_index("ctx") * 2 + lax.axis_index("uly")
+    half = lax.axis_index("ctx") % 2
+    where = jnp.stack([half, me]).astype(jnp.int32)
+    rand = rand_blocks.reshape(PART * RANDOMS)
+    keys_other = send(keys, SWAP_PERM)
+    values_other = send(values, SWAP_PERM)
+    queries_other = send(queries, SWAP_PERM)
+    dout_other = send(d_out, SWAP_PERM)
+    pairs = pack_pairs(where, keys, values, keys_other, values_other)
+    nears = [send(pair, NEAR_PERM) for pair in pairs]
+    fars = [send(pair, FAR_PERM) for pair in pairs]
+    corners = [send(near, FAR_PERM) for near in nears]
+    own, other, dq_own, dq_got = [], [], [], []
+    for chunk in range(CHUNKS):
+        dq_mine, dq_other, own_grads, near_grads, far_grads, corner_grads = attend(
+            chunk,
+            where,
+            rand,
+            queries,
+            d_out,
+            queries_other,
+            dout_other,
+            (pairs[chunk], nears[chunk], fars[chunk], corners[chunk]),
+        )
+        from_corner = send(corner_grads, FAR_PERM)
+        from_far = send(far_grads, FAR_PERM)
+        relayed = (near_grads + from_corner.astype(jnp.float32)).astype(jnp.bfloat16)
+        from_near = send(relayed, NEAR_PERM)
+        total = own_grads + from_far.astype(jnp.float32) + from_near.astype(jnp.float32)
+        total = total.astype(jnp.bfloat16)
+        own.append(total[:BLOCK])
+        other.append(send(total[BLOCK:], SWAP_PERM))
+        dq_own.append(dq_mine)
+        dq_got.append(send(dq_other, SWAP_PERM))
+    return tuple(finish(where, own, other, dq_own, dq_got))
+
+
+def per_device(queries, keys, values, d_out, rand_blocks):
+    dense = (
+        lax.axis_size("ctx") == 4
+        and lax.axis_size("uly") == 2
+        and rand_blocks.shape[0] == PART
+        and keys.shape == (BLOCK, 2 * HALF_KV)
+    )
+    plan = per_device_dense if dense else per_device_sparse
+    return plan(queries, keys, values, d_out, rand_blocks)
+
+
 def solution(mesh):
     in_specs = (
         P(("dp", "ctx", "uly"), None),

time: 364 us -> 83 us (0.23)
  blocking collectives: 101 us -> 0 us
  local copies, waits for them, and re-layouts: 90.3 us -> 4.07 us
  matrix products: 50.2 us -> 0 us
  waiting for transfers between devices: 73.3 us -> 35 us
  Pallas kernels: 0 us -> 29 us
  starting transfers between devices: 31.9 us -> 12.6 us
  other arithmetic: 14.7 us -> 1.03 us
    all_to_all x1 -> x0, blocking collectives: 101 us -> none  [per_device(): lax.all_to_all(sent_grads, 'ctx', split_axis=0, concat_axis=0, tiled=True)]
    all_to_all x8 -> x0, waiting for transfers between devices: 73.3 us -> none  [the longest x1 46.9 us: per_device(): lax.all_to_all(outgoing, 'ctx', split_axis=0, concat_axis=0, tiled=True)]
    dot_general x13 -> x0, matrix products: 50.2 us -> none  [the longest x1 14.1 us: per_device(): jnp.einsum('csb,csxd->bxd', slot_picker.astype(jnp.float32), returned, pr...]
    ppermute x0 -> x12, waiting for transfers between devices: none -> 35 us  [send(): return lax.ppermute(array, AXES, perm)]
    all_to_all x8 -> x0, starting transfers between devices: 31.9 us -> none  [the longest x1 4.93 us: per_device(): lax.all_to_all(outgoing, 'ctx', split_axis=0, concat_axis=0, tiled=True)]
    pallas_call x0 -> x3, Pallas kernels: none -> 29 us  [the longest x1 23.6 us: attend(): pl.pallas_call(attend_kernel, out_shape=[dq_shape, dq_shape, wide, wide,...]
    reshape x3 -> x1, local copies, waits for them, and re-layouts: 28.1 us -> 0.08 us  [per_device_dense(): rand = rand_blocks.reshape(PART * RANDOMS)]
    while x20 -> x0, local copies, waits for them, and re-layouts: 14.9 us -> none
  transfers between devices with their start and end apart: 8 -> 12, of which waited for: 6 -> 7; matrix products, arithmetic and copies ran while one was open for 11% -> 2% of each run, Pallas kernels for 0% -> 3%
where the time goes in v1:
time: 83 us; the launch traced here: 82.4 us
  waiting for transfers between devices  35 us (42%)
  Pallas kernels  29 us (35%)
  starting transfers between devices  12.6 us (15%)
  local copies, waits for them, and re-layouts  4.07 us (5%)
  other arithmetic  1.03 us (1%)
    ppermute x12, waiting for transfers between devices, send(): return lax.ppermute(array, AXES, perm)  35 us
    pallas_call x1, Pallas kernels, attend(): pl.pallas_call(attend_kernel, out_shape=[dq_shape, dq_shape, wide, wide,...  23.6 us
    ppermute x12, starting transfers between devices, send(): return lax.ppermute(array, AXES, perm)  12.6 us
    unnamed x19, local copies, waits for them, and re-layouts  3.25 us
    pallas_call x1, Pallas kernels, finish(): pl.pallas_call(partial(finish_kernel, CHUNKS), out_shape=[jax.ShapeDtypeS...  2.69 us
    pallas_call x1, Pallas kernels, pack_pairs(): pl.pallas_call(partial(pack_kernel, CHUNKS), out_shape=[jax.ShapeDtypeStr...  2.69 us
  transfers between devices with their start and end apart: 12, of which 7 were waited for; matrix products, arithmetic and copies ran while one was open for 2% of the time, Pallas kernels for 3%

profile of v1, /device:TPU:0, one launch (start us, length us, event | category | flops | bytes accessed | tf_op | source)
XLA Modules:
  0.0 82.4 jit_solution(14949147986081992538)
XLA Ops:
  0.6 0.0 copy-start.3
  0.6 0.5 collective-permute-start.2
  1.2 0.1 collective-permute-start.3
  1.2 0.4 collective-permute-start
  1.7 0.1 collective-permute-start.1
  1.7 0.7 pad_add_fusion.where_ref
  2.4 0.0 copy-start.8
  2.4 0.1 collective-permute-done.2.ko_ref
  2.5 0.0 copy-start.6
  2.5 0.5 collective-permute-done.3.vo_ref
  3.0 0.2 copy-done.6
  3.2 2.7 %pack_pairs.1.pair_ref = bf16[256,1024]{1,0:T(8,128)(2,1)} custom-call(s32[2]{0:T(128)} %pad_add_fusion.where_ref, bf16[128,1024]{1,0:T(8,128)(2,1)} %k_ref.1, bf16[128,1024]{1,0:T(8,128)(2,1)} %v_ref.1, bf16[128,1024]{1,0:T(8,128)(2,1)} %copy-done.6, bf16[128,1024]{1,0:T(8,128)(2,1)} %collective-permute-done.3.vo_ref), custom_call_target="tpu_custom_call" | custom-call | bytes 1048576 | tf_op jit(solution)/shard_map/pack_pairs/pallas_call | solution.py:213
  5.9 2.9 %collective-permute-start.4 = (bf16[256,1024]{1,0:T(8,128)(2,1)}, bf16[256,1024]{1,0:T(8,128)(2,1)}, u32[]{:S(2)}, u32[]{:S(2)}) collective-permute-start(bf16[256,1024]{1,0:T(8,128)(2,1)} %pack_pairs.1.pair_ref), channel_id=1, source_target_pairs={{0,4},{1,5},{2,3},{3,2},{4,0},{5,1},{6,7},{7,6},{8,12},{9,13},{10,... | collective-permute-start | bytes 1572872 | tf_op jit(solution)/shard_map/ppermute | solution.py:194
  8.8 1.5 %collective-permute-start.5 = (bf16[256,1024]{1,0:T(8,128)(2,1)}, bf16[256,1024]{1,0:T(8,128)(2,1)}, u32[]{:S(2)}, u32[]{:S(2)}) collective-permute-start(bf16[256,1024]{1,0:T(8,128)(2,1)} %pack_pairs.1.pair_ref), channel_id=1, source_target_pairs={{0,1},{1,0},{2,6},{3,7},{4,5},{5,4},{6,2},{7,3},{8,9},{9,8},{10,14... | collective-permute-start | bytes 1572872 | tf_op jit(solution)/shard_map/ppermute | solution.py:194
  10.3 10.8 %collective-permute-done.4.near_ref = bf16[256,1024]{1,0:T(8,128)(2,1)} collective-permute-done((bf16[256,1024]{1,0:T(8,128)(2,1)}, bf16[256,1024]{1,0:T(8,128)(2,1)}, u32[]{:S(2)}, u32[]{:S(2)}) %collective-permute-start.4) | collective-permute-done | bytes 524320 | tf_op jit(solution)/shard_map/ppermute | solution.py:194
  21.1 2.0 %collective-permute-start.6 = (bf16[256,1024]{1,0:T(8,128)(2,1)}, bf16[256,1024]{1,0:T(8,128)(2,1)}, u32[]{:S(2)}, u32[]{:S(2)}) collective-permute-start(bf16[256,1024]{1,0:T(8,128)(2,1)} %collective-permute-done.4.near_ref), channel_id=1, source_target_pairs={{0,1},{1,0},{2,6},{3,7},{4,5},{5,4},{6,2},{7,3},{8,9},{9,8},{10,14... | collective-permute-start | bytes 1572872 | tf_op jit(solution)/shard_map/ppermute | solution.py:194
  23.1 0.0 copy-done.8
  23.1 0.1 copy.9
  23.2 0.0 copy-start.2
  23.2 0.1 reshape.9.rand_ref
  23.3 0.0 collective-permute-done.5.far_ref
  23.3 0.0 collective-permute-done.qo_ref
  23.3 0.0 collective-permute-done.1.doo_ref
  23.3 7.3 %collective-permute-done.6.corner_ref = bf16[256,1024]{1,0:T(8,128)(2,1)} collective-permute-done((bf16[256,1024]{1,0:T(8,128)(2,1)}, bf16[256,1024]{1,0:T(8,128)(2,1)}, u32[]{:S(2)}, u32[]{:S(2)}) %collective-permute-start.6) | collective-permute-done | bytes 524320 | tf_op jit(solution)/shard_map/ppermute | solution.py:194
  30.6 0.0 copy-done.3
  30.6 0.0 copy-done.2
  30.6 0.0 copy-start.1
  30.6 1.0 %copy-done.1 = bf16[256,1024]{1,0:T(8,128)(2,1)S(1)} copy-done((bf16[256,1024]{1,0:T(8,128)(2,1)S(1)}, bf16[256,1024]{1,0:T(8,128)(2,1)}, u32[]{:S(2)}) %copy-start.1) | copy-done | bytes 524312
  31.6 1.2 %copy-done.4 = bf16[128,4096]{1,0:T(8,128)(2,1)S(1)} copy-done((bf16[128,4096]{1,0:T(8,128)(2,1)S(1)}, bf16[128,4096]{1,0:T(8,128)(2,1)}, u32[]{:S(2)}) %copy-start.4) | copy-done | bytes 1048600
  32.9 23.6 %attend.1 = (bf16[128,2048]{1,0:T(8,128)(2,1)S(1)}, bf16[128,2048]{1,0:T(8,128)(2,1)S(1)}, f32[256,1024]{1,0:T(8,128)S(1)}, f32[256,1024]{1,0:T(8,128)S(1)}, bf1...) custom-call(s32[2]{0:T(128)S(1)} %copy-done.2, s32[24]{0:T(128)S(1)} %reshape.9.rand_ref, ...), custom_call_target="tpu_custom_call" | custom-call | flops 10737418240 | bytes 4194304 | tf_op jit(solution)/shard_map/attend/pallas_call | solution.py:369
  56.5 0.0 copy-start
  56.5 2.1 %collective-permute-start.8 = (bf16[256,1024]{1,0:T(8,128)(2,1)S(1)}, bf16[256,1024]{1,0:T(8,128)(2,1)S(1)}, u32[]{:S(2)}, u32[]{:S(2)}) collective-permute-start(bf16[256,1024]{1,0:T(8,128)(2,1)S(1)} %get-tuple-element.12), channel_id=1, source_target_pairs={{0,1},{1,0},{2,6},{3,7},{4,5},{5,4},{6,2},{7,3},{8,9},{9,8},{10,14... | collective-permute-start | bytes 1572872 | tf_op jit(solution)/shard_map/ppermute | solution.py:194
  58.6 0.1 collective-permute-start.7
  58.6 7.1 %collective-permute-done.8 = bf16[256,1024]{1,0:T(8,128)(2,1)S(1)} collective-permute-done((bf16[256,1024]{1,0:T(8,128)(2,1)S(1)}, bf16[256,1024]{1,0:T(8,128)(2,1)S(1)}, u32[]{:S(2)}, u32[]{:S(2)}) %collective-permute-start.8) | collective-permute-done | bytes 524320 | tf_op jit(solution)/shard_map/ppermute | solution.py:194
  65.7 0.1 add_convert_fusion.1
  65.9 0.0 copy-done
  65.9 2.6 %collective-permute-start.9 = (bf16[256,1024]{1,0:T(8,128)(2,1)S(1)}, bf16[256,1024]{1,0:T(8,128)(2,1)S(1)}, u32[]{:S(2)}, u32[]{:S(2)}) collective-permute-start(bf16[256,1024]{1,0:T(8,128)(2,1)S(1)} %add_convert_fusion.1), channel_id=1, source_target_pairs={{0,4},{1,5},{2,3},{3,2},{4,0},{5,1},{6,7},{7,6},{8,12},{9,13},{10,... | collective-permute-start | bytes 1572872 | tf_op jit(solution)/shard_map/ppermute | solution.py:194
  68.5 0.0 collective-permute-start.11
  68.5 8.0 %collective-permute-done.7 = bf16[256,1024]{1,0:T(8,128)(2,1)S(1)} collective-permute-done((bf16[256,1024]{1,0:T(8,128)(2,1)S(1)}, bf16[256,1024]{1,0:T(8,128)(2,1)S(1)}, u32[]{:S(2)}, u32[]{:S(2)}) %collective-permute-start.7) | collective-permute-done | bytes 524320 | tf_op jit(solution)/shard_map/ppermute | solution.py:194
  76.5 0.0 collective-permute-done.9
  76.5 0.2 add_convert_fusion
  76.7 0.7 fusion
  77.5 0.3 collective-permute-start.10
  77.8 0.0 collective-permute-done.11.refs_3_
  77.8 1.2 %collective-permute-done.10.refs_1_ = bf16[128,1024]{1,0:T(8,128)(2,1)S(1)} collective-permute-done((bf16[128,1024]{1,0:T(8,128)(2,1)S(1)}, bf16[128,1024]{1,0:T(8,128)(2,1)S(1)}, u32[]{:S(2)}, u32[]{:S(2)}) %collective-permute-start.10) | collective-permute-done | bytes 262176 | tf_op jit(solution)/shard_map/ppermute | solution.py:194
  79.0 0.0 copy-done.5
  79.0 0.7 copy-done.7
  79.7 2.7 %finish.1 = (bf16[128,4096]{1,0:T(8,128)(2,1)}, bf16[128,1024]{1,0:T(8,128)(2,1)}, bf16[128,1024]{1,0:T(8,128)(2,1)}) custom-call(s32[2]{0:T(128)} %pad_add_fusion.where_ref, bf16[128,1024]{1,0:T(8,128)(2,1)} %get-tuple-element.16.refs_0_, bf16[128,1024]{1,0:T(8,128)(2,1)} %copy-done.7, bf16[128,2048]{1,0:T(8,128)(2,1)} %copy-done, bf16[128,2048]{1,0:T(8,128)(2,1)} %copy-done.5), custom_call_target="tpu_custom_call" | custom-call | bytes 3145728 | tf_op jit(solution)/shard_map/finish/pallas_call | solution.py:422
  (3 shorter events, 0.0 us)
Async XLA Ops:
  0.6 30.0 %copy-start.3 = (bf16[128,4096]{1,0:T(8,128)(2,1)S(1)}, bf16[128,4096]{1,0:T(8,128)(2,1)}, u32[]{:S(2)}) copy-start(bf16[128,4096]{1,0:T(8,128)(2,1)} %q_ref.1) | copy-start | bytes 3145732
  0.6 1.9 %collective-permute-start.2 = (bf16[128,1024]{1,0:T(8,128)(2,1)}, bf16[128,1024]{1,0:T(8,128)(2,1)S(1)}, u32[]{:S(2)}, u32[]{:S(2)}) collective-permute-start(bf16[128,1024]{1,0:T(8,128)(2,1)} %k_ref.1), channel_id=1, source_target_pairs={{0,2},{1,3},{2,0},{3,1},{4,6},{5,7},{6,4},{7,5},{8,10},{9,11},{10,... | collective-permute-start | bytes 786440 | tf_op jit(solution)/shard_map/ppermute | solution.py:194
  1.2 1.9 %collective-permute-start.3 = (bf16[128,1024]{1,0:T(8,128)(2,1)}, bf16[128,1024]{1,0:T(8,128)(2,1)}, u32[]{:S(2)}, u32[]{:S(2)}) collective-permute-start(bf16[128,1024]{1,0:T(8,128)(2,1)} %v_ref.1), channel_id=1, source_target_pairs={{0,2},{1,3},{2,0},{3,1},{4,6},{5,7},{6,4},{7,5},{8,10},{9,11},{10,... | collective-permute-start | bytes 786440 | tf_op jit(solution)/shard_map/ppermute | solution.py:194
  1.2 22.0 %collective-permute-start = (bf16[128,4096]{1,0:T(8,128)(2,1)}, bf16[128,4096]{1,0:T(8,128)(2,1)S(1)}, u32[]{:S(2)}, u32[]{:S(2)}) collective-permute-start(bf16[128,4096]{1,0:T(8,128)(2,1)} %q_ref.1), channel_id=1, source_target_pairs={{0,2},{1,3},{2,0},{3,1},{4,6},{5,7},{6,4},{7,5},{8,10},{9,11},{10,... | collective-permute-start | bytes 3145736 | tf_op jit(solution)/shard_map/ppermute | solution.py:194
  1.7 21.6 %collective-permute-start.1 = (bf16[128,4096]{1,0:T(8,128)(2,1)}, bf16[128,4096]{1,0:T(8,128)(2,1)S(1)}, u32[]{:S(2)}, u32[]{:S(2)}) collective-permute-start(bf16[128,4096]{1,0:T(8,128)(2,1)} %do_ref.1), channel_id=1, source_target_pairs={{0,2},{1,3},{2,0},{3,1},{4,6},{5,7},{6,4},{7,5},{8,10},{9,11},{10,... | collective-permute-start | bytes 3145736 | tf_op jit(solution)/shard_map/ppermute | solution.py:194
  2.4 20.7 %copy-start.8 = (s32[8,3]{0,1:T(4,128)S(1)}, s32[8,3]{0,1:T(4,128)}, u32[]{:S(2)}) copy-start(s32[8,3]{0,1:T(4,128)} %param.9) | copy-start | bytes 292
  2.5 0.7 copy-start.6
  5.9 15.2 %collective-permute-start.4 = (bf16[256,1024]{1,0:T(8,128)(2,1)}, bf16[256,1024]{1,0:T(8,128)(2,1)}, u32[]{:S(2)}, u32[]{:S(2)}) collective-permute-start(bf16[256,1024]{1,0:T(8,128)(2,1)} %pack_pairs.1.pair_ref), channel_id=1, source_target_pairs={{0,4},{1,5},{2,3},{3,2},{4,0},{5,1},{6,7},{7,6},{8,12},{9,13},{10,... | collective-permute-start | bytes 1572872 | tf_op jit(solution)/shard_map/ppermute | solution.py:194
  8.8 14.5 %collective-permute-start.5 = (bf16[256,1024]{1,0:T(8,128)(2,1)}, bf16[256,1024]{1,0:T(8,128)(2,1)}, u32[]{:S(2)}, u32[]{:S(2)}) collective-permute-start(bf16[256,1024]{1,0:T(8,128)(2,1)} %pack_pairs.1.pair_ref), channel_id=1, source_target_pairs={{0,1},{1,0},{2,6},{3,7},{4,5},{5,4},{6,2},{7,3},{8,9},{9,8},{10,14... | collective-permute-start | bytes 1572872 | tf_op jit(solution)/shard_map/ppermute | solution.py:194
  21.1 9.5 %collective-permute-start.6 = (bf16[256,1024]{1,0:T(8,128)(2,1)}, bf16[256,1024]{1,0:T(8,128)(2,1)}, u32[]{:S(2)}, u32[]{:S(2)}) collective-permute-start(bf16[256,1024]{1,0:T(8,128)(2,1)} %collective-permute-done.4.near_ref), channel_id=1, source_target_pairs={{0,1},{1,0},{2,6},{3,7},{4,5},{5,4},{6,2},{7,3},{8,9},{9,8},{10,14... | collective-permute-start | bytes 1572872 | tf_op jit(solution)/shard_map/ppermute | solution.py:194
  23.2 7.4 %copy-start.2 = (s32[2]{0:T(128)S(1)}, s32[2]{0:T(128)}, u32[]{:S(2)}) copy-start(s32[2]{0:T(128)} %pad_add_fusion.where_ref) | copy-start | bytes 28
  30.6 1.0 %copy-start.1 = (bf16[256,1024]{1,0:T(8,128)(2,1)S(1)}, bf16[256,1024]{1,0:T(8,128)(2,1)}, u32[]{:S(2)}) copy-start(bf16[256,1024]{1,0:T(8,128)(2,1)} %pack_pairs.1.pair_ref) | copy-start | bytes 1572868
  31.6 1.2 %copy-start.4 = (bf16[128,4096]{1,0:T(8,128)(2,1)S(1)}, bf16[128,4096]{1,0:T(8,128)(2,1)}, u32[]{:S(2)}) copy-start(bf16[128,4096]{1,0:T(8,128)(2,1)} %do_ref.1) | copy-start | bytes 3145732
  56.5 9.4 %copy-start = (bf16[128,2048]{1,0:T(8,128)(2,1)}, bf16[128,2048]{1,0:T(8,128)(2,1)S(1)}, u32[]{:S(2)}) copy-start(bf16[128,2048]{1,0:T(8,128)(2,1)S(1)} %get-tuple-element.13.refs_2_) | copy-start | bytes 1572868
  56.5 9.2 %collective-permute-start.8 = (bf16[256,1024]{1,0:T(8,128)(2,1)S(1)}, bf16[256,1024]{1,0:T(8,128)(2,1)S(1)}, u32[]{:S(2)}, u32[]{:S(2)}) collective-permute-start(bf16[256,1024]{1,0:T(8,128)(2,1)S(1)} %get-tuple-element.12), channel_id=1, source_target_pairs={{0,1},{1,0},{2,6},{3,7},{4,5},{5,4},{6,2},{7,3},{8,9},{9,8},{10,14... | collective-permute-start | bytes 1572872 | tf_op jit(solution)/shard_map/ppermute | solution.py:194
  58.6 17.9 %collective-permute-start.7 = (bf16[256,1024]{1,0:T(8,128)(2,1)S(1)}, bf16[256,1024]{1,0:T(8,128)(2,1)S(1)}, u32[]{:S(2)}, u32[]{:S(2)}) collective-permute-start(bf16[256,1024]{1,0:T(8,128)(2,1)S(1)} %get-tuple-element.10), channel_id=1, source_target_pairs={{0,1},{1,0},{2,6},{3,7},{4,5},{5,4},{6,2},{7,3},{8,9},{9,8},{10,14... | collective-permute-start | bytes 1572872 | tf_op jit(solution)/shard_map/ppermute | solution.py:194
  65.9 10.6 %collective-permute-start.9 = (bf16[256,1024]{1,0:T(8,128)(2,1)S(1)}, bf16[256,1024]{1,0:T(8,128)(2,1)S(1)}, u32[]{:S(2)}, u32[]{:S(2)}) collective-permute-start(bf16[256,1024]{1,0:T(8,128)(2,1)S(1)} %add_convert_fusion.1), channel_id=1, source_target_pairs={{0,4},{1,5},{2,3},{3,2},{4,0},{5,1},{6,7},{7,6},{8,12},{9,13},{10,... | collective-permute-start | bytes 1572872 | tf_op jit(solution)/shard_map/ppermute | solution.py:194
  68.5 9.2 %collective-permute-start.11 = (bf16[128,2048]{1,0:T(8,128)(2,1)S(1)}, bf16[128,2048]{1,0:T(8,128)(2,1)S(1)}, u32[]{:S(2)}, u32[]{:S(2)}) collective-permute-start(bf16[128,2048]{1,0:T(8,128)(2,1)S(1)} %get-tuple-element.14), channel_id=1, source_target_pairs={{0,2},{1,3},{2,0},{3,1},{4,6},{5,7},{6,4},{7,5},{8,10},{9,11},{10,... | collective-permute-start | bytes 1572872 | tf_op jit(solution)/shard_map/ppermute | solution.py:194
  77.5 1.5 %collective-permute-start.10 = (bf16[128,1024]{1,0:T(8,128)(2,1)S(1)}, bf16[128,1024]{1,0:T(8,128)(2,1)S(1)}, u32[]{:S(2)}, u32[]{:S(2)}) collective-permute-start(bf16[128,1024]{1,0:T(8,128)(2,1)S(1)} %get-tuple-element.15), channel_id=1, source_target_pairs={{0,2},{1,3},{2,0},{3,1},{4,6},{5,7},{6,4},{7,5},{8,10},{9,11},{10,... | collective-permute-start | bytes 786440 | tf_op jit(solution)/shard_map/ppermute | solution.py:194
  77.8 1.2 %copy-start.5 = (bf16[128,2048]{1,0:T(8,128)(2,1)}, bf16[128,2048]{1,0:T(8,128)(2,1)S(1)}, u32[]{:S(2)}) copy-start(bf16[128,2048]{1,0:T(8,128)(2,1)S(1)} %collective-permute-done.11.refs_3_) | copy-start | bytes 1572868
  79.0 0.7 copy-start.7

commit v2 on v1

--- a/solution.py
+++ b/solution.py
@@ -172,7 +172,9 @@
 LOG2E = 1.4426950408889634
 PART = 8
 HEAD_HALF = 4
-CHUNKS = 1
+CHUNKS = (2, 2)
+DIRECT = (True, True)
+VMEM_MIB = 48
 HALF_Q = HEAD_HALF * GROUP * HEAD_DIM
 HALF_KV = HEAD_HALF * HEAD_DIM
 PAIR = 2 * BLOCK
@@ -186,6 +188,7 @@
 
 
 SWAP_PERM = perm_to(SWAP, SWAP)
+CORNER_PERM = perm_to(5, 5)
 NEAR_PERM = perm_to(4, 1)
 FAR_PERM = perm_to(1, 4)
 
@@ -194,11 +197,11 @@
     return lax.ppermute(array, AXES, perm)
 
 
-def pack_kernel(chunks, where_ref, k_ref, v_ref, ko_ref, vo_ref, *outs):
-    heads = HEAD_HALF // chunks
-    for chunk in range(chunks):
+def pack_kernel(where_ref, k_ref, v_ref, ko_ref, vo_ref, *outs):
+    for chunk, heads in enumerate(CHUNKS):
         for head in range(heads):
-            src = slice((chunk * heads + head) * HEAD_DIM, (chunk * heads + head + 1) * HEAD_DIM)
+            at = sum(CHUNKS[:chunk]) + head
+            src = slice(at * HEAD_DIM, (at + 1) * HEAD_DIM)
             for side, ref in enumerate((k_ref, v_ref)):
                 cols = slice((2 * head + side) * HEAD_DIM, (2 * head + side + 1) * HEAD_DIM)
                 outs[chunk][0:BLOCK, cols] = ref[:, src]
@@ -208,16 +211,16 @@
 
 
 def pack_pairs(where, keys, values, keys_other, values_other):
-    width = 2 * HALF_KV // CHUNKS
+    shapes = [(PAIR, 2 * HEAD_DIM * heads) for heads in CHUNKS]
     spec = pl.BlockSpec((BLOCK, HALF_KV), lambda g, w: (0, w[0]))
     return pl.pallas_call(
-        partial(pack_kernel, CHUNKS),
-        out_shape=[jax.ShapeDtypeStruct((PAIR, width), jnp.bfloat16)] * CHUNKS,
+        pack_kernel,
+        out_shape=[jax.ShapeDtypeStruct(shape, jnp.bfloat16) for shape in shapes],
         grid_spec=pltpu.PrefetchScalarGridSpec(
             num_scalar_prefetch=1,
             grid=(1,),
             in_specs=[spec] * 4,
-            out_specs=[pl.BlockSpec((PAIR, width), lambda g, w: (0, 0))] * CHUNKS,
+            out_specs=[pl.BlockSpec(shape, lambda g, w: (0, 0)) for shape in shapes],
         ),
         name="pack_pairs",
         cost_estimate=pl.CostEstimate(flops=0, bytes_accessed=2**20, transcendentals=0),
@@ -243,156 +246,176 @@
     corner_out,
     s_ref,
     dp_ref,
-    qcat_ref,
-    docat_ref,
+    q_rows,
+    do_rows,
+    k_rows,
+    v_rows,
     dk_ref,
     dv_ref,
 ):
     scale = HEAD_DIM ** (-0.5)
-    step = pl.program_id(1)
+    factor = scale * LOG2E
     half = where_ref[0]
     me = where_ref[1]
     near = 4 - 3 * half
     far = 1 + 3 * half
-    block = me ^ (SWAP * step)
-    mine = step == 0
-    sources = (pair_ref, near_ref, far_ref, corner_ref)
     deltas = (0, near, far, near ^ far)
-
-    @pl.when(mine)
-    def _():
+    outs = (own_out, near_out, far_out, corner_out)
+    dq_outs = (dq_ref, dqo_ref)
+    rows = GROUP * BLOCK
+    unit = rows // 2
+    units = 2 * rows // unit
+    span = 4 * BLOCK
+    spans = PART * BLOCK // span
+    last = (((1,), (1,)), ((), ()))
+    plain = (((1,), (0,)), ((), ()))
+    first = (((0,), (0,)), ((), ()))
+    dot = partial(lax.dot_general, preferred_element_type=jnp.float32)
+
+    for b, (q, do) in enumerate(((q_ref, do_ref), (qo_ref, doo_ref))):
         for g in range(GROUP):
-            qcat_ref[g * BLOCK : (g + 1) * BLOCK, :] = q_ref[:, g * HEAD_DIM : (g + 1) * HEAD_DIM]
-            docat_ref[g * BLOCK : (g + 1) * BLOCK, :] = do_ref[:, g * HEAD_DIM : (g + 1) * HEAD_DIM]
-        dk_ref[...] = jnp.zeros_like(dk_ref)
-        dv_ref[...] = jnp.zeros_like(dv_ref)
-
-    @pl.when(jnp.logical_not(mine))
-    def _():
-        for g in range(GROUP):
-            qcat_ref[g * BLOCK : (g + 1) * BLOCK, :] = qo_ref[:, g * HEAD_DIM : (g + 1) * HEAD_DIM]
-            docat_ref[g * BLOCK : (g + 1) * BLOCK, :] = doo_ref[
-                :, g * HEAD_DIM : (g + 1) * HEAD_DIM
-            ]
-
-    def count_of(slot):
+            at = slice(b * rows + g * BLOCK, b * rows + (g + 1) * BLOCK)
+            q_rows[at, :] = q[:, g * HEAD_DIM : (g + 1) * HEAD_DIM]
+            do_rows[at, :] = do[:, g * HEAD_DIM : (g + 1) * HEAD_DIM]
+    for place, source in enumerate((pair_ref, near_ref, far_ref, corner_ref)):
+        at = slice(place * PAIR, (place + 1) * PAIR)
+        k_rows[at, :] = source[:, 0:HEAD_DIM]
+        v_rows[at, :] = source[:, HEAD_DIM : 2 * HEAD_DIM]
+
+    def count_of(b, slot):
+        block = me ^ (SWAP * b)
         listed = me ^ deltas[slot // 2] ^ (SWAP * (slot % 2))
-        total = jnp.int32(0)
+        total = (listed < GLOBALS).astype(jnp.int32)
         for w in range(WINDOW):
             total += (lax.rem(block + (w - WINDOW // 2 + PART), PART) == listed).astype(jnp.int32)
-        total += (listed < GLOBALS).astype(jnp.int32)
         for r in range(RANDOMS):
             total += (rand_ref[block * RANDOMS + r] == listed).astype(jnp.int32)
         return total
 
-    counts = [count_of(slot) for slot in range(PART)]
-    qcat = qcat_ref[...]
-    docat = docat_ref[...]
-    rows = GROUP * BLOCK
-    contract_last = (((1,), (1,)), ((), ()))
-    contract = (((1,), (0,)), ((), ()))
-
-    def key_of(slot):
-        base = (slot % 2) * BLOCK
-        return sources[slot // 2][base : base + BLOCK, 0:HEAD_DIM]
-
-    def value_of(slot):
-        base = (slot % 2) * BLOCK
-        return sources[slot // 2][base : base + BLOCK, HEAD_DIM : 2 * HEAD_DIM]
-
-    top = None
-    for slot in range(PART):
-        s = lax.dot_general(key_of(slot), qcat, contract_last, preferred_element_type=jnp.float32)
-        s_ref[slot] = s
-        part = jnp.max(s.reshape(BLOCK // 8, 8, rows), axis=0)
-        part = jnp.where(counts[slot] > 0, part, -1e30)
-        top = part if top is None else jnp.maximum(top, part)
-        dp_ref[slot] = lax.dot_general(
-            value_of(slot), docat, contract_last, preferred_element_type=jnp.float32
-        )
-    factor = scale * LOG2E
-    top = jnp.max(top, axis=0, keepdims=True) * factor
-    total = jnp.zeros((8, rows), jnp.float32)
-    delta = jnp.zeros((8, rows), jnp.float32)
-    for slot in range(PART):
-        shift = jnp.where(counts[slot] > 0, top, 1e30)
-        weight = counts[slot].astype(jnp.float32)
-        e = jnp.exp2(s_ref[slot] * factor - shift)
-        s_ref[slot] = e
-        total += weight * jnp.sum(e.reshape(BLOCK // 8, 8, rows), axis=0)
-        delta += weight * jnp.sum((e * dp_ref[slot]).reshape(BLOCK // 8, 8, rows), axis=0)
-    inverse = 1.0 / jnp.sum(total, axis=0, keepdims=True)
-    delta = jnp.sum(delta, axis=0, keepdims=True) * inverse
-    dq = None
-    for slot in range(PART):
-        p = s_ref[slot] * (counts[slot].astype(jnp.float32) * inverse)
-        ds = (p * (dp_ref[slot] - delta)).astype(jnp.bfloat16)
-        dv_ref[slot] += lax.dot_general(
-            p.astype(jnp.bfloat16), docat, contract, preferred_element_type=jnp.float32
-        )
-        dk_ref[slot] += lax.dot_general(ds, qcat, contract, preferred_element_type=jnp.float32)
-        term = lax.dot_general(
-            key_of(slot).T, ds, contract, preferred_element_type=jnp.float32
-        )
-        dq = term if dq is None else dq + term
-    dq = (dq * scale).T.astype(jnp.bfloat16)
-
-    @pl.when(mine)
-    def _():
-        for g in range(GROUP):
-            dq_ref[:, g * HEAD_DIM : (g + 1) * HEAD_DIM] = dq[g * BLOCK : (g + 1) * BLOCK]
-
-    @pl.when(jnp.logical_not(mine))
-    def _():
-        for g in range(GROUP):
-            dqo_ref[:, g * HEAD_DIM : (g + 1) * HEAD_DIM] = dq[g * BLOCK : (g + 1) * BLOCK]
-        for place, out in enumerate((own_out, near_out, far_out, corner_out)):
-            for r in range(2):
-                base = slice(r * BLOCK, (r + 1) * BLOCK)
-                out[base, 0:HEAD_DIM] = (dk_ref[2 * place + r] * scale).astype(out.dtype)
-                out[base, HEAD_DIM : 2 * HEAD_DIM] = dv_ref[2 * place + r].astype(out.dtype)
+    counts = [[count_of(b, slot) for slot in range(PART)] for b in range(2)]
+
+    def slots_of(u, n):
+        for i in range(span // BLOCK):
+            slot = n * (span // BLOCK) + i
+            yield i, slice(slot * BLOCK, (slot + 1) * BLOCK), counts[u * unit // rows][slot]
+
+    def fold(x, op):
+        return op(x.reshape(BLOCK // 8, 8, unit), axis=0)
+
+    def cols_of(u):
+        return slice(u * unit, (u + 1) * unit)
+
+    def span_of(n):
+        return slice(n * span, (n + 1) * span)
+
+    top, sums, inverse, dq = [None] * units, [None] * units, [None] * units, [None] * units
+
+    def score(u, n):
+        s = dot(k_rows[span_of(n), :], q_rows[cols_of(u), :], last)
+        s_ref[span_of(n), cols_of(u)] = s
+        for i, _, count in slots_of(u, n):
+            part = fold(s[i * BLOCK : (i + 1) * BLOCK], jnp.max)
+            part = jnp.where(count > 0, part, -1e30)
+            top[u] = part if top[u] is None else jnp.maximum(top[u], part)
+        if n == spans - 1:
+            top[u] = jnp.max(top[u], axis=0, keepdims=True) * factor
+
+    def soften(u, n):
+        dp = dot(v_rows[span_of(n), :], do_rows[cols_of(u), :], last)
+        dp_ref[span_of(n), cols_of(u)] = dp
+        for i, at, count in slots_of(u, n):
+            e = jnp.exp2(s_ref[at, cols_of(u)] * factor - jnp.where(count > 0, top[u], 1e30))
+            s_ref[at, cols_of(u)] = e
+            weight = count.astype(jnp.float32)
+            total = weight * fold(e, jnp.sum)
+            delta = weight * fold(e * dp[i * BLOCK : (i + 1) * BLOCK], jnp.sum)
+            sums[u] = (total, delta) if sums[u] is None else (sums[u][0] + total, sums[u][1] + delta)
+        if n == spans - 1:
+            inverse[u] = 1.0 / jnp.sum(sums[u][0], axis=0, keepdims=True)
+            sums[u] = jnp.sum(sums[u][1], axis=0, keepdims=True) * inverse[u]
+
+    def grads(u, n):
+        probs, scores = [], []
+        for _, at, count in slots_of(u, n):
+            p = s_ref[at, cols_of(u)] * (count.astype(jnp.float32) * inverse[u])
+            probs.append(p.astype(jnp.bfloat16))
+            scores.append((p * (dp_ref[at, cols_of(u)] - sums[u])).astype(jnp.bfloat16))
+        probs = jnp.concatenate(probs, axis=0)
+        scores = jnp.concatenate(scores, axis=0)
+        dv = dot(probs, do_rows[cols_of(u), :], plain)
+        dk = dot(scores, q_rows[cols_of(u), :], plain)
+        if u > 0:
+            dv = dv + dv_ref[span_of(n), :]
+            dk = dk + dk_ref[span_of(n), :]
+        if u < units - 1:
+            dv_ref[span_of(n), :] = dv
+            dk_ref[span_of(n), :] = dk
+        else:
+            dk = dk * scale
+            for place in range(span // PAIR):
+                out = outs[n * (span // PAIR) + place]
+                at = slice(place * PAIR, (place + 1) * PAIR)
+                out[:, 0:HEAD_DIM] = dk[at].astype(out.dtype)
+                out[:, HEAD_DIM : 2 * HEAD_DIM] = dv[at].astype(out.dtype)
+        term = dot(k_rows[span_of(n), :], scores, first)
+        dq[u] = term if dq[u] is None else dq[u] + term
+        if n == spans - 1:
+            out = (dq[u] * scale).T.astype(jnp.bfloat16)
+            for i in range(unit // BLOCK):
+                b, g = divmod(u * unit // BLOCK + i, GROUP)
+                dq_outs[b][:, g * HEAD_DIM : (g + 1) * HEAD_DIM] = out[i * BLOCK : (i + 1) * BLOCK]
+
+    stages = (score, soften, grads)
+    for t in range(units + len(stages) - 1):
+        for n in range(spans):
+            for k, stage in enumerate(stages):
+                if 0 <= t - k < units:
+                    stage(t - k, n)
 
 
 def attend(chunk, where, rand, queries, d_out, queries_other, dout_other, sources):
-    heads = HEAD_HALF // CHUNKS
+    heads = CHUNKS[chunk]
     qw = GROUP * HEAD_DIM
     kw = 2 * HEAD_DIM
-    first = chunk * heads
-    q_spec = pl.BlockSpec((BLOCK, qw), lambda j, b, w, r: (0, w[0] * HEAD_HALF + first + j))
-    kv_spec = pl.BlockSpec((PAIR, kw), lambda j, b, w, r: (0, j))
-    dq_spec = pl.BlockSpec((BLOCK, qw), lambda j, b, w, r: (0, j))
+    first = sum(CHUNKS[:chunk])
+    q_spec = pl.BlockSpec((BLOCK, qw), lambda j, w, r: (0, w[0] * HEAD_HALF + first + j))
+    kv_spec = pl.BlockSpec((PAIR, kw), lambda j, w, r: (0, j))
+    dq_spec = pl.BlockSpec((BLOCK, qw), lambda j, w, r: (0, j))
     rows = GROUP * BLOCK
     pairs = 2 * heads * rows * PART * BLOCK
     dq_shape = jax.ShapeDtypeStruct((BLOCK, heads * qw), jnp.bfloat16)
     wide = jax.ShapeDtypeStruct((PAIR, heads * kw), jnp.float32)
     narrow = jax.ShapeDtypeStruct((PAIR, heads * kw), jnp.bfloat16)
+    near_shape = narrow if DIRECT[chunk] else wide
     return pl.pallas_call(
         attend_kernel,
-        out_shape=[dq_shape, dq_shape, wide, wide, narrow, narrow],
+        out_shape=[dq_shape, dq_shape, wide, near_shape, narrow, narrow],
         grid_spec=pltpu.PrefetchScalarGridSpec(
             num_scalar_prefetch=2,
-            grid=(heads, 2),
+            grid=(heads,),
             in_specs=[q_spec] * 4 + [kv_spec] * 4,
             out_specs=[dq_spec] * 2 + [kv_spec] * 4,
             scratch_shapes=[
-                pltpu.VMEM((PART, BLOCK, rows), jnp.float32),
-                pltpu.VMEM((PART, BLOCK, rows), jnp.float32),
-                pltpu.VMEM((rows, HEAD_DIM), jnp.bfloat16),
-                pltpu.VMEM((rows, HEAD_DIM), jnp.bfloat16),
-                pltpu.VMEM((PART, BLOCK, HEAD_DIM), jnp.float32),
-                pltpu.VMEM((PART, BLOCK, HEAD_DIM), jnp.float32),
+                pltpu.VMEM((PART * BLOCK, 2 * rows), jnp.float32),
+                pltpu.VMEM((PART * BLOCK, 2 * rows), jnp.float32),
+                pltpu.VMEM((2 * rows, HEAD_DIM), jnp.bfloat16),
+                pltpu.VMEM((2 * rows, HEAD_DIM), jnp.bfloat16),
+                pltpu.VMEM((PART * BLOCK, HEAD_DIM), jnp.bfloat16),
+                pltpu.VMEM((PART * BLOCK, HEAD_DIM), jnp.bfloat16),
+                pltpu.VMEM((PART * BLOCK, HEAD_DIM), jnp.float32),
+                pltpu.VMEM((PART * BLOCK, HEAD_DIM), jnp.float32),
             ],
         ),
         name="attend",
-        compiler_params=pltpu.CompilerParams(vmem_limit_bytes=24 * 2**20),
+        compiler_params=pltpu.CompilerParams(vmem_limit_bytes=VMEM_MIB * 2**20),
         cost_estimate=pl.CostEstimate(
             flops=10 * pairs * HEAD_DIM * 2, bytes_accessed=4 * 2**20, transcendentals=pairs
         ),
     )(where, rand, queries, d_out, queries_other, dout_other, *sources)
 
 
-def finish_kernel(chunks, where_ref, *refs):
-    heads = HEAD_HALF // chunks
+def finish_kernel(where_ref, *refs):
+    chunks = len(CHUNKS)
     own, other, dq_own, dq_got = (refs[i * chunks : (i + 1) * chunks] for i in range(4))
     dq_ref, dk_ref, dv_ref = refs[4 * chunks :]
     half = where_ref[0]
@@ -401,9 +424,9 @@
         @pl.when(half == value)
         def _():
             for piece, place in ((own, value), (other, 1 - value)):
-                for chunk in range(chunks):
+                for chunk, heads in enumerate(CHUNKS):
                     for head in range(heads):
-                        at = place * HALF_KV + (chunk * heads + head) * HEAD_DIM
+                        at = place * HALF_KV + (sum(CHUNKS[:chunk]) + head) * HEAD_DIM
                         from_col = 2 * head * HEAD_DIM
                         dk_ref[:, at : at + HEAD_DIM] = piece[chunk][
                             0:BLOCK, from_col : from_col + HEAD_DIM
@@ -411,23 +434,23 @@
                         dv_ref[:, at : at + HEAD_DIM] = piece[chunk][
                             0:BLOCK, from_col + HEAD_DIM : from_col + 2 * HEAD_DIM
                         ]
-            width = HALF_Q // chunks
             for piece, place in ((dq_own, value), (dq_got, 1 - value)):
-                for chunk in range(chunks):
-                    at = place * HALF_Q + chunk * width
+                for chunk, heads in enumerate(CHUNKS):
+                    at = place * HALF_Q + sum(CHUNKS[:chunk]) * GROUP * HEAD_DIM
+                    width = heads * GROUP * HEAD_DIM
                     dq_ref[:, at : at + width] = piece[chunk][...]
 
 
 def finish(where, own, other, dq_own, dq_got):
     return pl.pallas_call(
-        partial(finish_kernel, CHUNKS),
+        finish_kernel,
         out_shape=[
             jax.ShapeDtypeStruct((BLOCK, 2 * HALF_Q), jnp.bfloat16),
             jax.ShapeDtypeStruct((BLOCK, 2 * HALF_KV), jnp.bfloat16),
             jax.ShapeDtypeStruct((BLOCK, 2 * HALF_KV), jnp.bfloat16),
         ],
         in_specs=[pl.BlockSpec(memory_space=pltpu.SMEM)]
-        + [pl.BlockSpec(memory_space=pltpu.VMEM)] * (4 * CHUNKS),
+        + [pl.BlockSpec(memory_space=pltpu.VMEM)] * (4 * len(CHUNKS)),
         out_specs=[pl.BlockSpec(memory_space=pltpu.VMEM)] * 3,
         name="finish",
         cost_estimate=pl.CostEstimate(flops=0, bytes_accessed=3 * 2**20, transcendentals=0),
@@ -441,14 +464,15 @@
     rand = rand_blocks.reshape(PART * RANDOMS)
     keys_other = send(keys, SWAP_PERM)
     values_other = send(values, SWAP_PERM)
+    pairs = pack_pairs(where, keys, values, keys_other, values_other)
+    queries, d_out, pairs = lax.optimization_barrier((queries, d_out, pairs))
     queries_other = send(queries, SWAP_PERM)
     dout_other = send(d_out, SWAP_PERM)
-    pairs = pack_pairs(where, keys, values, keys_other, values_other)
     nears = [send(pair, NEAR_PERM) for pair in pairs]
     fars = [send(pair, FAR_PERM) for pair in pairs]
     corners = [send(near, FAR_PERM) for near in nears]
     own, other, dq_own, dq_got = [], [], [], []
-    for chunk in range(CHUNKS):
+    for chunk in range(len(CHUNKS)):
         dq_mine, dq_other, own_grads, near_grads, far_grads, corner_grads = attend(
             chunk,
             where,
@@ -459,11 +483,14 @@
             dout_other,
             (pairs[chunk], nears[chunk], fars[chunk], corners[chunk]),
         )
-        from_corner = send(corner_grads, FAR_PERM)
-        from_far = send(far_grads, FAR_PERM)
-        relayed = (near_grads + from_corner.astype(jnp.float32)).astype(jnp.bfloat16)
-        from_near = send(relayed, NEAR_PERM)
-        total = own_grads + from_far.astype(jnp.float32) + from_near.astype(jnp.float32)
+        if DIRECT[chunk]:
+            arrived = [send(corner_grads, CORNER_PERM), send(near_grads, NEAR_PERM)]
+        else:
+            from_corner = send(corner_grads, FAR_PERM)
+            relayed = (near_grads + from_corner.astype(jnp.float32)).astype(jnp.bfloat16)
+            arrived = [send(relayed, NEAR_PERM)]
+        arrived.append(send(far_grads, FAR_PERM))
+        total = own_grads + sum(x.astype(jnp.float32) for x in arrived)
         total = total.astype(jnp.bfloat16)
         own.append(total[:BLOCK])
         other.append(send(total[BLOCK:], SWAP_PERM))

time: 83 us -> 68.5 us (0.83)
  waiting for transfers between devices: 35 us -> 19.3 us
  Pallas kernels: 29 us -> 22.8 us
  starting transfers between devices: 12.6 us -> 18.4 us
  local copies, waits for them, and re-layouts: 4.07 us -> 6.08 us
    ppermute x12 -> x20, waiting for transfers between devices: 35 us -> 19.3 us  [send(): return lax.ppermute(array, AXES, perm)]
    pallas_call x3 -> x4, Pallas kernels: 29 us -> 22.8 us  [the longest x2 17.4 us: attend(): pl.pallas_call(attend_kernel, out_shape=[dq_shape, dq_shape, wide, near_s...]
    ppermute x12 -> x20, starting transfers between devices: 12.6 us -> 18.4 us  [send(): return lax.ppermute(array, AXES, perm)]
    unnamed x19 -> x29, local copies, waits for them, and re-layouts: 3.25 us -> 4.65 us
  transfers between devices with their start and end apart: 12 -> 20, of which waited for: 7 -> 8; matrix products, arithmetic and copies ran while one was open for 2% -> 4% of each run, Pallas kernels for 3% -> 25%
where the time goes in v2:
time: 68.5 us; the launch traced here: 68.3 us
  Pallas kernels  22.8 us (33%)
  waiting for transfers between devices  19.3 us (28%)
  starting transfers between devices  18.4 us (27%)
  local copies, waits for them, and re-layouts  6.08 us (9%)
  other arithmetic  0.97 us (1%)
  between operations  0.78 us (1%)
    ppermute x20, waiting for transfers between devices, send(): return lax.ppermute(array, AXES, perm)  19.3 us
    ppermute x20, starting transfers between devices, send(): return lax.ppermute(array, AXES, perm)  18.4 us
    pallas_call x2, Pallas kernels, attend(): pl.pallas_call(attend_kernel, out_shape=[dq_shape, dq_shape, wide, near_s...  17.4 us
    unnamed x29, local copies, waits for them, and re-layouts  4.65 us
    pallas_call x1, Pallas kernels, finish(): pl.pallas_call(finish_kernel, out_shape=[jax.ShapeDtypeStruct((BLOCK, 2 *...  2.76 us
    pallas_call x1, Pallas kernels, pack_pairs(): pl.pallas_call(pack_kernel, out_shape=[jax.ShapeDtypeStruct(shape, jnp.bf...  2.63 us
  transfers between devices with their start and end apart: 20, of which 8 were waited for; matrix products, arithmetic and copies ran while one was open for 4% of the time, Pallas kernels for 25%

profile of v2, /device:TPU:0, one launch (start us, length us, event | category | flops | bytes accessed | tf_op | source)
XLA Modules:
  0.0 68.3 jit_solution(2552153844730580048)
XLA Ops:
  0.6 0.5 collective-permute-start
  1.2 0.1 collective-permute-start.1
  1.2 0.7 pad_add_fusion.where_ref
  1.9 0.6 collective-permute-done.ko_ref
  2.5 0.4 collective-permute-done.1.vo_ref
  2.9 0.3 copy-done.9
  3.2 0.7 %copy-done.10 = bf16[128,1024]{1,0:T(8,128)(2,1)} copy-done((bf16[128,1024]{1,0:T(8,128)(2,1)}, bf16[128,1024]{1,0:T(8,128)(2,1)S(1)}, u32[]{:S(2)}) %copy-start.10) | copy-done | bytes 262168
  3.9 2.6 %pack_pairs.1 = (bf16[256,512]{1,0:T(8,128)(2,1)}, bf16[256,512]{1,0:T(8,128)(2,1)}) custom-call(s32[2]{0:T(128)} %pad_add_fusion.where_ref, bf16[128,1024]{1,0:T(8,128)(2,1)} %k_ref.1, bf16[128,1024]{1,0:T(8,128)(2,1)} %v_ref.1, bf16[128,1024]{1,0:T(8,128)(2,1)} %copy-done.9, bf16[128,1024]{1,0:T(8,128)(2,1)} %copy-done.10), custom_call_target="tpu_custom_call" | custom-call | bytes 1048576 | tf_op jit(solution)/shard_map/pack_pairs/pallas_call | solution.py:216
  6.6 0.4 collective-permute-start.2
  7.0 0.1 collective-permute-start.3
  7.1 2.9 %collective-permute-start.10 = (bf16[256,512]{1,0:T(8,128)(2,1)}, bf16[256,512]{1,0:T(8,128)(2,1)S(1)}, u32[]{:S(2)}, u32[]{:S(2)}) collective-permute-start(bf16[256,512]{1,0:T(8,128)(2,1)} %get-tuple-element.30.pair_ref), channel_id=1, source_target_pairs={{0,4},{1,5},{2,3},{3,2},{4,0},{5,1},{6,7},{7,6},{8,12},{9,13},{10,... | collective-permute-start | bytes 786440 | tf_op jit(solution)/shard_map/ppermute | solution.py:197
  10.0 1.5 %collective-permute-start.11 = (bf16[256,512]{1,0:T(8,128)(2,1)}, bf16[256,512]{1,0:T(8,128)(2,1)S(1)}, u32[]{:S(2)}, u32[]{:S(2)}) collective-permute-start(bf16[256,512]{1,0:T(8,128)(2,1)} %get-tuple-element.30.pair_ref), channel_id=1, source_target_pairs={{0,1},{1,0},{2,6},{3,7},{4,5},{5,4},{6,2},{7,3},{8,9},{9,8},{10,14... | collective-permute-start | bytes 786440 | tf_op jit(solution)/shard_map/ppermute | solution.py:197
  11.5 0.5 collective-permute-start.4
  12.0 4.6 %collective-permute-done.10.near_ref = bf16[256,512]{1,0:T(8,128)(2,1)S(1)} collective-permute-done((bf16[256,512]{1,0:T(8,128)(2,1)}, bf16[256,512]{1,0:T(8,128)(2,1)S(1)}, u32[]{:S(2)}, u32[]{:S(2)}) %collective-permute-start.10) | collective-permute-done | bytes 262176 | tf_op jit(solution)/shard_map/ppermute | solution.py:197
  16.7 1.9 %collective-permute-start.12 = (bf16[256,512]{1,0:T(8,128)(2,1)S(1)}, bf16[256,512]{1,0:T(8,128)(2,1)S(1)}, u32[]{:S(2)}, u32[]{:S(2)}) collective-permute-start(bf16[256,512]{1,0:T(8,128)(2,1)S(1)} %collective-permute-done.10.near_ref), channel_id=1, source_target_pairs={{0,1},{1,0},{2,6},{3,7},{4,5},{5,4},{6,2},{7,3},{8,9},{9,8},{10,14... | collective-permute-start | bytes 786440 | tf_op jit(solution)/shard_map/ppermute | solution.py:197
  18.6 0.1 copy.9
  18.6 0.1 reshape.9.rand_ref
  18.7 0.7 %collective-permute-done.11.far_ref = bf16[256,512]{1,0:T(8,128)(2,1)S(1)} collective-permute-done((bf16[256,512]{1,0:T(8,128)(2,1)}, bf16[256,512]{1,0:T(8,128)(2,1)S(1)}, u32[]{:S(2)}, u32[]{:S(2)}) %collective-permute-start.11) | collective-permute-done | bytes 262176 | tf_op jit(solution)/shard_map/ppermute | solution.py:197
  19.4 1.5 %collective-permute-start.5 = (bf16[256,512]{1,0:T(8,128)(2,1)}, bf16[256,512]{1,0:T(8,128)(2,1)S(1)}, u32[]{:S(2)}, u32[]{:S(2)}) collective-permute-start(bf16[256,512]{1,0:T(8,128)(2,1)} %get-tuple-element.25.pair_ref), channel_id=1, source_target_pairs={{0,1},{1,0},{2,6},{3,7},{4,5},{5,4},{6,2},{7,3},{8,9},{9,8},{10,14... | collective-permute-start | bytes 786440 | tf_op jit(solution)/shard_map/ppermute | solution.py:197
  21.0 0.7 collective-permute-done.4.near_ref
  21.6 1.5 %collective-permute-start.6 = (bf16[256,512]{1,0:T(8,128)(2,1)S(1)}, bf16[256,512]{1,0:T(8,128)(2,1)S(1)}, u32[]{:S(2)}, u32[]{:S(2)}) collective-permute-start(bf16[256,512]{1,0:T(8,128)(2,1)S(1)} %collective-permute-done.4.near_ref), channel_id=1, source_target_pairs={{0,1},{1,0},{2,6},{3,7},{4,5},{5,4},{6,2},{7,3},{8,9},{9,8},{10,14... | collective-permute-start | bytes 786440 | tf_op jit(solution)/shard_map/ppermute | solution.py:197
  23.1 0.0 collective-permute-done.12.corner_ref
  23.1 0.0 collective-permute-done.2.qo_ref
  23.1 0.0 collective-permute-done.3.doo_ref
  23.1 0.0 copy-start.4
  23.1 1.2 %copy-done.4 = bf16[128,4096]{1,0:T(8,128)(2,1)S(1)} copy-done((bf16[128,4096]{1,0:T(8,128)(2,1)S(1)}, bf16[128,4096]{1,0:T(8,128)(2,1)}, u32[]{:S(2)}) %copy-start.4) | copy-done | bytes 1048600
  24.3 0.9 %copy-done.6 = bf16[256,512]{1,0:T(8,128)(2,1)S(1)} copy-done((bf16[256,512]{1,0:T(8,128)(2,1)S(1)}, bf16[256,512]{1,0:T(8,128)(2,1)}, u32[]{:S(2)}) %copy-start.6) | copy-done | bytes 262168
  25.3 8.7 %attend.3 = (bf16[128,1024]{1,0:T(8,128)(2,1)S(1)}, bf16[128,1024]{1,0:T(8,128)(2,1)S(1)}, f32[256,512]{1,0:T(8,128)S(1)}, bf16[256,512]{1,0:T(8,128)(2,1)S(1)},...) custom-call(s32[2]{0:T(128)S(1)} %copy-done.2, s32[24]{0:T(128)S(1)} %reshape.9.rand_ref, ...), custom_call_target="tpu_custom_call" | custom-call | flops 5368709120 | bytes 4194304 | tf_op jit(solution)/shard_map/attend/pallas_call | solution.py:390
  34.0 0.7 copy-done
  34.7 3.0 %collective-permute-start.13 = (bf16[256,512]{1,0:T(8,128)(2,1)S(1)}, bf16[256,512]{1,0:T(8,128)(2,1)S(1)}, u32[]{:S(2)}, u32[]{:S(2)}) collective-permute-start(bf16[256,512]{1,0:T(8,128)(2,1)S(1)} %get-tuple-element.32), channel_id=1, source_target_pairs={{0,5},{1,4},{2,7},{3,6},{4,1},{5,0},{6,3},{7,2},{8,13},{9,12},{10,... | collective-permute-start | bytes 786440 | tf_op jit(solution)/shard_map/ppermute | solution.py:197
  37.7 0.3 collective-permute-start.14
  38.0 0.5 collective-permute-start.15
  38.5 8.7 %attend.2 = (bf16[128,1024]{1,0:T(8,128)(2,1)S(1)}, bf16[128,1024]{1,0:T(8,128)(2,1)S(1)}, f32[256,512]{1,0:T(8,128)S(1)}, bf16[256,512]{1,0:T(8,128)(2,1)S(1)},...) custom-call(s32[2]{0:T(128)S(1)} %copy-done.2, s32[24]{0:T(128)S(1)} %reshape.9.rand_ref, ...), custom_call_target="tpu_custom_call" | custom-call | flops 5368709120 | bytes 4194304 | tf_op jit(solution)/shard_map/attend/pallas_call | solution.py:390
  47.2 2.7 %collective-permute-start.7 = (bf16[256,512]{1,0:T(8,128)(2,1)S(1)}, bf16[256,512]{1,0:T(8,128)(2,1)S(1)}, u32[]{:S(2)}, u32[]{:S(2)}) collective-permute-start(bf16[256,512]{1,0:T(8,128)(2,1)S(1)} %get-tuple-element.27), channel_id=1, source_target_pairs={{0,5},{1,4},{2,7},{3,6},{4,1},{5,0},{6,3},{7,2},{8,13},{9,12},{10,... | collective-permute-start | bytes 786440 | tf_op jit(solution)/shard_map/ppermute | solution.py:197
  50.0 0.0 collective-permute-done.13
  50.0 0.3 collective-permute-start.8
  50.3 0.6 collective-permute-start.9
  50.8 0.0 collective-permute-done.15
  50.8 0.0 collective-permute-start.18
  50.9 0.2 add_convert_fusion
  51.0 0.7 fusion
  51.7 5.6 %collective-permute-done.7 = bf16[256,512]{1,0:T(8,128)(2,1)S(1)} collective-permute-done((bf16[256,512]{1,0:T(8,128)(2,1)S(1)}, bf16[256,512]{1,0:T(8,128)(2,1)S(1)}, u32[]{:S(2)}, u32[]{:S(2)}) %collective-permute-start.7) | collective-permute-done | bytes 262176 | tf_op jit(solution)/shard_map/ppermute | solution.py:197
  57.3 5.3 %collective-permute-done.8 = bf16[256,512]{1,0:T(8,128)(2,1)S(1)} collective-permute-done((bf16[256,512]{1,0:T(8,128)(2,1)S(1)}, bf16[256,512]{1,0:T(8,128)(2,1)S(1)}, u32[]{:S(2)}, u32[]{:S(2)}) %collective-permute-start.8) | collective-permute-done | bytes 262176 | tf_op jit(solution)/shard_map/ppermute | solution.py:197
  62.6 0.2 add_convert_fusion.1
  62.8 0.7 fusion.1
  63.5 1.3 %collective-permute-done.16.refs_2_ = bf16[128,512]{1,0:T(8,128)(2,1)S(1)} collective-permute-done((bf16[128,512]{1,0:T(8,128)(2,1)S(1)}, bf16[128,512]{1,0:T(8,128)(2,1)S(1)}, u32[]{:S(2)}, u32[]{:S(2)}) %collective-permute-start.16) | collective-permute-done | bytes 131104 | tf_op jit(solution)/shard_map/ppermute | solution.py:197
  64.8 0.7 copy-done.12
  65.5 2.8 %finish.1 = (bf16[128,4096]{1,0:T(8,128)(2,1)}, bf16[128,1024]{1,0:T(8,128)(2,1)}, bf16[128,1024]{1,0:T(8,128)(2,1)}) custom-call(s32[2]{0:T(128)} %pad_add_fusion.where_ref, bf16[128,512]{1,0:T(8,128)(2,1)} %get-tuple-element.42.refs_0_, bf16[128,512]{1,0:T(8,128)(2,1)} %get-tuple-element.40.refs_1_, bf16[128,512]{1,0:T(8,128)(2,1)} %copy-done.12, ...), custom_call_target="tpu_custom_call" | custom-call | bytes 3145728 | tf_op jit(solution)/shard_map/finish/pallas_call | solution.py:445
  (31 shorter events, 0.1 us)
Async XLA Ops:
  0.6 5.9 %copy-start.3 = (bf16[128,4096]{1,0:T(8,128)(2,1)S(1)}, bf16[128,4096]{1,0:T(8,128)(2,1)}, u32[]{:S(2)}) copy-start(bf16[128,4096]{1,0:T(8,128)(2,1)} %q_ref.1) | copy-start | bytes 3145732
  0.6 1.9 %collective-permute-start = (bf16[128,1024]{1,0:T(8,128)(2,1)}, bf16[128,1024]{1,0:T(8,128)(2,1)S(1)}, u32[]{:S(2)}, u32[]{:S(2)}) collective-permute-start(bf16[128,1024]{1,0:T(8,128)(2,1)} %k_ref.1), channel_id=1, source_target_pairs={{0,2},{1,3},{2,0},{3,1},{4,6},{5,7},{6,4},{7,5},{8,10},{9,11},{10,... | collective-permute-start | bytes 786440 | tf_op jit(solution)/shard_map/ppermute | solution.py:197
  1.2 1.7 %collective-permute-start.1 = (bf16[128,1024]{1,0:T(8,128)(2,1)}, bf16[128,1024]{1,0:T(8,128)(2,1)S(1)}, u32[]{:S(2)}, u32[]{:S(2)}) collective-permute-start(bf16[128,1024]{1,0:T(8,128)(2,1)} %v_ref.1), channel_id=1, source_target_pairs={{0,2},{1,3},{2,0},{3,1},{4,6},{5,7},{6,4},{7,5},{8,10},{9,11},{10,... | collective-permute-start | bytes 786440 | tf_op jit(solution)/shard_map/ppermute | solution.py:197
  2.5 0.7 %copy-start.9 = (bf16[128,1024]{1,0:T(8,128)(2,1)}, bf16[128,1024]{1,0:T(8,128)(2,1)S(1)}, u32[]{:S(2)}) copy-start(bf16[128,1024]{1,0:T(8,128)(2,1)S(1)} %collective-permute-done.ko_ref) | copy-start | bytes 786436
  3.2 0.7 %copy-start.10 = (bf16[128,1024]{1,0:T(8,128)(2,1)}, bf16[128,1024]{1,0:T(8,128)(2,1)S(1)}, u32[]{:S(2)}) copy-start(bf16[128,1024]{1,0:T(8,128)(2,1)S(1)} %collective-permute-done.1.vo_ref) | copy-start | bytes 786436
  6.6 12.0 %copy-start.13 = (s32[8,3]{0,1:T(4,128)S(1)}, s32[8,3]{0,1:T(4,128)}, u32[]{:S(2)}) copy-start(s32[8,3]{0,1:T(4,128)} %param.9) | copy-start | bytes 292
  6.6 16.5 %collective-permute-start.2 = (bf16[128,4096]{1,0:T(8,128)(2,1)S(1)}, bf16[128,4096]{1,0:T(8,128)(2,1)S(1)}, u32[]{:S(2)}, u32[]{:S(2)}) collective-permute-start(bf16[128,4096]{1,0:T(8,128)(2,1)S(1)} %copy-done.3), channel_id=1, source_target_pairs={{0,2},{1,3},{2,0},{3,1},{4,6},{5,7},{6,4},{7,5},{8,10},{9,11},{10,... | collective-permute-start | bytes 3145736 | tf_op jit(solution)/shard_map/ppermute | solution.py:197
  7.0 16.1 %collective-permute-start.3 = (bf16[128,4096]{1,0:T(8,128)(2,1)}, bf16[128,4096]{1,0:T(8,128)(2,1)}, u32[]{:S(2)}, u32[]{:S(2)}) collective-permute-start(bf16[128,4096]{1,0:T(8,128)(2,1)} %do_ref.1), channel_id=1, source_target_pairs={{0,2},{1,3},{2,0},{3,1},{4,6},{5,7},{6,4},{7,5},{8,10},{9,11},{10,... | collective-permute-start | bytes 3145736 | tf_op jit(solution)/shard_map/ppermute | solution.py:197
  7.1 9.6 %collective-permute-start.10 = (bf16[256,512]{1,0:T(8,128)(2,1)}, bf16[256,512]{1,0:T(8,128)(2,1)S(1)}, u32[]{:S(2)}, u32[]{:S(2)}) collective-permute-start(bf16[256,512]{1,0:T(8,128)(2,1)} %get-tuple-element.30.pair_ref), channel_id=1, source_target_pairs={{0,4},{1,5},{2,3},{3,2},{4,0},{5,1},{6,7},{7,6},{8,12},{9,13},{10,... | collective-permute-start | bytes 786440 | tf_op jit(solution)/shard_map/ppermute | solution.py:197
  10.0 9.5 %collective-permute-start.11 = (bf16[256,512]{1,0:T(8,128)(2,1)}, bf16[256,512]{1,0:T(8,128)(2,1)S(1)}, u32[]{:S(2)}, u32[]{:S(2)}) collective-permute-start(bf16[256,512]{1,0:T(8,128)(2,1)} %get-tuple-element.30.pair_ref), channel_id=1, source_target_pairs={{0,1},{1,0},{2,6},{3,7},{4,5},{5,4},{6,2},{7,3},{8,9},{9,8},{10,14... | collective-permute-start | bytes 786440 | tf_op jit(solution)/shard_map/ppermute | solution.py:197
  11.5 10.1 %collective-permute-start.4 = (bf16[256,512]{1,0:T(8,128)(2,1)}, bf16[256,512]{1,0:T(8,128)(2,1)S(1)}, u32[]{:S(2)}, u32[]{:S(2)}) collective-permute-start(bf16[256,512]{1,0:T(8,128)(2,1)} %get-tuple-element.25.pair_ref), channel_id=1, source_target_pairs={{0,4},{1,5},{2,3},{3,2},{4,0},{5,1},{6,7},{7,6},{8,12},{9,13},{10,... | collective-permute-start | bytes 786440 | tf_op jit(solution)/shard_map/ppermute | solution.py:197
  16.7 6.4 %collective-permute-start.12 = (bf16[256,512]{1,0:T(8,128)(2,1)S(1)}, bf16[256,512]{1,0:T(8,128)(2,1)S(1)}, u32[]{:S(2)}, u32[]{:S(2)}) collective-permute-start(bf16[256,512]{1,0:T(8,128)(2,1)S(1)} %collective-permute-done.10.near_ref), channel_id=1, source_target_pairs={{0,1},{1,0},{2,6},{3,7},{4,5},{5,4},{6,2},{7,3},{8,9},{9,8},{10,14... | collective-permute-start | bytes 786440 | tf_op jit(solution)/shard_map/ppermute | solution.py:197
  18.6 4.5 %copy-start.2 = (s32[2]{0:T(128)S(1)}, s32[2]{0:T(128)}, u32[]{:S(2)}) copy-start(s32[2]{0:T(128)} %pad_add_fusion.where_ref) | copy-start | bytes 28
  19.4 19.1 %collective-permute-start.5 = (bf16[256,512]{1,0:T(8,128)(2,1)}, bf16[256,512]{1,0:T(8,128)(2,1)S(1)}, u32[]{:S(2)}, u32[]{:S(2)}) collective-permute-start(bf16[256,512]{1,0:T(8,128)(2,1)} %get-tuple-element.25.pair_ref), channel_id=1, source_target_pairs={{0,1},{1,0},{2,6},{3,7},{4,5},{5,4},{6,2},{7,3},{8,9},{9,8},{10,14... | collective-permute-start | bytes 786440 | tf_op jit(solution)/shard_map/ppermute | solution.py:197
  21.6 16.9 %collective-permute-start.6 = (bf16[256,512]{1,0:T(8,128)(2,1)S(1)}, bf16[256,512]{1,0:T(8,128)(2,1)S(1)}, u32[]{:S(2)}, u32[]{:S(2)}) collective-permute-start(bf16[256,512]{1,0:T(8,128)(2,1)S(1)} %collective-permute-done.4.near_ref), channel_id=1, source_target_pairs={{0,1},{1,0},{2,6},{3,7},{4,5},{5,4},{6,2},{7,3},{8,9},{9,8},{10,14... | collective-permute-start | bytes 786440 | tf_op jit(solution)/shard_map/ppermute | solution.py:197
  23.1 1.2 %copy-start.4 = (bf16[128,4096]{1,0:T(8,128)(2,1)S(1)}, bf16[128,4096]{1,0:T(8,128)(2,1)}, u32[]{:S(2)}) copy-start(bf16[128,4096]{1,0:T(8,128)(2,1)} %do_ref.1) | copy-start | bytes 3145732
  24.3 0.9 %copy-start.6 = (bf16[256,512]{1,0:T(8,128)(2,1)S(1)}, bf16[256,512]{1,0:T(8,128)(2,1)}, u32[]{:S(2)}) copy-start(bf16[256,512]{1,0:T(8,128)(2,1)} %get-tuple-element.30.pair_ref) | copy-start | bytes 786436
  25.3 13.2 %copy-start.5 = (bf16[256,512]{1,0:T(8,128)(2,1)S(1)}, bf16[256,512]{1,0:T(8,128)(2,1)}, u32[]{:S(2)}) copy-start(bf16[256,512]{1,0:T(8,128)(2,1)} %get-tuple-element.25.pair_ref) | copy-start | bytes 786436
  34.0 0.7 %copy-start = (bf16[128,1024]{1,0:T(8,128)(2,1)}, bf16[128,1024]{1,0:T(8,128)(2,1)S(1)}, u32[]{:S(2)}) copy-start(bf16[128,1024]{1,0:T(8,128)(2,1)S(1)} %get-tuple-element.36.refs_5_) | copy-start | bytes 786436
  34.7 15.3 %collective-permute-start.13 = (bf16[256,512]{1,0:T(8,128)(2,1)S(1)}, bf16[256,512]{1,0:T(8,128)(2,1)S(1)}, u32[]{:S(2)}, u32[]{:S(2)}) collective-permute-start(bf16[256,512]{1,0:T(8,128)(2,1)S(1)} %get-tuple-element.32), channel_id=1, source_target_pairs={{0,5},{1,4},{2,7},{3,6},{4,1},{5,0},{6,3},{7,2},{8,13},{9,12},{10,... | collective-permute-start | bytes 786440 | tf_op jit(solution)/shard_map/ppermute | solution.py:197
  37.7 12.6 %collective-permute-start.14 = (bf16[256,512]{1,0:T(8,128)(2,1)S(1)}, bf16[256,512]{1,0:T(8,128)(2,1)S(1)}, u32[]{:S(2)}, u32[]{:S(2)}) collective-permute-start(bf16[256,512]{1,0:T(8,128)(2,1)S(1)} %get-tuple-element.33), channel_id=1, source_target_pairs={{0,4},{1,5},{2,3},{3,2},{4,0},{5,1},{6,7},{7,6},{8,12},{9,13},{10,... | collective-permute-start | bytes 786440 | tf_op jit(solution)/shard_map/ppermute | solution.py:197
  38.0 12.9 %collective-permute-start.15 = (bf16[256,512]{1,0:T(8,128)(2,1)S(1)}, bf16[256,512]{1,0:T(8,128)(2,1)S(1)}, u32[]{:S(2)}, u32[]{:S(2)}) collective-permute-start(bf16[256,512]{1,0:T(8,128)(2,1)S(1)} %get-tuple-element.34), channel_id=1, source_target_pairs={{0,1},{1,0},{2,6},{3,7},{4,5},{5,4},{6,2},{7,3},{8,9},{9,8},{10,14... | collective-permute-start | bytes 786440 | tf_op jit(solution)/shard_map/ppermute | solution.py:197
  38.5 25.0 %collective-permute-start.19 = (bf16[128,1024]{1,0:T(8,128)(2,1)S(1)}, bf16[128,1024]{1,0:T(8,128)(2,1)S(1)}, u32[]{:S(2)}, u32[]{:S(2)}) collective-permute-start(bf16[128,1024]{1,0:T(8,128)(2,1)S(1)} %get-tuple-element.38), channel_id=1, source_target_pairs={{0,2},{1,3},{2,0},{3,1},{4,6},{5,7},{6,4},{7,5},{8,10},{9,11},{10,... | collective-permute-start | bytes 786440 | tf_op jit(solution)/shard_map/ppermute | solution.py:197
  47.2 3.8 %copy-start.1 = (bf16[128,1024]{1,0:T(8,128)(2,1)}, bf16[128,1024]{1,0:T(8,128)(2,1)S(1)}, u32[]{:S(2)}) copy-start(bf16[128,1024]{1,0:T(8,128)(2,1)S(1)} %get-tuple-element.35.refs_4_) | copy-start | bytes 786436
  47.2 10.1 %collective-permute-start.7 = (bf16[256,512]{1,0:T(8,128)(2,1)S(1)}, bf16[256,512]{1,0:T(8,128)(2,1)S(1)}, u32[]{:S(2)}, u32[]{:S(2)}) collective-permute-start(bf16[256,512]{1,0:T(8,128)(2,1)S(1)} %get-tuple-element.27), channel_id=1, source_target_pairs={{0,5},{1,4},{2,7},{3,6},{4,1},{5,0},{6,3},{7,2},{8,13},{9,12},{10,... | collective-permute-start | bytes 786440 | tf_op jit(solution)/shard_map/ppermute | solution.py:197
  50.0 12.7 %collective-permute-start.8 = (bf16[256,512]{1,0:T(8,128)(2,1)S(1)}, bf16[256,512]{1,0:T(8,128)(2,1)S(1)}, u32[]{:S(2)}, u32[]{:S(2)}) collective-permute-start(bf16[256,512]{1,0:T(8,128)(2,1)S(1)} %get-tuple-element.28), channel_id=1, source_target_pairs={{0,4},{1,5},{2,3},{3,2},{4,0},{5,1},{6,7},{7,6},{8,12},{9,13},{10,... | collective-permute-start | bytes 786440 | tf_op jit(solution)/shard_map/ppermute | solution.py:197
  50.3 12.3 %collective-permute-start.9 = (bf16[256,512]{1,0:T(8,128)(2,1)S(1)}, bf16[256,512]{1,0:T(8,128)(2,1)S(1)}, u32[]{:S(2)}, u32[]{:S(2)}) collective-permute-start(bf16[256,512]{1,0:T(8,128)(2,1)S(1)} %get-tuple-element.29), channel_id=1, source_target_pairs={{0,1},{1,0},{2,6},{3,7},{4,5},{5,4},{6,2},{7,3},{8,9},{9,8},{10,14... | collective-permute-start | bytes 786440 | tf_op jit(solution)/shard_map/ppermute | solution.py:197
  50.8 12.6 %collective-permute-start.18 = (bf16[128,1024]{1,0:T(8,128)(2,1)S(1)}, bf16[128,1024]{1,0:T(8,128)(2,1)S(1)}, u32[]{:S(2)}, u32[]{:S(2)}) collective-permute-start(bf16[128,1024]{1,0:T(8,128)(2,1)S(1)} %get-tuple-element.37), channel_id=1, source_target_pairs={{0,2},{1,3},{2,0},{3,1},{4,6},{5,7},{6,4},{7,5},{8,10},{9,11},{10,... | collective-permute-start | bytes 786440 | tf_op jit(solution)/shard_map/ppermute | solution.py:197
  57.3 6.2 %collective-permute-start.17 = (bf16[128,512]{1,0:T(8,128)(2,1)S(1)}, bf16[128,512]{1,0:T(8,128)(2,1)S(1)}, u32[]{:S(2)}, u32[]{:S(2)}) collective-permute-start(bf16[128,512]{1,0:T(8,128)(2,1)S(1)} %get-tuple-element.39), channel_id=1, source_target_pairs={{0,2},{1,3},{2,0},{3,1},{4,6},{5,7},{6,4},{7,5},{8,10},{9,11},{10,... | collective-permute-start | bytes 393224 | tf_op jit(solution)/shard_map/ppermute | solution.py:197
  63.5 1.3 %collective-permute-start.16 = (bf16[128,512]{1,0:T(8,128)(2,1)S(1)}, bf16[128,512]{1,0:T(8,128)(2,1)S(1)}, u32[]{:S(2)}, u32[]{:S(2)}) collective-permute-start(bf16[128,512]{1,0:T(8,128)(2,1)S(1)} %get-tuple-element.41), channel_id=1, source_target_pairs={{0,2},{1,3},{2,0},{3,1},{4,6},{5,7},{6,4},{7,5},{8,10},{9,11},{10,... | collective-permute-start | bytes 393224 | tf_op jit(solution)/shard_map/ppermute | solution.py:197
  63.5 1.3 %copy-start.7 = (bf16[128,1024]{1,0:T(8,128)(2,1)}, bf16[128,1024]{1,0:T(8,128)(2,1)S(1)}, u32[]{:S(2)}) copy-start(bf16[128,1024]{1,0:T(8,128)(2,1)S(1)} %collective-permute-done.19.refs_7_) | copy-start | bytes 786436
  63.5 1.3 %copy-start.8 = (bf16[128,1024]{1,0:T(8,128)(2,1)}, bf16[128,1024]{1,0:T(8,128)(2,1)S(1)}, u32[]{:S(2)}) copy-start(bf16[128,1024]{1,0:T(8,128)(2,1)S(1)} %collective-permute-done.18.refs_6_) | copy-start | bytes 786436
  63.5 1.3 %copy-start.11 = (bf16[128,512]{1,0:T(8,128)(2,1)}, bf16[128,512]{1,0:T(8,128)(2,1)S(1)}, u32[]{:S(2)}) copy-start(bf16[128,512]{1,0:T(8,128)(2,1)S(1)} %collective-permute-done.17.refs_3_) | copy-start | bytes 393220
  64.8 0.7 copy-start.12

commit v3 on v2

--- a/solution.py
+++ b/solution.py
@@ -173,8 +173,10 @@
 PART = 8
 HEAD_HALF = 4
 CHUNKS = (2, 2)
-DIRECT = (True, True)
 VMEM_MIB = 48
+PIN2 = PIN3 = lambda x: x
+OUT = lambda x: x
+PIN = partial(pltpu.with_memory_space_constraint, memory_space=pltpu.HBM)
 HALF_Q = HEAD_HALF * GROUP * HEAD_DIM
 HALF_KV = HEAD_HALF * HEAD_DIM
 PAIR = 2 * BLOCK
@@ -197,34 +199,48 @@
     return lax.ppermute(array, AXES, perm)
 
 
-def pack_kernel(where_ref, k_ref, v_ref, ko_ref, vo_ref, *outs):
+def move_all(copies):
+    for copy in copies:
+        copy.start()
+    for copy in copies:
+        copy.wait()
+
+
+def lanes(start, width):
+    return pl.ds(pl.multiple_of(start, HEAD_DIM), width)
+
+
+def pack_kernel(where_ref, k_ref, v_ref, ko_ref, vo_ref, *refs):
+    outs, sems = refs[:-1], refs[-1]
+    copies = []
     for chunk, heads in enumerate(CHUNKS):
         for head in range(heads):
-            at = sum(CHUNKS[:chunk]) + head
-            src = slice(at * HEAD_DIM, (at + 1) * HEAD_DIM)
-            for side, ref in enumerate((k_ref, v_ref)):
-                cols = slice((2 * head + side) * HEAD_DIM, (2 * head + side + 1) * HEAD_DIM)
-                outs[chunk][0:BLOCK, cols] = ref[:, src]
-            for side, ref in enumerate((ko_ref, vo_ref)):
-                cols = slice((2 * head + side) * HEAD_DIM, (2 * head + side + 1) * HEAD_DIM)
-                outs[chunk][BLOCK:PAIR, cols] = ref[:, src]
+            at = where_ref[0] * HALF_KV + (sum(CHUNKS[:chunk]) + head) * HEAD_DIM
+            for row, pieces in enumerate(((k_ref, v_ref), (ko_ref, vo_ref))):
+                for side, ref in enumerate(pieces):
+                    to = outs[chunk].at[
+                        row * BLOCK : (row + 1) * BLOCK,
+                        (2 * head + side) * HEAD_DIM : (2 * head + side + 1) * HEAD_DIM,
+                    ]
+                    sem = sems.at[len(copies)]
+                    source = ref.at[:, lanes(at, HEAD_DIM)]
+                    copies.append(pltpu.make_async_copy(source, to, sem))
+    move_all(copies)
 
 
 def pack_pairs(where, keys, values, keys_other, values_other):
-    shapes = [(PAIR, 2 * HEAD_DIM * heads) for heads in CHUNKS]
-    spec = pl.BlockSpec((BLOCK, HALF_KV), lambda g, w: (0, w[0]))
     return pl.pallas_call(
         pack_kernel,
-        out_shape=[jax.ShapeDtypeStruct(shape, jnp.bfloat16) for shape in shapes],
-        grid_spec=pltpu.PrefetchScalarGridSpec(
-            num_scalar_prefetch=1,
-            grid=(1,),
-            in_specs=[spec] * 4,
-            out_specs=[pl.BlockSpec(shape, lambda g, w: (0, 0)) for shape in shapes],
-        ),
+        out_shape=[
+            jax.ShapeDtypeStruct((PAIR, 2 * HEAD_DIM * heads), jnp.bfloat16) for heads in CHUNKS
+        ],
+        in_specs=[pl.BlockSpec(memory_space=pltpu.SMEM)] + [pl.BlockSpec(memory_space=pl.ANY)] * 4,
+        out_specs=[pl.BlockSpec(memory_space=pltpu.VMEM)] * len(CHUNKS),
+        scratch_shapes=[pltpu.SemaphoreType.DMA((4 * HEAD_HALF,))],
         name="pack_pairs",
+        compiler_params=pltpu.CompilerParams(vmem_limit_bytes=VMEM_MIB * 2**20),
         cost_estimate=pl.CostEstimate(flops=0, bytes_accessed=2**20, transcendentals=0),
-    )(where, keys, values, keys_other, values_other)
+    )(where, PIN(keys), PIN(values), keys_other, values_other)
 
 
 def attend_kernel(
@@ -386,10 +402,9 @@
     dq_shape = jax.ShapeDtypeStruct((BLOCK, heads * qw), jnp.bfloat16)
     wide = jax.ShapeDtypeStruct((PAIR, heads * kw), jnp.float32)
     narrow = jax.ShapeDtypeStruct((PAIR, heads * kw), jnp.bfloat16)
-    near_shape = narrow if DIRECT[chunk] else wide
     return pl.pallas_call(
         attend_kernel,
-        out_shape=[dq_shape, dq_shape, wide, near_shape, narrow, narrow],
+        out_shape=[OUT(dq_shape), OUT(dq_shape), wide, narrow, narrow, narrow],
         grid_spec=pltpu.PrefetchScalarGridSpec(
             num_scalar_prefetch=2,
             grid=(heads,),
@@ -411,50 +426,58 @@
         cost_estimate=pl.CostEstimate(
             flops=10 * pairs * HEAD_DIM * 2, bytes_accessed=4 * 2**20, transcendentals=pairs
         ),
-    )(where, rand, queries, d_out, queries_other, dout_other, *sources)
-
-
-def finish_kernel(where_ref, *refs):
-    chunks = len(CHUNKS)
-    own, other, dq_own, dq_got = (refs[i * chunks : (i + 1) * chunks] for i in range(4))
-    dq_ref, dk_ref, dv_ref = refs[4 * chunks :]
-    half = where_ref[0]
-    for value in range(2):
-
-        @pl.when(half == value)
-        def _():
-            for piece, place in ((own, value), (other, 1 - value)):
-                for chunk, heads in enumerate(CHUNKS):
-                    for head in range(heads):
-                        at = place * HALF_KV + (sum(CHUNKS[:chunk]) + head) * HEAD_DIM
-                        from_col = 2 * head * HEAD_DIM
-                        dk_ref[:, at : at + HEAD_DIM] = piece[chunk][
-                            0:BLOCK, from_col : from_col + HEAD_DIM
-                        ]
-                        dv_ref[:, at : at + HEAD_DIM] = piece[chunk][
-                            0:BLOCK, from_col + HEAD_DIM : from_col + 2 * HEAD_DIM
-                        ]
-            for piece, place in ((dq_own, value), (dq_got, 1 - value)):
-                for chunk, heads in enumerate(CHUNKS):
-                    at = place * HALF_Q + sum(CHUNKS[:chunk]) * GROUP * HEAD_DIM
-                    width = heads * GROUP * HEAD_DIM
-                    dq_ref[:, at : at + width] = piece[chunk][...]
-
-
-def finish(where, own, other, dq_own, dq_got):
+    )(where, rand, *map(PIN, (queries, d_out, queries_other, dout_other)), *map(PIN2, sources))
+
+
+def place_kernel(columns, where_ref, *refs):
+    inputs = refs[: len(columns) * 2]
+    outs, sems = refs[len(columns) * 2 : -1], refs[-1]
+    copies = []
+    for i, pieces in enumerate(columns):
+        for half in range(2):
+            place = where_ref[0] ^ half
+            for out, at, start, width in pieces:
+                at = at + place * (outs[out].shape[1] // 2)
+                source = inputs[2 * i + half].at[:, start : start + width]
+                to = outs[out].at[:, lanes(at, width)]
+                copies.append(pltpu.make_async_copy(source, to, sems.at[len(copies)]))
+    move_all(copies)
+
+
+def place(columns, where, inputs, widths, name):
+    count = 2 * sum(len(pieces) for pieces in columns)
     return pl.pallas_call(
-        finish_kernel,
-        out_shape=[
-            jax.ShapeDtypeStruct((BLOCK, 2 * HALF_Q), jnp.bfloat16),
-            jax.ShapeDtypeStruct((BLOCK, 2 * HALF_KV), jnp.bfloat16),
-            jax.ShapeDtypeStruct((BLOCK, 2 * HALF_KV), jnp.bfloat16),
-        ],
+        partial(place_kernel, columns),
+        out_shape=[jax.ShapeDtypeStruct((BLOCK, width), jnp.bfloat16) for width in widths],
         in_specs=[pl.BlockSpec(memory_space=pltpu.SMEM)]
-        + [pl.BlockSpec(memory_space=pltpu.VMEM)] * (4 * len(CHUNKS)),
-        out_specs=[pl.BlockSpec(memory_space=pltpu.VMEM)] * 3,
-        name="finish",
-        cost_estimate=pl.CostEstimate(flops=0, bytes_accessed=3 * 2**20, transcendentals=0),
-    )(where, *own, *other, *dq_own, *dq_got)
+        + [pl.BlockSpec(memory_space=pl.ANY)] * len(inputs),
+        out_specs=[pl.BlockSpec(memory_space=pltpu.VMEM)] * len(widths),
+        scratch_shapes=[pltpu.SemaphoreType.DMA((count,))],
+        name=name,
+        cost_estimate=pl.CostEstimate(flops=0, bytes_accessed=2**20, transcendentals=0),
+    )(where, *inputs)
+
+
+def place_queries(where, own, got):
+    columns, inputs = [], []
+    for chunk, heads in enumerate(CHUNKS):
+        width = heads * GROUP * HEAD_DIM
+        columns.append([(0, sum(CHUNKS[:chunk]) * GROUP * HEAD_DIM, 0, width)])
+        inputs += [own[chunk], got[chunk]]
+    return place(columns, where, inputs, [2 * HALF_Q], "place_queries")[0]
+
+
+def place_pairs(where, own, got):
+    columns, inputs = [], []
+    for chunk, heads in enumerate(CHUNKS):
+        pieces = []
+        for head in range(heads):
+            at = (sum(CHUNKS[:chunk]) + head) * HEAD_DIM
+            for side in range(2):
+                pieces.append((side, at, (2 * head + side) * HEAD_DIM, HEAD_DIM))
+        columns.append(pieces)
+        inputs += [own[chunk], got[chunk]]
+    return place(columns, where, inputs, [2 * HALF_KV] * 2, "place_pairs")
 
 
 def per_device_dense(queries, keys, values, d_out, rand_blocks):
@@ -471,7 +494,7 @@
     nears = [send(pair, NEAR_PERM) for pair in pairs]
     fars = [send(pair, FAR_PERM) for pair in pairs]
     corners = [send(near, FAR_PERM) for near in nears]
-    own, other, dq_own, dq_got = [], [], [], []
+    terms, dq_own, dq_got = [], [], []
     for chunk in range(len(CHUNKS)):
         dq_mine, dq_other, own_grads, near_grads, far_grads, corner_grads = attend(
             chunk,
@@ -483,20 +506,26 @@
             dout_other,
             (pairs[chunk], nears[chunk], fars[chunk], corners[chunk]),
         )
-        if DIRECT[chunk]:
-            arrived = [send(corner_grads, CORNER_PERM), send(near_grads, NEAR_PERM)]
-        else:
-            from_corner = send(corner_grads, FAR_PERM)
-            relayed = (near_grads + from_corner.astype(jnp.float32)).astype(jnp.bfloat16)
-            arrived = [send(relayed, NEAR_PERM)]
-        arrived.append(send(far_grads, FAR_PERM))
-        total = own_grads + sum(x.astype(jnp.float32) for x in arrived)
-        total = total.astype(jnp.bfloat16)
-        own.append(total[:BLOCK])
-        other.append(send(total[BLOCK:], SWAP_PERM))
+        arrived = [
+            send(corner_grads, CORNER_PERM),
+            send(near_grads, NEAR_PERM),
+            send(far_grads, FAR_PERM),
+        ]
+        terms.append((own_grads, arrived))
         dq_own.append(dq_mine)
         dq_got.append(send(dq_other, SWAP_PERM))
-    return tuple(finish(where, own, other, dq_own, dq_got))
+    d_queries = place_queries(where, dq_own, dq_got)
+    terms[-1], d_queries = lax.optimization_barrier((terms[-1], d_queries))
+    own, other = [], []
+    for own_grads, arrived in terms:
+        mine, theirs = (
+            sum((x[at].astype(jnp.float32) for x in arrived), own_grads[at]).astype(jnp.bfloat16)
+            for at in (slice(0, BLOCK), slice(BLOCK, PAIR))
+        )
+        own.append(mine)
+        other.append(send(theirs, SWAP_PERM))
+    d_keys, d_values = place_pairs(where, own, other)
+    return (d_queries, d_keys, d_values)
 
 
 def per_device(queries, keys, values, d_out, rand_blocks):

time: 68.5 us -> 65.1 us (0.950)
  local copies, waits for them, and re-layouts: 6.08 us -> 2.22 us
  waiting for transfers between devices: 19.3 us -> 15.7 us
  Pallas kernels: 22.8 us -> 24.8 us
  starting transfers between devices: 18.4 us -> 19.5 us
    ppermute x20, waiting for transfers between devices: 19.3 us -> 15.7 us  [send(): return lax.ppermute(array, AXES, perm)]
    unnamed x29 -> x19, local copies, waits for them, and re-layouts: 4.65 us -> 2.14 us
    pallas_call x4 -> x5, Pallas kernels: 22.8 us -> 24.8 us  [the longest x2 17.8 us: attend(): pl.pallas_call(attend_kernel, out_shape=[OUT(dq_shape), OUT(dq_shape), wi...]
    slice x2 -> x0, local copies, waits for them, and re-layouts: 1.35 us -> none  [per_device_dense(): other.append(send(total[BLOCK:], SWAP_PERM))]
    convert_element_type x2, other arithmetic: 0.32 us -> 1.57 us  [per_device_dense(): sum((x[at].astype(jnp.float32) for x in arrived), own_grads[at])]
    ppermute x20, starting transfers between devices: 18.4 us -> 19.5 us  [send(): return lax.ppermute(array, AXES, perm)]
  transfers between devices with their start and end apart: 20 -> 20, of which waited for: 8 -> 8; matrix products, arithmetic and copies ran while one was open for 4% -> 3% of each run, Pallas kernels for 25% -> 32%
where the time goes in v3:
time: 65.1 us; the launch traced here: 64.7 us
  Pallas kernels  24.8 us (38%)
  starting transfers between devices  19.5 us (30%)
  waiting for transfers between devices  15.7 us (24%)
  local copies, waits for them, and re-layouts  2.22 us (3%)
  other arithmetic  1.64 us (3%)
  between operations  0.76 us (1%)
    ppermute x20, starting transfers between devices, send(): return lax.ppermute(array, AXES, perm)  19.5 us
    pallas_call x2, Pallas kernels, attend(): pl.pallas_call(attend_kernel, out_shape=[OUT(dq_shape), OUT(dq_shape), wi...  17.8 us
    ppermute x20, waiting for transfers between devices, send(): return lax.ppermute(array, AXES, perm)  15.7 us
    pallas_call x2, Pallas kernels, place(): pl.pallas_call(partial(place_kernel, columns), out_shape=[jax.ShapeDtypeS...  5.46 us
    unnamed x19, local copies, waits for them, and re-layouts  2.14 us
    pallas_call x1, Pallas kernels, pack_pairs(): pl.pallas_call(pack_kernel, out_shape=[jax.ShapeDtypeStruct((PAIR, 2 * HE...  1.58 us
    convert_element_type x2, other arithmetic, per_device_dense(): sum((x[at].astype(jnp.float32) for x in arrived), own_grads[at])  1.57 us
  transfers between devices with their start and end apart: 20, of which 8 were waited for; matrix products, arithmetic and copies ran while one was open for 3% of the time, Pallas kernels for 32%

profile of v3, /device:TPU:0, one launch (start us, length us, event | category | flops | bytes accessed | tf_op | source)
XLA Modules:
  0.0 64.7 jit_solution(16558794269156002375)
XLA Ops:
  0.6 0.0 copy-start.8
  0.6 0.5 collective-permute-start
  1.2 0.1 collective-permute-start.1
  1.2 0.1 pad_add_fusion.where_ref
  1.3 1.2 %collective-permute-done.ko_ref = bf16[128,1024]{1,0:T(8,128)(2,1)S(1)} collective-permute-done((bf16[128,1024]{1,0:T(8,128)(2,1)}, bf16[128,1024]{1,0:T(8,128)(2,1)S(1)}, u32[]{:S(2)}, u32[]{:S(2)}) %collective-permute-start) | collective-permute-done | bytes 262176 | tf_op jit(solution)/shard_map/ppermute | solution.py:199
  2.5 0.4 collective-permute-done.1.vo_ref
  2.9 1.6 %pack_pairs.1 = (bf16[256,512]{1,0:T(8,128)(2,1)S(1)}, bf16[256,512]{1,0:T(8,128)(2,1)S(1)}) custom-call(s32[2]{0:T(128)S(1)} %pad_add_fusion.where_ref, bf16[128,1024]{1,0:T(8,128)(2,1)} %k_ref.1, bf16[128,1024]{1,0:T(8,128)(2,1)} %v_ref.1, bf16[128,1024]{1,0:T(8,128)(2,1)S(1)} %collective-permute-done.ko_ref, ...), custom_call_target="tpu_custom_call" | custom-call | bytes 1048576 | tf_op jit(solution)/shard_map/pack_pairs/pallas_call | solution.py:232
  4.5 0.0 copy-start.7
  4.5 0.4 collective-permute-start.2
  5.0 0.1 collective-permute-start.3
  5.1 2.9 %collective-permute-start.10 = (bf16[256,512]{1,0:T(8,128)(2,1)S(1)}, bf16[256,512]{1,0:T(8,128)(2,1)S(1)}, u32[]{:S(2)}, u32[]{:S(2)}) collective-permute-start(bf16[256,512]{1,0:T(8,128)(2,1)S(1)} %get-tuple-element.37.pair_ref), channel_id=1, source_target_pairs={{0,4},{1,5},{2,3},{3,2},{4,0},{5,1},{6,7},{7,6},{8,12},{9,13},{10,... | collective-permute-start | bytes 786440 | tf_op jit(solution)/shard_map/ppermute | solution.py:199
  8.0 0.0 collective-permute-start.4
  8.0 2.0 %collective-permute-start.11 = (bf16[256,512]{1,0:T(8,128)(2,1)S(1)}, bf16[256,512]{1,0:T(8,128)(2,1)S(1)}, u32[]{:S(2)}, u32[]{:S(2)}) collective-permute-start(bf16[256,512]{1,0:T(8,128)(2,1)S(1)} %get-tuple-element.37.pair_ref), channel_id=1, source_target_pairs={{0,1},{1,0},{2,6},{3,7},{4,5},{5,4},{6,2},{7,3},{8,9},{9,8},{10,14... | collective-permute-start | bytes 786440 | tf_op jit(solution)/shard_map/ppermute | solution.py:199
  10.0 4.1 %collective-permute-done.10.near_ref = bf16[256,512]{1,0:T(8,128)(2,1)S(1)} collective-permute-done((bf16[256,512]{1,0:T(8,128)(2,1)S(1)}, bf16[256,512]{1,0:T(8,128)(2,1)S(1)}, u32[]{:S(2)}, u32[]{:S(2)}) %collective-permute-start.10) | collective-permute-done | bytes 262176 | tf_op jit(solution)/shard_map/ppermute | solution.py:199
  14.1 2.4 %collective-permute-start.12 = (bf16[256,512]{1,0:T(8,128)(2,1)S(1)}, bf16[256,512]{1,0:T(8,128)(2,1)S(1)}, u32[]{:S(2)}, u32[]{:S(2)}) collective-permute-start(bf16[256,512]{1,0:T(8,128)(2,1)S(1)} %collective-permute-done.10.near_ref), channel_id=1, source_target_pairs={{0,1},{1,0},{2,6},{3,7},{4,5},{5,4},{6,2},{7,3},{8,9},{9,8},{10,14... | collective-permute-start | bytes 786440 | tf_op jit(solution)/shard_map/ppermute | solution.py:199
  16.6 0.1 copy.9
  16.7 0.1 reshape.9.rand_ref
  16.8 3.0 %collective-permute-done.4.near_ref = bf16[256,512]{1,0:T(8,128)(2,1)S(1)} collective-permute-done((bf16[256,512]{1,0:T(8,128)(2,1)S(1)}, bf16[256,512]{1,0:T(8,128)(2,1)S(1)}, u32[]{:S(2)}, u32[]{:S(2)}) %collective-permute-start.4) | collective-permute-done | bytes 262176 | tf_op jit(solution)/shard_map/ppermute | solution.py:199
  19.8 2.4 %collective-permute-start.5 = (bf16[256,512]{1,0:T(8,128)(2,1)S(1)}, bf16[256,512]{1,0:T(8,128)(2,1)S(1)}, u32[]{:S(2)}, u32[]{:S(2)}) collective-permute-start(bf16[256,512]{1,0:T(8,128)(2,1)S(1)} %get-tuple-element.32.pair_ref), channel_id=1, source_target_pairs={{0,1},{1,0},{2,6},{3,7},{4,5},{5,4},{6,2},{7,3},{8,9},{9,8},{10,14... | collective-permute-start | bytes 786440 | tf_op jit(solution)/shard_map/ppermute | solution.py:199
  22.2 0.0 collective-permute-start.6
  22.2 0.0 collective-permute-done.12.corner_ref
  22.2 0.0 collective-permute-done.2.qo_ref
  22.2 8.9 %attend.3 = (bf16[128,1024]{1,0:T(8,128)(2,1)S(1)}, bf16[128,1024]{1,0:T(8,128)(2,1)S(1)}, f32[256,512]{1,0:T(8,128)S(1)}, bf16[256,512]{1,0:T(8,128)(2,1)S(1)},...) custom-call(s32[2]{0:T(128)S(1)} %pad_add_fusion.where_ref, s32[24]{0:T(128)S(1)} %reshape.9.rand_ref, ...), custom_call_target="tpu_custom_call" | custom-call | flops 5368709120 | bytes 4194304 | tf_op jit(solution)/shard_map/attend/pallas_call | solution.py:405
  31.2 0.0 copy-start
  31.2 0.7 %copy-done = bf16[128,1024]{1,0:T(8,128)(2,1)} copy-done((bf16[128,1024]{1,0:T(8,128)(2,1)}, bf16[128,1024]{1,0:T(8,128)(2,1)S(1)}, u32[]{:S(2)}) %copy-start) | copy-done | bytes 262168
  31.9 2.9 %collective-permute-start.15 = (bf16[256,512]{1,0:T(8,128)(2,1)S(1)}, bf16[256,512]{1,0:T(8,128)(2,1)S(1)}, u32[]{:S(2)}, u32[]{:S(2)}) collective-permute-start(bf16[256,512]{1,0:T(8,128)(2,1)S(1)} %get-tuple-element.44), channel_id=1, source_target_pairs={{0,5},{1,4},{2,7},{3,6},{4,1},{5,0},{6,3},{7,2},{8,13},{9,12},{10,... | collective-permute-start | bytes 786440 | tf_op jit(solution)/shard_map/ppermute | solution.py:199
  34.8 0.5 collective-permute-start.16
  35.3 0.0 collective-permute-start.17
  35.4 8.9 %attend.2 = (bf16[128,1024]{1,0:T(8,128)(2,1)S(1)}, bf16[128,1024]{1,0:T(8,128)(2,1)S(1)}, f32[256,512]{1,0:T(8,128)S(1)}, bf16[256,512]{1,0:T(8,128)(2,1)S(1)},...) custom-call(s32[2]{0:T(128)S(1)} %pad_add_fusion.where_ref, s32[24]{0:T(128)S(1)} %reshape.9.rand_ref, ...), custom_call_target="tpu_custom_call" | custom-call | flops 5368709120 | bytes 4194304 | tf_op jit(solution)/shard_map/attend/pallas_call | solution.py:405
  44.3 3.0 %collective-permute-start.7 = (bf16[256,512]{1,0:T(8,128)(2,1)S(1)}, bf16[256,512]{1,0:T(8,128)(2,1)S(1)}, u32[]{:S(2)}, u32[]{:S(2)}) collective-permute-start(bf16[256,512]{1,0:T(8,128)(2,1)S(1)} %get-tuple-element.34), channel_id=1, source_target_pairs={{0,5},{1,4},{2,7},{3,6},{4,1},{5,0},{6,3},{7,2},{8,13},{9,12},{10,... | collective-permute-start | bytes 786440 | tf_op jit(solution)/shard_map/ppermute | solution.py:199
  47.3 0.0 collective-permute-start.14
  47.3 0.4 collective-permute-done.16
  47.7 1.5 %collective-permute-start.8 = (bf16[256,512]{1,0:T(8,128)(2,1)S(1)}, bf16[256,512]{1,0:T(8,128)(2,1)S(1)}, u32[]{:S(2)}, u32[]{:S(2)}) collective-permute-start(bf16[256,512]{1,0:T(8,128)(2,1)S(1)} %get-tuple-element.35), channel_id=1, source_target_pairs={{0,4},{1,5},{2,3},{3,2},{4,0},{5,1},{6,7},{7,6},{8,12},{9,13},{10,... | collective-permute-start | bytes 786440 | tf_op jit(solution)/shard_map/ppermute | solution.py:199
  49.2 0.0 collective-permute-done.17
  49.2 0.5 collective-permute-start.9
  49.7 0.8 %add_convert_fusion.2 = (bf16[128,512]{1,0:T(8,128)(2,1)S(1)}, bf16[128,512]{1,0:T(8,128)(2,1)}) fusion(f32[256,512]{1,0:T(8,128)S(1)} %get-tuple-element.43, bf16[256,512]{1,0:T(8,128)(2,1)S(1)} %collective-permute-done.17, bf16[256,512]{1,0:T(8,128)(2,1)S(1)} %collective-permute-done.16, bf16[256,512]{1,0:T(8,128)(2,1)S(1)} %collective-permute-done.15), kind=kLoop, calls=%fused_computation.2 | loop fusion | flops 917504 | bytes 1572864 | tf_op jit(solution)/shard_map/convert_element_type | solution.py:522
  50.5 0.0 collective-permute-done.13.refs_1_
  50.5 0.1 collective-permute-start.18
  50.5 0.0 collective-permute-done.14.refs_3_
  50.6 0.6 copy-done.3
  51.2 0.1 copy-done.4
  51.3 2.9 %place_queries.1 = bf16[128,4096]{1,0:T(8,128)(2,1)} custom-call(s32[2]{0:T(128)} %copy-done.2, bf16[128,1024]{1,0:T(8,128)(2,1)} %copy-done, bf16[128,1024]{1,0:T(8,128)(2,1)} %copy-done.3, bf16[128,1024]{1,0:T(8,128)(2,1)} %copy-done.1, bf16[128,1024]{1,0:T(8,128)(2,1)} %copy-done.4), custom_call_target="tpu_custom_call" | custom-call | bytes 1048576 | tf_op jit(solution)/shard_map/place_queries/pallas_call | solution.py:449
  54.1 0.3 collective-permute-done.7
  54.5 4.8 %collective-permute-done.8 = bf16[256,512]{1,0:T(8,128)(2,1)S(1)} collective-permute-done((bf16[256,512]{1,0:T(8,128)(2,1)S(1)}, bf16[256,512]{1,0:T(8,128)(2,1)S(1)}, u32[]{:S(2)}, u32[]{:S(2)}) %collective-permute-start.8) | collective-permute-done | bytes 262176 | tf_op jit(solution)/shard_map/ppermute | solution.py:199
  59.3 0.8 %add_convert_fusion = (bf16[128,512]{1,0:T(8,128)(2,1)S(1)}, bf16[128,512]{1,0:T(8,128)(2,1)}) fusion(f32[256,512]{1,0:T(8,128)S(1)} %get-tuple-element.47, bf16[256,512]{1,0:T(8,128)(2,1)S(1)} %collective-permute-done.9, bf16[256,512]{1,0:T(8,128)(2,1)S(1)} %collective-permute-done.8, bf16[256,512]{1,0:T(8,128)(2,1)S(1)} %collective-permute-done.7), kind=kLoop, calls=%fused_computation | loop fusion | flops 917504 | bytes 1572864 | tf_op jit(solution)/shard_map/convert_element_type | solution.py:522
  60.1 1.3 %collective-permute-done.19.refs_3_ = bf16[128,512]{1,0:T(8,128)(2,1)S(1)} collective-permute-done((bf16[128,512]{1,0:T(8,128)(2,1)S(1)}, bf16[128,512]{1,0:T(8,128)(2,1)S(1)}, u32[]{:S(2)}, u32[]{:S(2)}) %collective-permute-start.19) | collective-permute-done | bytes 131104 | tf_op jit(solution)/shard_map/ppermute | solution.py:199
  61.4 0.6 copy-done.6
  62.1 2.6 %place_pairs.1 = (bf16[128,1024]{1,0:T(8,128)(2,1)}, bf16[128,1024]{1,0:T(8,128)(2,1)}) custom-call(s32[2]{0:T(128)} %copy-done.2, bf16[128,512]{1,0:T(8,128)(2,1)} %get-tuple-element.56.refs_0_, bf16[128,512]{1,0:T(8,128)(2,1)} %copy-done.5, bf16[128,512]{1,0:T(8,128)(2,1)} %get-tuple-element.54.refs_2_, bf16[128,512]{1,0:T(8,128)(2,1)} %copy-done.6), custom_call_target="tpu_custom_call" | custom-call | bytes 1048576 | tf_op jit(solution)/shard_map/place_pairs/pallas_call | solution.py:449
  (20 shorter events, 0.0 us)
Async XLA Ops:
  0.6 3.9 %copy-start.8 = (bf16[128,4096]{1,0:T(8,128)(2,1)S(1)}, bf16[128,4096]{1,0:T(8,128)(2,1)}, u32[]{:S(2)}) copy-start(bf16[128,4096]{1,0:T(8,128)(2,1)} %q_ref.1) | copy-start | bytes 3145732
  0.6 1.9 %collective-permute-start = (bf16[128,1024]{1,0:T(8,128)(2,1)}, bf16[128,1024]{1,0:T(8,128)(2,1)S(1)}, u32[]{:S(2)}, u32[]{:S(2)}) collective-permute-start(bf16[128,1024]{1,0:T(8,128)(2,1)} %k_ref.1), channel_id=1, source_target_pairs={{0,2},{1,3},{2,0},{3,1},{4,6},{5,7},{6,4},{7,5},{8,10},{9,11},{10,... | collective-permute-start | bytes 786440 | tf_op jit(solution)/shard_map/ppermute | solution.py:199
  1.2 1.7 %collective-permute-start.1 = (bf16[128,1024]{1,0:T(8,128)(2,1)}, bf16[128,1024]{1,0:T(8,128)(2,1)S(1)}, u32[]{:S(2)}, u32[]{:S(2)}) collective-permute-start(bf16[128,1024]{1,0:T(8,128)(2,1)} %v_ref.1), channel_id=1, source_target_pairs={{0,2},{1,3},{2,0},{3,1},{4,6},{5,7},{6,4},{7,5},{8,10},{9,11},{10,... | collective-permute-start | bytes 786440 | tf_op jit(solution)/shard_map/ppermute | solution.py:199
  1.3 34.0 %copy-start.2 = (s32[2]{0:T(128)}, s32[2]{0:T(128)S(1)}, u32[]{:S(2)}) copy-start(s32[2]{0:T(128)S(1)} %pad_add_fusion.where_ref) | copy-start | bytes 28
  4.5 12.1 %copy-start.7 = (s32[8,3]{0,1:T(4,128)S(1)}, s32[8,3]{0,1:T(4,128)}, u32[]{:S(2)}) copy-start(s32[8,3]{0,1:T(4,128)} %param.9) | copy-start | bytes 292
  4.5 17.7 %collective-permute-start.2 = (bf16[128,4096]{1,0:T(8,128)(2,1)S(1)}, bf16[128,4096]{1,0:T(8,128)(2,1)}, u32[]{:S(2)}, u32[]{:S(2)}) collective-permute-start(bf16[128,4096]{1,0:T(8,128)(2,1)S(1)} %copy-done.8), channel_id=1, source_target_pairs={{0,2},{1,3},{2,0},{3,1},{4,6},{5,7},{6,4},{7,5},{8,10},{9,11},{10,... | collective-permute-start | bytes 3145736 | tf_op jit(solution)/shard_map/ppermute | solution.py:199
  5.0 17.3 %collective-permute-start.3 = (bf16[128,4096]{1,0:T(8,128)(2,1)}, bf16[128,4096]{1,0:T(8,128)(2,1)}, u32[]{:S(2)}, u32[]{:S(2)}) collective-permute-start(bf16[128,4096]{1,0:T(8,128)(2,1)} %do_ref.1), channel_id=1, source_target_pairs={{0,2},{1,3},{2,0},{3,1},{4,6},{5,7},{6,4},{7,5},{8,10},{9,11},{10,... | collective-permute-start | bytes 3145736 | tf_op jit(solution)/shard_map/ppermute | solution.py:199
  5.1 9.1 %collective-permute-start.10 = (bf16[256,512]{1,0:T(8,128)(2,1)S(1)}, bf16[256,512]{1,0:T(8,128)(2,1)S(1)}, u32[]{:S(2)}, u32[]{:S(2)}) collective-permute-start(bf16[256,512]{1,0:T(8,128)(2,1)S(1)} %get-tuple-element.37.pair_ref), channel_id=1, source_target_pairs={{0,4},{1,5},{2,3},{3,2},{4,0},{5,1},{6,7},{7,6},{8,12},{9,13},{10,... | collective-permute-start | bytes 786440 | tf_op jit(solution)/shard_map/ppermute | solution.py:199
  8.0 11.8 %collective-permute-start.4 = (bf16[256,512]{1,0:T(8,128)(2,1)S(1)}, bf16[256,512]{1,0:T(8,128)(2,1)S(1)}, u32[]{:S(2)}, u32[]{:S(2)}) collective-permute-start(bf16[256,512]{1,0:T(8,128)(2,1)S(1)} %get-tuple-element.32.pair_ref), channel_id=1, source_target_pairs={{0,4},{1,5},{2,3},{3,2},{4,0},{5,1},{6,7},{7,6},{8,12},{9,13},{10,... | collective-permute-start | bytes 786440 | tf_op jit(solution)/shard_map/ppermute | solution.py:199
  8.0 14.2 %collective-permute-start.11 = (bf16[256,512]{1,0:T(8,128)(2,1)S(1)}, bf16[256,512]{1,0:T(8,128)(2,1)S(1)}, u32[]{:S(2)}, u32[]{:S(2)}) collective-permute-start(bf16[256,512]{1,0:T(8,128)(2,1)S(1)} %get-tuple-element.37.pair_ref), channel_id=1, source_target_pairs={{0,1},{1,0},{2,6},{3,7},{4,5},{5,4},{6,2},{7,3},{8,9},{9,8},{10,14... | collective-permute-start | bytes 786440 | tf_op jit(solution)/shard_map/ppermute | solution.py:199
  14.1 8.1 %collective-permute-start.12 = (bf16[256,512]{1,0:T(8,128)(2,1)S(1)}, bf16[256,512]{1,0:T(8,128)(2,1)S(1)}, u32[]{:S(2)}, u32[]{:S(2)}) collective-permute-start(bf16[256,512]{1,0:T(8,128)(2,1)S(1)} %collective-permute-done.10.near_ref), channel_id=1, source_target_pairs={{0,1},{1,0},{2,6},{3,7},{4,5},{5,4},{6,2},{7,3},{8,9},{9,8},{10,14... | collective-permute-start | bytes 786440 | tf_op jit(solution)/shard_map/ppermute | solution.py:199
  19.8 15.6 %collective-permute-start.5 = (bf16[256,512]{1,0:T(8,128)(2,1)S(1)}, bf16[256,512]{1,0:T(8,128)(2,1)S(1)}, u32[]{:S(2)}, u32[]{:S(2)}) collective-permute-start(bf16[256,512]{1,0:T(8,128)(2,1)S(1)} %get-tuple-element.32.pair_ref), channel_id=1, source_target_pairs={{0,1},{1,0},{2,6},{3,7},{4,5},{5,4},{6,2},{7,3},{8,9},{9,8},{10,14... | collective-permute-start | bytes 786440 | tf_op jit(solution)/shard_map/ppermute | solution.py:199
  22.2 13.2 %collective-permute-start.6 = (bf16[256,512]{1,0:T(8,128)(2,1)S(1)}, bf16[256,512]{1,0:T(8,128)(2,1)S(1)}, u32[]{:S(2)}, u32[]{:S(2)}) collective-permute-start(bf16[256,512]{1,0:T(8,128)(2,1)S(1)} %collective-permute-done.4.near_ref), channel_id=1, source_target_pairs={{0,1},{1,0},{2,6},{3,7},{4,5},{5,4},{6,2},{7,3},{8,9},{9,8},{10,14... | collective-permute-start | bytes 786440 | tf_op jit(solution)/shard_map/ppermute | solution.py:199
  31.2 0.7 %copy-start = (bf16[128,1024]{1,0:T(8,128)(2,1)}, bf16[128,1024]{1,0:T(8,128)(2,1)S(1)}, u32[]{:S(2)}) copy-start(bf16[128,1024]{1,0:T(8,128)(2,1)S(1)} %get-tuple-element.38.refs_0_) | copy-start | bytes 786436
  31.9 18.6 %collective-permute-start.13 = (bf16[128,1024]{1,0:T(8,128)(2,1)S(1)}, bf16[128,1024]{1,0:T(8,128)(2,1)S(1)}, u32[]{:S(2)}, u32[]{:S(2)}) collective-permute-start(bf16[128,1024]{1,0:T(8,128)(2,1)S(1)} %get-tuple-element.39), channel_id=1, source_target_pairs={{0,2},{1,3},{2,0},{3,1},{4,6},{5,7},{6,4},{7,5},{8,10},{9,11},{10,... | collective-permute-start | bytes 786440 | tf_op jit(solution)/shard_map/ppermute | solution.py:199
  31.9 15.4 %collective-permute-start.15 = (bf16[256,512]{1,0:T(8,128)(2,1)S(1)}, bf16[256,512]{1,0:T(8,128)(2,1)S(1)}, u32[]{:S(2)}, u32[]{:S(2)}) collective-permute-start(bf16[256,512]{1,0:T(8,128)(2,1)S(1)} %get-tuple-element.44), channel_id=1, source_target_pairs={{0,5},{1,4},{2,7},{3,6},{4,1},{5,0},{6,3},{7,2},{8,13},{9,12},{10,... | collective-permute-start | bytes 786440 | tf_op jit(solution)/shard_map/ppermute | solution.py:199
  34.8 12.9 %collective-permute-start.16 = (bf16[256,512]{1,0:T(8,128)(2,1)S(1)}, bf16[256,512]{1,0:T(8,128)(2,1)S(1)}, u32[]{:S(2)}, u32[]{:S(2)}) collective-permute-start(bf16[256,512]{1,0:T(8,128)(2,1)S(1)} %get-tuple-element.45), channel_id=1, source_target_pairs={{0,4},{1,5},{2,3},{3,2},{4,0},{5,1},{6,7},{7,6},{8,12},{9,13},{10,... | collective-permute-start | bytes 786440 | tf_op jit(solution)/shard_map/ppermute | solution.py:199
  35.3 13.9 %collective-permute-start.17 = (bf16[256,512]{1,0:T(8,128)(2,1)S(1)}, bf16[256,512]{1,0:T(8,128)(2,1)S(1)}, u32[]{:S(2)}, u32[]{:S(2)}) collective-permute-start(bf16[256,512]{1,0:T(8,128)(2,1)S(1)} %get-tuple-element.46), channel_id=1, source_target_pairs={{0,1},{1,0},{2,6},{3,7},{4,5},{5,4},{6,2},{7,3},{8,9},{9,8},{10,14... | collective-permute-start | bytes 786440 | tf_op jit(solution)/shard_map/ppermute | solution.py:199
  44.3 6.2 %copy-start.1 = (bf16[128,1024]{1,0:T(8,128)(2,1)}, bf16[128,1024]{1,0:T(8,128)(2,1)S(1)}, u32[]{:S(2)}) copy-start(bf16[128,1024]{1,0:T(8,128)(2,1)S(1)} %get-tuple-element.40.refs_2_) | copy-start | bytes 786436
  44.3 10.2 %collective-permute-start.7 = (bf16[256,512]{1,0:T(8,128)(2,1)S(1)}, bf16[256,512]{1,0:T(8,128)(2,1)S(1)}, u32[]{:S(2)}, u32[]{:S(2)}) collective-permute-start(bf16[256,512]{1,0:T(8,128)(2,1)S(1)} %get-tuple-element.34), channel_id=1, source_target_pairs={{0,5},{1,4},{2,7},{3,6},{4,1},{5,0},{6,3},{7,2},{8,13},{9,12},{10,... | collective-permute-start | bytes 786440 | tf_op jit(solution)/shard_map/ppermute | solution.py:199
  47.3 3.3 %collective-permute-start.14 = (bf16[128,1024]{1,0:T(8,128)(2,1)S(1)}, bf16[128,1024]{1,0:T(8,128)(2,1)S(1)}, u32[]{:S(2)}, u32[]{:S(2)}) collective-permute-start(bf16[128,1024]{1,0:T(8,128)(2,1)S(1)} %get-tuple-element.41), channel_id=1, source_target_pairs={{0,2},{1,3},{2,0},{3,1},{4,6},{5,7},{6,4},{7,5},{8,10},{9,11},{10,... | collective-permute-start | bytes 786440 | tf_op jit(solution)/shard_map/ppermute | solution.py:199
  47.7 11.6 %collective-permute-start.8 = (bf16[256,512]{1,0:T(8,128)(2,1)S(1)}, bf16[256,512]{1,0:T(8,128)(2,1)S(1)}, u32[]{:S(2)}, u32[]{:S(2)}) collective-permute-start(bf16[256,512]{1,0:T(8,128)(2,1)S(1)} %get-tuple-element.35), channel_id=1, source_target_pairs={{0,4},{1,5},{2,3},{3,2},{4,0},{5,1},{6,7},{7,6},{8,12},{9,13},{10,... | collective-permute-start | bytes 786440 | tf_op jit(solution)/shard_map/ppermute | solution.py:199
  49.2 10.1 %collective-permute-start.9 = (bf16[256,512]{1,0:T(8,128)(2,1)S(1)}, bf16[256,512]{1,0:T(8,128)(2,1)S(1)}, u32[]{:S(2)}, u32[]{:S(2)}) collective-permute-start(bf16[256,512]{1,0:T(8,128)(2,1)S(1)} %get-tuple-element.36), channel_id=1, source_target_pairs={{0,1},{1,0},{2,6},{3,7},{4,5},{5,4},{6,2},{7,3},{8,9},{9,8},{10,14... | collective-permute-start | bytes 786440 | tf_op jit(solution)/shard_map/ppermute | solution.py:199
  50.5 0.7 %copy-start.3 = (bf16[128,1024]{1,0:T(8,128)(2,1)}, bf16[128,1024]{1,0:T(8,128)(2,1)S(1)}, u32[]{:S(2)}) copy-start(bf16[128,1024]{1,0:T(8,128)(2,1)S(1)} %collective-permute-done.13.refs_1_) | copy-start | bytes 786436
  50.5 9.6 %collective-permute-start.18 = (bf16[128,512]{1,0:T(8,128)(2,1)S(1)}, bf16[128,512]{1,0:T(8,128)(2,1)S(1)}, u32[]{:S(2)}, u32[]{:S(2)}) collective-permute-start(bf16[128,512]{1,0:T(8,128)(2,1)S(1)} %get-tuple-element.55), channel_id=1, source_target_pairs={{0,2},{1,3},{2,0},{3,1},{4,6},{5,7},{6,4},{7,5},{8,10},{9,11},{10,... | collective-permute-start | bytes 393224 | tf_op jit(solution)/shard_map/ppermute | solution.py:199
  50.6 0.7 %copy-start.4 = (bf16[128,1024]{1,0:T(8,128)(2,1)}, bf16[128,1024]{1,0:T(8,128)(2,1)S(1)}, u32[]{:S(2)}) copy-start(bf16[128,1024]{1,0:T(8,128)(2,1)S(1)} %collective-permute-done.14.refs_3_) | copy-start | bytes 786436
  60.1 1.3 %collective-permute-start.19 = (bf16[128,512]{1,0:T(8,128)(2,1)S(1)}, bf16[128,512]{1,0:T(8,128)(2,1)S(1)}, u32[]{:S(2)}, u32[]{:S(2)}) collective-permute-start(bf16[128,512]{1,0:T(8,128)(2,1)S(1)} %get-tuple-element.53), channel_id=1, source_target_pairs={{0,2},{1,3},{2,0},{3,1},{4,6},{5,7},{6,4},{7,5},{8,10},{9,11},{10,... | collective-permute-start | bytes 393224 | tf_op jit(solution)/shard_map/ppermute | solution.py:199
  60.1 1.3 %copy-start.5 = (bf16[128,512]{1,0:T(8,128)(2,1)}, bf16[128,512]{1,0:T(8,128)(2,1)S(1)}, u32[]{:S(2)}) copy-start(bf16[128,512]{1,0:T(8,128)(2,1)S(1)} %collective-permute-done.18.refs_1_) | copy-start | bytes 393220
  61.4 0.6 copy-start.6

commit v4 on v3

--- a/solution.py
+++ b/solution.py
@@ -506,16 +506,15 @@
             dout_other,
             (pairs[chunk], nears[chunk], fars[chunk], corners[chunk]),
         )
-        arrived = [
-            send(corner_grads, CORNER_PERM),
-            send(near_grads, NEAR_PERM),
-            send(far_grads, FAR_PERM),
-        ]
+        arrived = [send(corner_grads, CORNER_PERM), send(near_grads, NEAR_PERM)]
+        if terms:
+            far_grads, terms[-1] = lax.optimization_barrier((far_grads, terms[-1]))
+        arrived.append(send(far_grads, FAR_PERM))
         terms.append((own_grads, arrived))
         dq_own.append(dq_mine)
         dq_got.append(send(dq_other, SWAP_PERM))
     d_queries = place_queries(where, dq_own, dq_got)
-    terms[-1], d_queries = lax.optimization_barrier((terms[-1], d_queries))
+
     own, other = [], []
     for own_grads, arrived in terms:
         mine, theirs = (
@@ -524,7 +523,19 @@
         )
         own.append(mine)
         other.append(send(theirs, SWAP_PERM))
-    d_keys, d_values = place_pairs(where, own, other)
+    first = half == 0
+    d_keys, d_values = (
+        jnp.concatenate(
+            [
+                jnp.where(first == (side == 0), mine[:, at : at + HEAD_DIM], got[:, at : at + HEAD_DIM])
+                for side in range(2)
+                for mine, got in zip(own, other)
+                for at in range(place * HEAD_DIM, mine.shape[1], 2 * HEAD_DIM)
+            ],
+            axis=1,
+        )
+        for place in range(2)
+    )
     return (d_queries, d_keys, d_values)
 
 

time: 65.1 us -> 64.1 us (0.985)
  waiting for transfers between devices: 15.7 us -> 19.1 us
  Pallas kernels: 24.8 us -> 22.2 us
  other arithmetic: 1.64 us -> 0.68 us
  starting transfers between devices: 19.5 us -> 18.8 us
    ppermute x20, waiting for transfers between devices: 15.7 us -> 19.1 us  [send(): return lax.ppermute(array, AXES, perm)]
    pallas_call x2 -> x1, Pallas kernels: 5.46 us -> 2.86 us  [place(): pl.pallas_call(partial(place_kernel, columns), out_shape=[jax.ShapeDtypeS...]
    convert_element_type x2, other arithmetic: 1.57 us -> 0.28 us  [per_device_dense(): sum((x[at].astype(jnp.float32) for x in arrived), own_grads[at])]
    ppermute x20, starting transfers between devices: 19.5 us -> 18.8 us  [send(): return lax.ppermute(array, AXES, perm)]
  transfers between devices with their start and end apart: 20 -> 20, of which waited for: 8 -> 8; matrix products, arithmetic and copies ran while one was open for 3% -> 1% of each run, Pallas kernels for 32% -> 32%
where the time goes in v4:
time: 64.1 us; the launch traced here: 63.9 us
  Pallas kernels  22.2 us (35%)
  waiting for transfers between devices  19.1 us (30%)
  starting transfers between devices  18.8 us (29%)
  local copies, waits for them, and re-layouts  2.28 us (4%)
  between operations  0.82 us (1%)
  other arithmetic  0.68 us (1%)
    ppermute x20, waiting for transfers between devices, send(): return lax.ppermute(array, AXES, perm)  19.1 us
    ppermute x20, starting transfers between devices, send(): return lax.ppermute(array, AXES, perm)  18.8 us
    pallas_call x2, Pallas kernels, attend(): pl.pallas_call(attend_kernel, out_shape=[OUT(dq_shape), OUT(dq_shape), wi...  17.8 us
    pallas_call x1, Pallas kernels, place(): pl.pallas_call(partial(place_kernel, columns), out_shape=[jax.ShapeDtypeS...  2.86 us
    unnamed x19, local copies, waits for them, and re-layouts  2.2 us
    pallas_call x1, Pallas kernels, pack_pairs(): pl.pallas_call(pack_kernel, out_shape=[jax.ShapeDtypeStruct((PAIR, 2 * HE...  1.58 us
  transfers between devices with their start and end apart: 20, of which 8 were waited for; matrix products, arithmetic and copies ran while one was open for 1% of the time, Pallas kernels for 32%

profile of v4, /device:TPU:0, one launch (start us, length us, event | category | flops | bytes accessed | tf_op | source)
XLA Modules:
  0.0 63.9 jit_solution(3277982321081428276)
XLA Ops:
  0.6 0.0 copy-start.8
  0.6 0.5 collective-permute-start
  1.2 0.1 collective-permute-start.1
  1.2 0.1 pad_add_fusion.where_ref
  1.3 1.2 %collective-permute-done.ko_ref = bf16[128,1024]{1,0:T(8,128)(2,1)S(1)} collective-permute-done((bf16[128,1024]{1,0:T(8,128)(2,1)}, bf16[128,1024]{1,0:T(8,128)(2,1)S(1)}, u32[]{:S(2)}, u32[]{:S(2)}) %collective-permute-start) | collective-permute-done | bytes 262176 | tf_op jit(solution)/shard_map/ppermute | solution.py:199
  2.5 0.4 collective-permute-done.1.vo_ref
  2.9 1.6 %pack_pairs.1 = (bf16[256,512]{1,0:T(8,128)(2,1)S(1)}, bf16[256,512]{1,0:T(8,128)(2,1)S(1)}) custom-call(s32[2]{0:T(128)S(1)} %pad_add_fusion.where_ref, bf16[128,1024]{1,0:T(8,128)(2,1)} %k_ref.1, bf16[128,1024]{1,0:T(8,128)(2,1)} %v_ref.1, bf16[128,1024]{1,0:T(8,128)(2,1)S(1)} %collective-permute-done.ko_ref, ...), custom_call_target="tpu_custom_call" | custom-call | bytes 1048576 | tf_op jit(solution)/shard_map/pack_pairs/pallas_call | solution.py:232
  4.5 0.0 copy-start.7
  4.5 0.4 collective-permute-start.2
  5.0 0.1 collective-permute-start.3
  5.1 2.9 %collective-permute-start.4 = (bf16[256,512]{1,0:T(8,128)(2,1)S(1)}, bf16[256,512]{1,0:T(8,128)(2,1)S(1)}, u32[]{:S(2)}, u32[]{:S(2)}) collective-permute-start(bf16[256,512]{1,0:T(8,128)(2,1)S(1)} %get-tuple-element.30.pair_ref), channel_id=1, source_target_pairs={{0,4},{1,5},{2,3},{3,2},{4,0},{5,1},{6,7},{7,6},{8,12},{9,13},{10,... | collective-permute-start | bytes 786440 | tf_op jit(solution)/shard_map/ppermute | solution.py:199
  8.0 0.0 collective-permute-start.8
  8.0 2.0 %collective-permute-start.5 = (bf16[256,512]{1,0:T(8,128)(2,1)S(1)}, bf16[256,512]{1,0:T(8,128)(2,1)S(1)}, u32[]{:S(2)}, u32[]{:S(2)}) collective-permute-start(bf16[256,512]{1,0:T(8,128)(2,1)S(1)} %get-tuple-element.30.pair_ref), channel_id=1, source_target_pairs={{0,1},{1,0},{2,6},{3,7},{4,5},{5,4},{6,2},{7,3},{8,9},{9,8},{10,14... | collective-permute-start | bytes 786440 | tf_op jit(solution)/shard_map/ppermute | solution.py:199
  10.0 4.1 %collective-permute-done.4.near_ref = bf16[256,512]{1,0:T(8,128)(2,1)S(1)} collective-permute-done((bf16[256,512]{1,0:T(8,128)(2,1)S(1)}, bf16[256,512]{1,0:T(8,128)(2,1)S(1)}, u32[]{:S(2)}, u32[]{:S(2)}) %collective-permute-start.4) | collective-permute-done | bytes 262176 | tf_op jit(solution)/shard_map/ppermute | solution.py:199
  14.1 2.4 %collective-permute-start.6 = (bf16[256,512]{1,0:T(8,128)(2,1)S(1)}, bf16[256,512]{1,0:T(8,128)(2,1)S(1)}, u32[]{:S(2)}, u32[]{:S(2)}) collective-permute-start(bf16[256,512]{1,0:T(8,128)(2,1)S(1)} %collective-permute-done.4.near_ref), channel_id=1, source_target_pairs={{0,1},{1,0},{2,6},{3,7},{4,5},{5,4},{6,2},{7,3},{8,9},{9,8},{10,14... | collective-permute-start | bytes 786440 | tf_op jit(solution)/shard_map/ppermute | solution.py:199
  16.6 0.1 copy.9
  16.7 0.1 reshape.9.rand_ref
  16.8 3.0 %collective-permute-done.8.near_ref = bf16[256,512]{1,0:T(8,128)(2,1)S(1)} collective-permute-done((bf16[256,512]{1,0:T(8,128)(2,1)S(1)}, bf16[256,512]{1,0:T(8,128)(2,1)S(1)}, u32[]{:S(2)}, u32[]{:S(2)}) %collective-permute-start.8) | collective-permute-done | bytes 262176 | tf_op jit(solution)/shard_map/ppermute | solution.py:199
  19.8 2.4 %collective-permute-start.9 = (bf16[256,512]{1,0:T(8,128)(2,1)S(1)}, bf16[256,512]{1,0:T(8,128)(2,1)S(1)}, u32[]{:S(2)}, u32[]{:S(2)}) collective-permute-start(bf16[256,512]{1,0:T(8,128)(2,1)S(1)} %get-tuple-element.33.pair_ref), channel_id=1, source_target_pairs={{0,1},{1,0},{2,6},{3,7},{4,5},{5,4},{6,2},{7,3},{8,9},{9,8},{10,14... | collective-permute-start | bytes 786440 | tf_op jit(solution)/shard_map/ppermute | solution.py:199
  22.2 0.0 collective-permute-start.10
  22.2 8.9 %attend.2 = (bf16[128,1024]{1,0:T(8,128)(2,1)S(1)}, bf16[128,1024]{1,0:T(8,128)(2,1)S(1)}, f32[256,512]{1,0:T(8,128)S(1)}, bf16[256,512]{1,0:T(8,128)(2,1)S(1)},...) custom-call(s32[2]{0:T(128)S(1)} %pad_add_fusion.where_ref, s32[24]{0:T(128)S(1)} %reshape.9.rand_ref, ...), custom_call_target="tpu_custom_call" | custom-call | flops 5368709120 | bytes 4194304 | tf_op jit(solution)/shard_map/attend/pallas_call | solution.py:405
  31.2 0.0 copy-start
  31.2 0.7 %copy-done = bf16[128,1024]{1,0:T(8,128)(2,1)} copy-done((bf16[128,1024]{1,0:T(8,128)(2,1)}, bf16[128,1024]{1,0:T(8,128)(2,1)S(1)}, u32[]{:S(2)}) %copy-start) | copy-done | bytes 262168
  31.9 2.9 %collective-permute-start.12 = (bf16[256,512]{1,0:T(8,128)(2,1)S(1)}, bf16[256,512]{1,0:T(8,128)(2,1)S(1)}, u32[]{:S(2)}, u32[]{:S(2)}) collective-permute-start(bf16[256,512]{1,0:T(8,128)(2,1)S(1)} %get-tuple-element.38), channel_id=1, source_target_pairs={{0,5},{1,4},{2,7},{3,6},{4,1},{5,0},{6,3},{7,2},{8,13},{9,12},{10,... | collective-permute-start | bytes 786440 | tf_op jit(solution)/shard_map/ppermute | solution.py:199
  34.8 0.5 collective-permute-start.13
  35.3 0.0 collective-permute-start.14
  35.4 8.9 %attend.3 = (bf16[128,1024]{1,0:T(8,128)(2,1)S(1)}, bf16[128,1024]{1,0:T(8,128)(2,1)S(1)}, f32[256,512]{1,0:T(8,128)S(1)}, bf16[256,512]{1,0:T(8,128)(2,1)S(1)},...) custom-call(s32[2]{0:T(128)S(1)} %pad_add_fusion.where_ref, s32[24]{0:T(128)S(1)} %reshape.9.rand_ref, ...), custom_call_target="tpu_custom_call" | custom-call | flops 5368709120 | bytes 4194304 | tf_op jit(solution)/shard_map/attend/pallas_call | solution.py:405
  44.3 0.1 collective-permute-start.11
  44.4 0.5 collective-permute-start.7
  44.9 1.0 %collective-permute-done.13 = bf16[256,512]{1,0:T(8,128)(2,1)S(1)} collective-permute-done((bf16[256,512]{1,0:T(8,128)(2,1)S(1)}, bf16[256,512]{1,0:T(8,128)(2,1)S(1)}, u32[]{:S(2)}, u32[]{:S(2)}) %collective-permute-start.13) | collective-permute-done | bytes 262176 | tf_op jit(solution)/shard_map/ppermute | solution.py:199
  45.8 0.1 add_convert_fusion.3
  46.0 0.1 collective-permute-start.15
  46.0 2.0 %collective-permute-start.16 = (bf16[256,512]{1,0:T(8,128)(2,1)S(1)}, bf16[256,512]{1,0:T(8,128)(2,1)S(1)}, u32[]{:S(2)}, u32[]{:S(2)}) collective-permute-start(bf16[256,512]{1,0:T(8,128)(2,1)S(1)} %get-tuple-element.46), channel_id=1, source_target_pairs={{0,5},{1,4},{2,7},{3,6},{4,1},{5,0},{6,3},{7,2},{8,13},{9,12},{10,... | collective-permute-start | bytes 786440 | tf_op jit(solution)/shard_map/ppermute | solution.py:199
  48.1 0.9 %collective-permute-start.17 = (bf16[256,512]{1,0:T(8,128)(2,1)S(1)}, bf16[256,512]{1,0:T(8,128)(2,1)S(1)}, u32[]{:S(2)}, u32[]{:S(2)}) collective-permute-start(bf16[256,512]{1,0:T(8,128)(2,1)S(1)} %get-tuple-element.47), channel_id=1, source_target_pairs={{0,4},{1,5},{2,3},{3,2},{4,0},{5,1},{6,7},{7,6},{8,12},{9,13},{10,... | collective-permute-start | bytes 786440 | tf_op jit(solution)/shard_map/ppermute | solution.py:199
  49.0 0.6 collective-permute-start.18
  49.6 0.1 copy-done.3
  49.7 0.6 copy-done.4
  50.3 2.9 %place_queries.1 = bf16[128,4096]{1,0:T(8,128)(2,1)} custom-call(s32[2]{0:T(128)} %copy-done.2, bf16[128,1024]{1,0:T(8,128)(2,1)} %copy-done, bf16[128,1024]{1,0:T(8,128)(2,1)} %copy-done.4, bf16[128,1024]{1,0:T(8,128)(2,1)} %copy-done.1, bf16[128,1024]{1,0:T(8,128)(2,1)} %copy-done.3), custom_call_target="tpu_custom_call" | custom-call | bytes 1048576 | tf_op jit(solution)/shard_map/place_queries/pallas_call | solution.py:449
  53.2 3.0 %collective-permute-done.16 = bf16[256,512]{1,0:T(8,128)(2,1)S(1)} collective-permute-done((bf16[256,512]{1,0:T(8,128)(2,1)S(1)}, bf16[256,512]{1,0:T(8,128)(2,1)S(1)}, u32[]{:S(2)}, u32[]{:S(2)}) %collective-permute-start.16) | collective-permute-done | bytes 262176 | tf_op jit(solution)/shard_map/ppermute | solution.py:199
  56.2 5.1 %collective-permute-done.17 = bf16[256,512]{1,0:T(8,128)(2,1)S(1)} collective-permute-done((bf16[256,512]{1,0:T(8,128)(2,1)S(1)}, bf16[256,512]{1,0:T(8,128)(2,1)S(1)}, u32[]{:S(2)}, u32[]{:S(2)}) %collective-permute-start.17) | collective-permute-done | bytes 262176 | tf_op jit(solution)/shard_map/ppermute | solution.py:199
  61.3 0.0 collective-permute-done.18
  61.3 0.1 add_convert_fusion.1
  61.4 0.1 collective-permute-start.19
  61.5 1.3 %collective-permute-done.19 = bf16[128,512]{1,0:T(8,128)(2,1)S(1)} collective-permute-done((bf16[128,512]{1,0:T(8,128)(2,1)S(1)}, bf16[128,512]{1,0:T(8,128)(2,1)S(1)}, u32[]{:S(2)}, u32[]{:S(2)}) %collective-permute-start.19) | collective-permute-done | bytes 131104 | tf_op jit(solution)/shard_map/ppermute | solution.py:199
  63.0 0.0 copy-start.5
  63.2 0.0 copy-start.6
  63.2 0.6 copy-done.5
  63.7 0.1 copy-done.6
  (31 shorter events, 0.4 us)
Async XLA Ops:
  0.6 3.9 %copy-start.8 = (bf16[128,4096]{1,0:T(8,128)(2,1)S(1)}, bf16[128,4096]{1,0:T(8,128)(2,1)}, u32[]{:S(2)}) copy-start(bf16[128,4096]{1,0:T(8,128)(2,1)} %q_ref.1) | copy-start | bytes 3145732
  0.6 1.9 %collective-permute-start = (bf16[128,1024]{1,0:T(8,128)(2,1)}, bf16[128,1024]{1,0:T(8,128)(2,1)S(1)}, u32[]{:S(2)}, u32[]{:S(2)}) collective-permute-start(bf16[128,1024]{1,0:T(8,128)(2,1)} %k_ref.1), channel_id=1, source_target_pairs={{0,2},{1,3},{2,0},{3,1},{4,6},{5,7},{6,4},{7,5},{8,10},{9,11},{10,... | collective-permute-start | bytes 786440 | tf_op jit(solution)/shard_map/ppermute | solution.py:199
  1.2 1.7 %collective-permute-start.1 = (bf16[128,1024]{1,0:T(8,128)(2,1)}, bf16[128,1024]{1,0:T(8,128)(2,1)S(1)}, u32[]{:S(2)}, u32[]{:S(2)}) collective-permute-start(bf16[128,1024]{1,0:T(8,128)(2,1)} %v_ref.1), channel_id=1, source_target_pairs={{0,2},{1,3},{2,0},{3,1},{4,6},{5,7},{6,4},{7,5},{8,10},{9,11},{10,... | collective-permute-start | bytes 786440 | tf_op jit(solution)/shard_map/ppermute | solution.py:199
  1.3 34.0 %copy-start.2 = (s32[2]{0:T(128)}, s32[2]{0:T(128)S(1)}, u32[]{:S(2)}) copy-start(s32[2]{0:T(128)S(1)} %pad_add_fusion.where_ref) | copy-start | bytes 28
  4.5 12.1 %copy-start.7 = (s32[8,3]{0,1:T(4,128)S(1)}, s32[8,3]{0,1:T(4,128)}, u32[]{:S(2)}) copy-start(s32[8,3]{0,1:T(4,128)} %param.9) | copy-start | bytes 292
  4.5 17.7 %collective-permute-start.2 = (bf16[128,4096]{1,0:T(8,128)(2,1)S(1)}, bf16[128,4096]{1,0:T(8,128)(2,1)}, u32[]{:S(2)}, u32[]{:S(2)}) collective-permute-start(bf16[128,4096]{1,0:T(8,128)(2,1)S(1)} %copy-done.8), channel_id=1, source_target_pairs={{0,2},{1,3},{2,0},{3,1},{4,6},{5,7},{6,4},{7,5},{8,10},{9,11},{10,... | collective-permute-start | bytes 3145736 | tf_op jit(solution)/shard_map/ppermute | solution.py:199
  5.0 17.3 %collective-permute-start.3 = (bf16[128,4096]{1,0:T(8,128)(2,1)}, bf16[128,4096]{1,0:T(8,128)(2,1)}, u32[]{:S(2)}, u32[]{:S(2)}) collective-permute-start(bf16[128,4096]{1,0:T(8,128)(2,1)} %do_ref.1), channel_id=1, source_target_pairs={{0,2},{1,3},{2,0},{3,1},{4,6},{5,7},{6,4},{7,5},{8,10},{9,11},{10,... | collective-permute-start | bytes 3145736 | tf_op jit(solution)/shard_map/ppermute | solution.py:199
  5.1 9.1 %collective-permute-start.4 = (bf16[256,512]{1,0:T(8,128)(2,1)S(1)}, bf16[256,512]{1,0:T(8,128)(2,1)S(1)}, u32[]{:S(2)}, u32[]{:S(2)}) collective-permute-start(bf16[256,512]{1,0:T(8,128)(2,1)S(1)} %get-tuple-element.30.pair_ref), channel_id=1, source_target_pairs={{0,4},{1,5},{2,3},{3,2},{4,0},{5,1},{6,7},{7,6},{8,12},{9,13},{10,... | collective-permute-start | bytes 786440 | tf_op jit(solution)/shard_map/ppermute | solution.py:199
  8.0 11.8 %collective-permute-start.8 = (bf16[256,512]{1,0:T(8,128)(2,1)S(1)}, bf16[256,512]{1,0:T(8,128)(2,1)S(1)}, u32[]{:S(2)}, u32[]{:S(2)}) collective-permute-start(bf16[256,512]{1,0:T(8,128)(2,1)S(1)} %get-tuple-element.33.pair_ref), channel_id=1, source_target_pairs={{0,4},{1,5},{2,3},{3,2},{4,0},{5,1},{6,7},{7,6},{8,12},{9,13},{10,... | collective-permute-start | bytes 786440 | tf_op jit(solution)/shard_map/ppermute | solution.py:199
  8.0 14.2 %collective-permute-start.5 = (bf16[256,512]{1,0:T(8,128)(2,1)S(1)}, bf16[256,512]{1,0:T(8,128)(2,1)S(1)}, u32[]{:S(2)}, u32[]{:S(2)}) collective-permute-start(bf16[256,512]{1,0:T(8,128)(2,1)S(1)} %get-tuple-element.30.pair_ref), channel_id=1, source_target_pairs={{0,1},{1,0},{2,6},{3,7},{4,5},{5,4},{6,2},{7,3},{8,9},{9,8},{10,14... | collective-permute-start | bytes 786440 | tf_op jit(solution)/shard_map/ppermute | solution.py:199
  14.1 8.1 %collective-permute-start.6 = (bf16[256,512]{1,0:T(8,128)(2,1)S(1)}, bf16[256,512]{1,0:T(8,128)(2,1)S(1)}, u32[]{:S(2)}, u32[]{:S(2)}) collective-permute-start(bf16[256,512]{1,0:T(8,128)(2,1)S(1)} %collective-permute-done.4.near_ref), channel_id=1, source_target_pairs={{0,1},{1,0},{2,6},{3,7},{4,5},{5,4},{6,2},{7,3},{8,9},{9,8},{10,14... | collective-permute-start | bytes 786440 | tf_op jit(solution)/shard_map/ppermute | solution.py:199
  19.8 15.6 %collective-permute-start.9 = (bf16[256,512]{1,0:T(8,128)(2,1)S(1)}, bf16[256,512]{1,0:T(8,128)(2,1)S(1)}, u32[]{:S(2)}, u32[]{:S(2)}) collective-permute-start(bf16[256,512]{1,0:T(8,128)(2,1)S(1)} %get-tuple-element.33.pair_ref), channel_id=1, source_target_pairs={{0,1},{1,0},{2,6},{3,7},{4,5},{5,4},{6,2},{7,3},{8,9},{9,8},{10,14... | collective-permute-start | bytes 786440 | tf_op jit(solution)/shard_map/ppermute | solution.py:199
  22.2 13.2 %collective-permute-start.10 = (bf16[256,512]{1,0:T(8,128)(2,1)S(1)}, bf16[256,512]{1,0:T(8,128)(2,1)S(1)}, u32[]{:S(2)}, u32[]{:S(2)}) collective-permute-start(bf16[256,512]{1,0:T(8,128)(2,1)S(1)} %collective-permute-done.8.near_ref), channel_id=1, source_target_pairs={{0,1},{1,0},{2,6},{3,7},{4,5},{5,4},{6,2},{7,3},{8,9},{9,8},{10,14... | collective-permute-start | bytes 786440 | tf_op jit(solution)/shard_map/ppermute | solution.py:199
  31.2 0.7 %copy-start = (bf16[128,1024]{1,0:T(8,128)(2,1)}, bf16[128,1024]{1,0:T(8,128)(2,1)S(1)}, u32[]{:S(2)}) copy-start(bf16[128,1024]{1,0:T(8,128)(2,1)S(1)} %get-tuple-element.31.refs_0_) | copy-start | bytes 786436
  31.9 13.0 %collective-permute-start.12 = (bf16[256,512]{1,0:T(8,128)(2,1)S(1)}, bf16[256,512]{1,0:T(8,128)(2,1)S(1)}, u32[]{:S(2)}, u32[]{:S(2)}) collective-permute-start(bf16[256,512]{1,0:T(8,128)(2,1)S(1)} %get-tuple-element.38), channel_id=1, source_target_pairs={{0,5},{1,4},{2,7},{3,6},{4,1},{5,0},{6,3},{7,2},{8,13},{9,12},{10,... | collective-permute-start | bytes 786440 | tf_op jit(solution)/shard_map/ppermute | solution.py:199
  34.8 11.0 %collective-permute-start.13 = (bf16[256,512]{1,0:T(8,128)(2,1)S(1)}, bf16[256,512]{1,0:T(8,128)(2,1)S(1)}, u32[]{:S(2)}, u32[]{:S(2)}) collective-permute-start(bf16[256,512]{1,0:T(8,128)(2,1)S(1)} %get-tuple-element.39), channel_id=1, source_target_pairs={{0,4},{1,5},{2,3},{3,2},{4,0},{5,1},{6,7},{7,6},{8,12},{9,13},{10,... | collective-permute-start | bytes 786440 | tf_op jit(solution)/shard_map/ppermute | solution.py:199
  35.3 10.5 %collective-permute-start.14 = (bf16[256,512]{1,0:T(8,128)(2,1)S(1)}, bf16[256,512]{1,0:T(8,128)(2,1)S(1)}, u32[]{:S(2)}, u32[]{:S(2)}) collective-permute-start(bf16[256,512]{1,0:T(8,128)(2,1)S(1)} %get-tuple-element.40), channel_id=1, source_target_pairs={{0,1},{1,0},{2,6},{3,7},{4,5},{5,4},{6,2},{7,3},{8,9},{9,8},{10,14... | collective-permute-start | bytes 786440 | tf_op jit(solution)/shard_map/ppermute | solution.py:199
  44.3 1.7 %copy-start.1 = (bf16[128,1024]{1,0:T(8,128)(2,1)}, bf16[128,1024]{1,0:T(8,128)(2,1)S(1)}, u32[]{:S(2)}) copy-start(bf16[128,1024]{1,0:T(8,128)(2,1)S(1)} %get-tuple-element.34.refs_2_) | copy-start | bytes 786436
  44.3 4.7 %collective-permute-start.11 = (bf16[128,1024]{1,0:T(8,128)(2,1)S(1)}, bf16[128,1024]{1,0:T(8,128)(2,1)S(1)}, u32[]{:S(2)}, u32[]{:S(2)}) collective-permute-start(bf16[128,1024]{1,0:T(8,128)(2,1)S(1)} %get-tuple-element.35), channel_id=1, source_target_pairs={{0,2},{1,3},{2,0},{3,1},{4,6},{5,7},{6,4},{7,5},{8,10},{9,11},{10,... | collective-permute-start | bytes 786440 | tf_op jit(solution)/shard_map/ppermute | solution.py:199
  44.4 5.3 %collective-permute-start.7 = (bf16[128,1024]{1,0:T(8,128)(2,1)S(1)}, bf16[128,1024]{1,0:T(8,128)(2,1)S(1)}, u32[]{:S(2)}, u32[]{:S(2)}) collective-permute-start(bf16[128,1024]{1,0:T(8,128)(2,1)S(1)} %get-tuple-element.32), channel_id=1, source_target_pairs={{0,2},{1,3},{2,0},{3,1},{4,6},{5,7},{6,4},{7,5},{8,10},{9,11},{10,... | collective-permute-start | bytes 786440 | tf_op jit(solution)/shard_map/ppermute | solution.py:199
  46.0 7.2 %collective-permute-start.15 = (bf16[128,512]{1,0:T(8,128)(2,1)S(1)}, bf16[128,512]{1,0:T(8,128)(2,1)S(1)}, u32[]{:S(2)}, u32[]{:S(2)}) collective-permute-start(bf16[128,512]{1,0:T(8,128)(2,1)S(1)} %get-tuple-element.52), channel_id=1, source_target_pairs={{0,2},{1,3},{2,0},{3,1},{4,6},{5,7},{6,4},{7,5},{8,10},{9,11},{10,... | collective-permute-start | bytes 393224 | tf_op jit(solution)/shard_map/ppermute | solution.py:199
  46.0 10.1 %collective-permute-start.16 = (bf16[256,512]{1,0:T(8,128)(2,1)S(1)}, bf16[256,512]{1,0:T(8,128)(2,1)S(1)}, u32[]{:S(2)}, u32[]{:S(2)}) collective-permute-start(bf16[256,512]{1,0:T(8,128)(2,1)S(1)} %get-tuple-element.46), channel_id=1, source_target_pairs={{0,5},{1,4},{2,7},{3,6},{4,1},{5,0},{6,3},{7,2},{8,13},{9,12},{10,... | collective-permute-start | bytes 786440 | tf_op jit(solution)/shard_map/ppermute | solution.py:199
  48.1 13.2 %collective-permute-start.17 = (bf16[256,512]{1,0:T(8,128)(2,1)S(1)}, bf16[256,512]{1,0:T(8,128)(2,1)S(1)}, u32[]{:S(2)}, u32[]{:S(2)}) collective-permute-start(bf16[256,512]{1,0:T(8,128)(2,1)S(1)} %get-tuple-element.47), channel_id=1, source_target_pairs={{0,4},{1,5},{2,3},{3,2},{4,0},{5,1},{6,7},{7,6},{8,12},{9,13},{10,... | collective-permute-start | bytes 786440 | tf_op jit(solution)/shard_map/ppermute | solution.py:199
  49.0 0.7 %copy-start.3 = (bf16[128,1024]{1,0:T(8,128)(2,1)}, bf16[128,1024]{1,0:T(8,128)(2,1)S(1)}, u32[]{:S(2)}) copy-start(bf16[128,1024]{1,0:T(8,128)(2,1)S(1)} %collective-permute-done.11.refs_3_) | copy-start | bytes 786436
  49.0 12.3 %collective-permute-start.18 = (bf16[256,512]{1,0:T(8,128)(2,1)S(1)}, bf16[256,512]{1,0:T(8,128)(2,1)S(1)}, u32[]{:S(2)}, u32[]{:S(2)}) collective-permute-start(bf16[256,512]{1,0:T(8,128)(2,1)S(1)} %get-tuple-element.48), channel_id=1, source_target_pairs={{0,1},{1,0},{2,6},{3,7},{4,5},{5,4},{6,2},{7,3},{8,9},{9,8},{10,14... | collective-permute-start | bytes 786440 | tf_op jit(solution)/shard_map/ppermute | solution.py:199
  49.6 0.7 %copy-start.4 = (bf16[128,1024]{1,0:T(8,128)(2,1)}, bf16[128,1024]{1,0:T(8,128)(2,1)S(1)}, u32[]{:S(2)}) copy-start(bf16[128,1024]{1,0:T(8,128)(2,1)S(1)} %collective-permute-done.7.refs_1_) | copy-start | bytes 786436
  61.4 1.4 %collective-permute-start.19 = (bf16[128,512]{1,0:T(8,128)(2,1)S(1)}, bf16[128,512]{1,0:T(8,128)(2,1)S(1)}, u32[]{:S(2)}, u32[]{:S(2)}) collective-permute-start(bf16[128,512]{1,0:T(8,128)(2,1)S(1)} %get-tuple-element.50), channel_id=1, source_target_pairs={{0,2},{1,3},{2,0},{3,1},{4,6},{5,7},{6,4},{7,5},{8,10},{9,11},{10,... | collective-permute-start | bytes 393224 | tf_op jit(solution)/shard_map/ppermute | solution.py:199
  63.0 0.7 %copy-start.5 = (bf16[128,1024]{1,0:T(8,128)(2,1)}, bf16[128,1024]{1,0:T(8,128)(2,1)S(1)}, u32[]{:S(2)}) copy-start(bf16[128,1024]{1,0:T(8,128)(2,1)S(1)} %get-tuple-element.53) | copy-start | bytes 786436
  63.2 0.7 %copy-start.6 = (bf16[128,1024]{1,0:T(8,128)(2,1)}, bf16[128,1024]{1,0:T(8,128)(2,1)S(1)}, u32[]{:S(2)}) copy-start(bf16[128,1024]{1,0:T(8,128)(2,1)S(1)} %constant_dynamic-update-slice_fusion) | copy-start | bytes 786436

commit v5 on v4

--- a/solution.py
+++ b/solution.py
@@ -173,6 +173,7 @@
 PART = 8
 HEAD_HALF = 4
 CHUNKS = (2, 2)
+RELAY = (False, True)
 VMEM_MIB = 48
 PIN2 = PIN3 = lambda x: x
 OUT = lambda x: x
@@ -404,7 +405,7 @@
     narrow = jax.ShapeDtypeStruct((PAIR, heads * kw), jnp.bfloat16)
     return pl.pallas_call(
         attend_kernel,
-        out_shape=[OUT(dq_shape), OUT(dq_shape), wide, narrow, narrow, narrow],
+        out_shape=[OUT(dq_shape), OUT(dq_shape), wide, wide if RELAY[chunk] else narrow, narrow, narrow],
         grid_spec=pltpu.PrefetchScalarGridSpec(
             num_scalar_prefetch=2,
             grid=(heads,),
@@ -506,7 +507,11 @@
             dout_other,
             (pairs[chunk], nears[chunk], fars[chunk], corners[chunk]),
         )
-        arrived = [send(corner_grads, CORNER_PERM), send(near_grads, NEAR_PERM)]
+        if RELAY[chunk]:
+            from_corner = send(corner_grads, FAR_PERM).astype(jnp.float32)
+            arrived = [send((near_grads + from_corner).astype(jnp.bfloat16), NEAR_PERM)]
+        else:
+            arrived = [send(corner_grads, CORNER_PERM), send(near_grads, NEAR_PERM)]
         if terms:
             far_grads, terms[-1] = lax.optimization_barrier((far_grads, terms[-1]))
         arrived.append(send(far_grads, FAR_PERM))

time: 64.1 us -> 62.1 us (0.969)
  waiting for transfers between devices: 19.1 us -> 14.4 us
  starting transfers between devices: 18.8 us -> 21.2 us
    ppermute x20, waiting for transfers between devices: 19.1 us -> 14.4 us  [send(): return lax.ppermute(array, AXES, perm)]
    ppermute x20, starting transfers between devices: 18.8 us -> 21.2 us  [send(): return lax.ppermute(array, AXES, perm)]
  transfers between devices with their start and end apart: 20 -> 20, of which waited for: 8 -> 7; matrix products, arithmetic and copies ran while one was open for 1% -> 1% of each run, Pallas kernels for 32% -> 33%
where the time goes in v5:
time: 62.1 us; the launch traced here: 61.8 us
  Pallas kernels  22.3 us (36%)
  starting transfers between devices  21.2 us (34%)
  waiting for transfers between devices  14.4 us (23%)
  local copies, waits for them, and re-layouts  2.36 us (4%)
  between operations  0.83 us (1%)
  other arithmetic  0.74 us (1%)
    ppermute x20, starting transfers between devices, send(): return lax.ppermute(array, AXES, perm)  21.2 us
    pallas_call x2, Pallas kernels, attend(): pl.pallas_call(attend_kernel, out_shape=[OUT(dq_shape), OUT(dq_shape), wi...  17.8 us
    ppermute x20, waiting for transfers between devices, send(): return lax.ppermute(array, AXES, perm)  14.4 us
    pallas_call x1, Pallas kernels, place(): pl.pallas_call(partial(place_kernel, columns), out_shape=[jax.ShapeDtypeS...  2.86 us
    unnamed x19, local copies, waits for them, and re-layouts  2.27 us
    pallas_call x1, Pallas kernels, pack_pairs(): pl.pallas_call(pack_kernel, out_shape=[jax.ShapeDtypeStruct((PAIR, 2 * HE...  1.58 us
  transfers between devices with their start and end apart: 20, of which 7 were waited for; matrix products, arithmetic and copies ran while one was open for 1% of the time, Pallas kernels for 33%

profile of v5, /device:TPU:0, one launch (start us, length us, event | category | flops | bytes accessed | tf_op | source)
XLA Modules:
  0.0 61.8 jit_solution(17267353552171229273)
XLA Ops:
  0.6 0.0 copy-start.8
  0.6 0.5 collective-permute-start
  1.2 0.1 collective-permute-start.1
  1.2 0.1 pad_add_fusion.where_ref
  1.3 1.2 %collective-permute-done.ko_ref = bf16[128,1024]{1,0:T(8,128)(2,1)S(1)} collective-permute-done((bf16[128,1024]{1,0:T(8,128)(2,1)}, bf16[128,1024]{1,0:T(8,128)(2,1)S(1)}, u32[]{:S(2)}, u32[]{:S(2)}) %collective-permute-start) | collective-permute-done | bytes 262176 | tf_op jit(solution)/shard_map/ppermute | solution.py:200
  2.5 0.4 collective-permute-done.1.vo_ref
  2.9 1.6 %pack_pairs.1 = (bf16[256,512]{1,0:T(8,128)(2,1)S(1)}, bf16[256,512]{1,0:T(8,128)(2,1)S(1)}) custom-call(s32[2]{0:T(128)S(1)} %pad_add_fusion.where_ref, bf16[128,1024]{1,0:T(8,128)(2,1)} %k_ref.1, bf16[128,1024]{1,0:T(8,128)(2,1)} %v_ref.1, bf16[128,1024]{1,0:T(8,128)(2,1)S(1)} %collective-permute-done.ko_ref, ...), custom_call_target="tpu_custom_call" | custom-call | bytes 1048576 | tf_op jit(solution)/shard_map/pack_pairs/pallas_call | solution.py:233
  4.5 0.0 copy-start.7
  4.5 0.4 collective-permute-start.2
  5.0 0.1 collective-permute-start.3
  5.1 2.9 %collective-permute-start.4 = (bf16[256,512]{1,0:T(8,128)(2,1)S(1)}, bf16[256,512]{1,0:T(8,128)(2,1)S(1)}, u32[]{:S(2)}, u32[]{:S(2)}) collective-permute-start(bf16[256,512]{1,0:T(8,128)(2,1)S(1)} %get-tuple-element.30.pair_ref), channel_id=1, source_target_pairs={{0,4},{1,5},{2,3},{3,2},{4,0},{5,1},{6,7},{7,6},{8,12},{9,13},{10,... | collective-permute-start | bytes 786440 | tf_op jit(solution)/shard_map/ppermute | solution.py:200
  8.0 0.0 collective-permute-start.8
  8.0 2.0 %collective-permute-start.5 = (bf16[256,512]{1,0:T(8,128)(2,1)S(1)}, bf16[256,512]{1,0:T(8,128)(2,1)S(1)}, u32[]{:S(2)}, u32[]{:S(2)}) collective-permute-start(bf16[256,512]{1,0:T(8,128)(2,1)S(1)} %get-tuple-element.30.pair_ref), channel_id=1, source_target_pairs={{0,1},{1,0},{2,6},{3,7},{4,5},{5,4},{6,2},{7,3},{8,9},{9,8},{10,14... | collective-permute-start | bytes 786440 | tf_op jit(solution)/shard_map/ppermute | solution.py:200
  10.0 4.1 %collective-permute-done.4.near_ref = bf16[256,512]{1,0:T(8,128)(2,1)S(1)} collective-permute-done((bf16[256,512]{1,0:T(8,128)(2,1)S(1)}, bf16[256,512]{1,0:T(8,128)(2,1)S(1)}, u32[]{:S(2)}, u32[]{:S(2)}) %collective-permute-start.4) | collective-permute-done | bytes 262176 | tf_op jit(solution)/shard_map/ppermute | solution.py:200
  14.1 2.4 %collective-permute-start.6 = (bf16[256,512]{1,0:T(8,128)(2,1)S(1)}, bf16[256,512]{1,0:T(8,128)(2,1)S(1)}, u32[]{:S(2)}, u32[]{:S(2)}) collective-permute-start(bf16[256,512]{1,0:T(8,128)(2,1)S(1)} %collective-permute-done.4.near_ref), channel_id=1, source_target_pairs={{0,1},{1,0},{2,6},{3,7},{4,5},{5,4},{6,2},{7,3},{8,9},{9,8},{10,14... | collective-permute-start | bytes 786440 | tf_op jit(solution)/shard_map/ppermute | solution.py:200
  16.6 0.1 copy.9
  16.7 0.1 reshape.9.rand_ref
  16.8 3.0 %collective-permute-done.8.near_ref = bf16[256,512]{1,0:T(8,128)(2,1)S(1)} collective-permute-done((bf16[256,512]{1,0:T(8,128)(2,1)S(1)}, bf16[256,512]{1,0:T(8,128)(2,1)S(1)}, u32[]{:S(2)}, u32[]{:S(2)}) %collective-permute-start.8) | collective-permute-done | bytes 262176 | tf_op jit(solution)/shard_map/ppermute | solution.py:200
  19.8 2.4 %collective-permute-start.9 = (bf16[256,512]{1,0:T(8,128)(2,1)S(1)}, bf16[256,512]{1,0:T(8,128)(2,1)S(1)}, u32[]{:S(2)}, u32[]{:S(2)}) collective-permute-start(bf16[256,512]{1,0:T(8,128)(2,1)S(1)} %get-tuple-element.33.pair_ref), channel_id=1, source_target_pairs={{0,1},{1,0},{2,6},{3,7},{4,5},{5,4},{6,2},{7,3},{8,9},{9,8},{10,14... | collective-permute-start | bytes 786440 | tf_op jit(solution)/shard_map/ppermute | solution.py:200
  22.2 0.0 collective-permute-done.5.far_ref
  22.2 0.0 collective-permute-start.10
  22.2 8.9 %attend.2 = (bf16[128,1024]{1,0:T(8,128)(2,1)S(1)}, bf16[128,1024]{1,0:T(8,128)(2,1)S(1)}, f32[256,512]{1,0:T(8,128)S(1)}, bf16[256,512]{1,0:T(8,128)(2,1)S(1)},...) custom-call(s32[2]{0:T(128)S(1)} %pad_add_fusion.where_ref, s32[24]{0:T(128)S(1)} %reshape.9.rand_ref, ...), custom_call_target="tpu_custom_call" | custom-call | flops 5368709120 | bytes 4194304 | tf_op jit(solution)/shard_map/attend/pallas_call | solution.py:406
  31.2 0.0 copy-start
  31.2 0.7 %copy-done = bf16[128,1024]{1,0:T(8,128)(2,1)} copy-done((bf16[128,1024]{1,0:T(8,128)(2,1)}, bf16[128,1024]{1,0:T(8,128)(2,1)S(1)}, u32[]{:S(2)}) %copy-start) | copy-done | bytes 262168
  31.9 2.9 %collective-permute-start.12 = (bf16[256,512]{1,0:T(8,128)(2,1)S(1)}, bf16[256,512]{1,0:T(8,128)(2,1)S(1)}, u32[]{:S(2)}, u32[]{:S(2)}) collective-permute-start(bf16[256,512]{1,0:T(8,128)(2,1)S(1)} %get-tuple-element.38), channel_id=1, source_target_pairs={{0,5},{1,4},{2,7},{3,6},{4,1},{5,0},{6,3},{7,2},{8,13},{9,12},{10,... | collective-permute-start | bytes 786440 | tf_op jit(solution)/shard_map/ppermute | solution.py:200
  34.8 0.5 collective-permute-start.13
  35.3 0.0 collective-permute-start.14
  35.4 8.9 %attend.3 = (bf16[128,1024]{1,0:T(8,128)(2,1)S(1)}, bf16[128,1024]{1,0:T(8,128)(2,1)S(1)}, f32[256,512]{1,0:T(8,128)S(1)}, f32[256,512]{1,0:T(8,128)S(1)}, bf16[...) custom-call(s32[2]{0:T(128)S(1)} %pad_add_fusion.where_ref, s32[24]{0:T(128)S(1)} %reshape.9.rand_ref, ...), custom_call_target="tpu_custom_call" | custom-call | flops 5368709120 | bytes 4194304 | tf_op jit(solution)/shard_map/attend/pallas_call | solution.py:406
  44.3 2.0 %collective-permute-start.16 = (bf16[256,512]{1,0:T(8,128)(2,1)S(1)}, bf16[256,512]{1,0:T(8,128)(2,1)S(1)}, u32[]{:S(2)}, u32[]{:S(2)}) collective-permute-start(bf16[256,512]{1,0:T(8,128)(2,1)S(1)} %get-tuple-element.47), channel_id=1, source_target_pairs={{0,1},{1,0},{2,6},{3,7},{4,5},{5,4},{6,2},{7,3},{8,9},{9,8},{10,14... | collective-permute-start | bytes 786440 | tf_op jit(solution)/shard_map/ppermute | solution.py:200
  46.4 0.5 collective-permute-start.7
  46.9 0.1 add_convert_fusion.4
  47.0 0.1 collective-permute-start.15
  47.1 3.7 %collective-permute-done.16 = bf16[256,512]{1,0:T(8,128)(2,1)S(1)} collective-permute-done((bf16[256,512]{1,0:T(8,128)(2,1)S(1)}, bf16[256,512]{1,0:T(8,128)(2,1)S(1)}, u32[]{:S(2)}, u32[]{:S(2)}) %collective-permute-start.16) | collective-permute-done | bytes 262176 | tf_op jit(solution)/shard_map/ppermute | solution.py:200
  50.8 0.1 add_convert_fusion
  50.9 2.0 %collective-permute-start.17 = (bf16[256,512]{1,0:T(8,128)(2,1)S(1)}, bf16[256,512]{1,0:T(8,128)(2,1)S(1)}, u32[]{:S(2)}, u32[]{:S(2)}) collective-permute-start(bf16[256,512]{1,0:T(8,128)(2,1)S(1)} %add_convert_fusion), channel_id=1, source_target_pairs={{0,4},{1,5},{2,3},{3,2},{4,0},{5,1},{6,7},{7,6},{8,12},{9,13},{10,... | collective-permute-start | bytes 786440 | tf_op jit(solution)/shard_map/ppermute | solution.py:200
  52.8 2.1 %collective-permute-start.18 = (bf16[256,512]{1,0:T(8,128)(2,1)S(1)}, bf16[256,512]{1,0:T(8,128)(2,1)S(1)}, u32[]{:S(2)}, u32[]{:S(2)}) collective-permute-start(bf16[256,512]{1,0:T(8,128)(2,1)S(1)} %get-tuple-element.48), channel_id=1, source_target_pairs={{0,1},{1,0},{2,6},{3,7},{4,5},{5,4},{6,2},{7,3},{8,9},{9,8},{10,14... | collective-permute-start | bytes 786440 | tf_op jit(solution)/shard_map/ppermute | solution.py:200
  54.9 0.0 copy-start.4
  54.9 0.7 %copy-done.3 = bf16[128,1024]{1,0:T(8,128)(2,1)} copy-done((bf16[128,1024]{1,0:T(8,128)(2,1)}, bf16[128,1024]{1,0:T(8,128)(2,1)S(1)}, u32[]{:S(2)}) %copy-start.3) | copy-done | bytes 262168
  55.6 0.1 copy-done.4
  55.7 2.9 %place_queries.1 = bf16[128,4096]{1,0:T(8,128)(2,1)} custom-call(s32[2]{0:T(128)} %copy-done.2, bf16[128,1024]{1,0:T(8,128)(2,1)} %copy-done, bf16[128,1024]{1,0:T(8,128)(2,1)} %copy-done.4, bf16[128,1024]{1,0:T(8,128)(2,1)} %copy-done.1, bf16[128,1024]{1,0:T(8,128)(2,1)} %copy-done.3), custom_call_target="tpu_custom_call" | custom-call | bytes 1048576 | tf_op jit(solution)/shard_map/place_queries/pallas_call | solution.py:450
  58.6 0.6 %collective-permute-done.18 = bf16[256,512]{1,0:T(8,128)(2,1)S(1)} collective-permute-done((bf16[256,512]{1,0:T(8,128)(2,1)S(1)}, bf16[256,512]{1,0:T(8,128)(2,1)S(1)}, u32[]{:S(2)}, u32[]{:S(2)}) %collective-permute-start.18) | collective-permute-done | bytes 262176 | tf_op jit(solution)/shard_map/ppermute | solution.py:200
  59.2 0.1 add_convert_fusion.2
  59.4 0.1 collective-permute-start.19
  59.5 1.3 %collective-permute-done.19 = bf16[128,512]{1,0:T(8,128)(2,1)S(1)} collective-permute-done((bf16[128,512]{1,0:T(8,128)(2,1)S(1)}, bf16[128,512]{1,0:T(8,128)(2,1)S(1)}, u32[]{:S(2)}, u32[]{:S(2)}) %collective-permute-start.19) | collective-permute-done | bytes 131104 | tf_op jit(solution)/shard_map/ppermute | solution.py:200
  61.0 0.0 copy-start.5
  61.1 0.0 copy-start.6
  61.1 0.6 copy-done.5
  61.7 0.1 copy-done.6
  (32 shorter events, 0.4 us)
Async XLA Ops:
  0.6 3.9 %copy-start.8 = (bf16[128,4096]{1,0:T(8,128)(2,1)S(1)}, bf16[128,4096]{1,0:T(8,128)(2,1)}, u32[]{:S(2)}) copy-start(bf16[128,4096]{1,0:T(8,128)(2,1)} %q_ref.1) | copy-start | bytes 3145732
  0.6 1.9 %collective-permute-start = (bf16[128,1024]{1,0:T(8,128)(2,1)}, bf16[128,1024]{1,0:T(8,128)(2,1)S(1)}, u32[]{:S(2)}, u32[]{:S(2)}) collective-permute-start(bf16[128,1024]{1,0:T(8,128)(2,1)} %k_ref.1), channel_id=1, source_target_pairs={{0,2},{1,3},{2,0},{3,1},{4,6},{5,7},{6,4},{7,5},{8,10},{9,11},{10,... | collective-permute-start | bytes 786440 | tf_op jit(solution)/shard_map/ppermute | solution.py:200
  1.2 1.7 %collective-permute-start.1 = (bf16[128,1024]{1,0:T(8,128)(2,1)}, bf16[128,1024]{1,0:T(8,128)(2,1)S(1)}, u32[]{:S(2)}, u32[]{:S(2)}) collective-permute-start(bf16[128,1024]{1,0:T(8,128)(2,1)} %v_ref.1), channel_id=1, source_target_pairs={{0,2},{1,3},{2,0},{3,1},{4,6},{5,7},{6,4},{7,5},{8,10},{9,11},{10,... | collective-permute-start | bytes 786440 | tf_op jit(solution)/shard_map/ppermute | solution.py:200
  1.3 34.0 %copy-start.2 = (s32[2]{0:T(128)}, s32[2]{0:T(128)S(1)}, u32[]{:S(2)}) copy-start(s32[2]{0:T(128)S(1)} %pad_add_fusion.where_ref) | copy-start | bytes 28
  4.5 12.1 %copy-start.7 = (s32[8,3]{0,1:T(4,128)S(1)}, s32[8,3]{0,1:T(4,128)}, u32[]{:S(2)}) copy-start(s32[8,3]{0,1:T(4,128)} %param.9) | copy-start | bytes 292
  4.5 17.7 %collective-permute-start.2 = (bf16[128,4096]{1,0:T(8,128)(2,1)S(1)}, bf16[128,4096]{1,0:T(8,128)(2,1)}, u32[]{:S(2)}, u32[]{:S(2)}) collective-permute-start(bf16[128,4096]{1,0:T(8,128)(2,1)S(1)} %copy-done.8), channel_id=1, source_target_pairs={{0,2},{1,3},{2,0},{3,1},{4,6},{5,7},{6,4},{7,5},{8,10},{9,11},{10,... | collective-permute-start | bytes 3145736 | tf_op jit(solution)/shard_map/ppermute | solution.py:200
  5.0 17.3 %collective-permute-start.3 = (bf16[128,4096]{1,0:T(8,128)(2,1)}, bf16[128,4096]{1,0:T(8,128)(2,1)}, u32[]{:S(2)}, u32[]{:S(2)}) collective-permute-start(bf16[128,4096]{1,0:T(8,128)(2,1)} %do_ref.1), channel_id=1, source_target_pairs={{0,2},{1,3},{2,0},{3,1},{4,6},{5,7},{6,4},{7,5},{8,10},{9,11},{10,... | collective-permute-start | bytes 3145736 | tf_op jit(solution)/shard_map/ppermute | solution.py:200
  5.1 9.1 %collective-permute-start.4 = (bf16[256,512]{1,0:T(8,128)(2,1)S(1)}, bf16[256,512]{1,0:T(8,128)(2,1)S(1)}, u32[]{:S(2)}, u32[]{:S(2)}) collective-permute-start(bf16[256,512]{1,0:T(8,128)(2,1)S(1)} %get-tuple-element.30.pair_ref), channel_id=1, source_target_pairs={{0,4},{1,5},{2,3},{3,2},{4,0},{5,1},{6,7},{7,6},{8,12},{9,13},{10,... | collective-permute-start | bytes 786440 | tf_op jit(solution)/shard_map/ppermute | solution.py:200
  8.0 11.8 %collective-permute-start.8 = (bf16[256,512]{1,0:T(8,128)(2,1)S(1)}, bf16[256,512]{1,0:T(8,128)(2,1)S(1)}, u32[]{:S(2)}, u32[]{:S(2)}) collective-permute-start(bf16[256,512]{1,0:T(8,128)(2,1)S(1)} %get-tuple-element.33.pair_ref), channel_id=1, source_target_pairs={{0,4},{1,5},{2,3},{3,2},{4,0},{5,1},{6,7},{7,6},{8,12},{9,13},{10,... | collective-permute-start | bytes 786440 | tf_op jit(solution)/shard_map/ppermute | solution.py:200
  8.0 14.2 %collective-permute-start.5 = (bf16[256,512]{1,0:T(8,128)(2,1)S(1)}, bf16[256,512]{1,0:T(8,128)(2,1)S(1)}, u32[]{:S(2)}, u32[]{:S(2)}) collective-permute-start(bf16[256,512]{1,0:T(8,128)(2,1)S(1)} %get-tuple-element.30.pair_ref), channel_id=1, source_target_pairs={{0,1},{1,0},{2,6},{3,7},{4,5},{5,4},{6,2},{7,3},{8,9},{9,8},{10,14... | collective-permute-start | bytes 786440 | tf_op jit(solution)/shard_map/ppermute | solution.py:200
  14.1 8.1 %collective-permute-start.6 = (bf16[256,512]{1,0:T(8,128)(2,1)S(1)}, bf16[256,512]{1,0:T(8,128)(2,1)S(1)}, u32[]{:S(2)}, u32[]{:S(2)}) collective-permute-start(bf16[256,512]{1,0:T(8,128)(2,1)S(1)} %collective-permute-done.4.near_ref), channel_id=1, source_target_pairs={{0,1},{1,0},{2,6},{3,7},{4,5},{5,4},{6,2},{7,3},{8,9},{9,8},{10,14... | collective-permute-start | bytes 786440 | tf_op jit(solution)/shard_map/ppermute | solution.py:200
  19.8 15.6 %collective-permute-start.9 = (bf16[256,512]{1,0:T(8,128)(2,1)S(1)}, bf16[256,512]{1,0:T(8,128)(2,1)S(1)}, u32[]{:S(2)}, u32[]{:S(2)}) collective-permute-start(bf16[256,512]{1,0:T(8,128)(2,1)S(1)} %get-tuple-element.33.pair_ref), channel_id=1, source_target_pairs={{0,1},{1,0},{2,6},{3,7},{4,5},{5,4},{6,2},{7,3},{8,9},{9,8},{10,14... | collective-permute-start | bytes 786440 | tf_op jit(solution)/shard_map/ppermute | solution.py:200
  22.2 13.2 %collective-permute-start.10 = (bf16[256,512]{1,0:T(8,128)(2,1)S(1)}, bf16[256,512]{1,0:T(8,128)(2,1)S(1)}, u32[]{:S(2)}, u32[]{:S(2)}) collective-permute-start(bf16[256,512]{1,0:T(8,128)(2,1)S(1)} %collective-permute-done.8.near_ref), channel_id=1, source_target_pairs={{0,1},{1,0},{2,6},{3,7},{4,5},{5,4},{6,2},{7,3},{8,9},{9,8},{10,14... | collective-permute-start | bytes 786440 | tf_op jit(solution)/shard_map/ppermute | solution.py:200
  31.2 0.7 %copy-start = (bf16[128,1024]{1,0:T(8,128)(2,1)}, bf16[128,1024]{1,0:T(8,128)(2,1)S(1)}, u32[]{:S(2)}) copy-start(bf16[128,1024]{1,0:T(8,128)(2,1)S(1)} %get-tuple-element.31.refs_0_) | copy-start | bytes 786436
  31.9 14.5 %collective-permute-start.12 = (bf16[256,512]{1,0:T(8,128)(2,1)S(1)}, bf16[256,512]{1,0:T(8,128)(2,1)S(1)}, u32[]{:S(2)}, u32[]{:S(2)}) collective-permute-start(bf16[256,512]{1,0:T(8,128)(2,1)S(1)} %get-tuple-element.38), channel_id=1, source_target_pairs={{0,5},{1,4},{2,7},{3,6},{4,1},{5,0},{6,3},{7,2},{8,13},{9,12},{10,... | collective-permute-start | bytes 786440 | tf_op jit(solution)/shard_map/ppermute | solution.py:200
  34.8 12.1 %collective-permute-start.13 = (bf16[256,512]{1,0:T(8,128)(2,1)S(1)}, bf16[256,512]{1,0:T(8,128)(2,1)S(1)}, u32[]{:S(2)}, u32[]{:S(2)}) collective-permute-start(bf16[256,512]{1,0:T(8,128)(2,1)S(1)} %get-tuple-element.39), channel_id=1, source_target_pairs={{0,4},{1,5},{2,3},{3,2},{4,0},{5,1},{6,7},{7,6},{8,12},{9,13},{10,... | collective-permute-start | bytes 786440 | tf_op jit(solution)/shard_map/ppermute | solution.py:200
  35.3 11.6 %collective-permute-start.14 = (bf16[256,512]{1,0:T(8,128)(2,1)S(1)}, bf16[256,512]{1,0:T(8,128)(2,1)S(1)}, u32[]{:S(2)}, u32[]{:S(2)}) collective-permute-start(bf16[256,512]{1,0:T(8,128)(2,1)S(1)} %get-tuple-element.40), channel_id=1, source_target_pairs={{0,1},{1,0},{2,6},{3,7},{4,5},{5,4},{6,2},{7,3},{8,9},{9,8},{10,14... | collective-permute-start | bytes 786440 | tf_op jit(solution)/shard_map/ppermute | solution.py:200
  44.3 2.7 %copy-start.1 = (bf16[128,1024]{1,0:T(8,128)(2,1)}, bf16[128,1024]{1,0:T(8,128)(2,1)S(1)}, u32[]{:S(2)}) copy-start(bf16[128,1024]{1,0:T(8,128)(2,1)S(1)} %get-tuple-element.34.refs_2_) | copy-start | bytes 786436
  44.3 6.5 %collective-permute-start.16 = (bf16[256,512]{1,0:T(8,128)(2,1)S(1)}, bf16[256,512]{1,0:T(8,128)(2,1)S(1)}, u32[]{:S(2)}, u32[]{:S(2)}) collective-permute-start(bf16[256,512]{1,0:T(8,128)(2,1)S(1)} %get-tuple-element.47), channel_id=1, source_target_pairs={{0,1},{1,0},{2,6},{3,7},{4,5},{5,4},{6,2},{7,3},{8,9},{9,8},{10,14... | collective-permute-start | bytes 786440 | tf_op jit(solution)/shard_map/ppermute | solution.py:200
  46.4 8.6 %collective-permute-start.11 = (bf16[128,1024]{1,0:T(8,128)(2,1)S(1)}, bf16[128,1024]{1,0:T(8,128)(2,1)S(1)}, u32[]{:S(2)}, u32[]{:S(2)}) collective-permute-start(bf16[128,1024]{1,0:T(8,128)(2,1)S(1)} %get-tuple-element.35), channel_id=1, source_target_pairs={{0,2},{1,3},{2,0},{3,1},{4,6},{5,7},{6,4},{7,5},{8,10},{9,11},{10,... | collective-permute-start | bytes 786440 | tf_op jit(solution)/shard_map/ppermute | solution.py:200
  46.4 8.6 %collective-permute-start.7 = (bf16[128,1024]{1,0:T(8,128)(2,1)S(1)}, bf16[128,1024]{1,0:T(8,128)(2,1)S(1)}, u32[]{:S(2)}, u32[]{:S(2)}) collective-permute-start(bf16[128,1024]{1,0:T(8,128)(2,1)S(1)} %get-tuple-element.32), channel_id=1, source_target_pairs={{0,2},{1,3},{2,0},{3,1},{4,6},{5,7},{6,4},{7,5},{8,10},{9,11},{10,... | collective-permute-start | bytes 786440 | tf_op jit(solution)/shard_map/ppermute | solution.py:200
  47.0 11.5 %collective-permute-start.15 = (bf16[128,512]{1,0:T(8,128)(2,1)S(1)}, bf16[128,512]{1,0:T(8,128)(2,1)S(1)}, u32[]{:S(2)}, u32[]{:S(2)}) collective-permute-start(bf16[128,512]{1,0:T(8,128)(2,1)S(1)} %get-tuple-element.50), channel_id=1, source_target_pairs={{0,2},{1,3},{2,0},{3,1},{4,6},{5,7},{6,4},{7,5},{8,10},{9,11},{10,... | collective-permute-start | bytes 393224 | tf_op jit(solution)/shard_map/ppermute | solution.py:200
  50.9 7.7 %collective-permute-start.17 = (bf16[256,512]{1,0:T(8,128)(2,1)S(1)}, bf16[256,512]{1,0:T(8,128)(2,1)S(1)}, u32[]{:S(2)}, u32[]{:S(2)}) collective-permute-start(bf16[256,512]{1,0:T(8,128)(2,1)S(1)} %add_convert_fusion), channel_id=1, source_target_pairs={{0,4},{1,5},{2,3},{3,2},{4,0},{5,1},{6,7},{7,6},{8,12},{9,13},{10,... | collective-permute-start | bytes 786440 | tf_op jit(solution)/shard_map/ppermute | solution.py:200
  52.8 6.4 %collective-permute-start.18 = (bf16[256,512]{1,0:T(8,128)(2,1)S(1)}, bf16[256,512]{1,0:T(8,128)(2,1)S(1)}, u32[]{:S(2)}, u32[]{:S(2)}) collective-permute-start(bf16[256,512]{1,0:T(8,128)(2,1)S(1)} %get-tuple-element.48), channel_id=1, source_target_pairs={{0,1},{1,0},{2,6},{3,7},{4,5},{5,4},{6,2},{7,3},{8,9},{9,8},{10,14... | collective-permute-start | bytes 786440 | tf_op jit(solution)/shard_map/ppermute | solution.py:200
  54.9 0.7 %copy-start.3 = (bf16[128,1024]{1,0:T(8,128)(2,1)}, bf16[128,1024]{1,0:T(8,128)(2,1)S(1)}, u32[]{:S(2)}) copy-start(bf16[128,1024]{1,0:T(8,128)(2,1)S(1)} %collective-permute-done.11.refs_3_) | copy-start | bytes 786436
  54.9 0.8 %copy-start.4 = (bf16[128,1024]{1,0:T(8,128)(2,1)}, bf16[128,1024]{1,0:T(8,128)(2,1)S(1)}, u32[]{:S(2)}) copy-start(bf16[128,1024]{1,0:T(8,128)(2,1)S(1)} %collective-permute-done.7.refs_1_) | copy-start | bytes 786436
  59.4 1.4 %collective-permute-start.19 = (bf16[128,512]{1,0:T(8,128)(2,1)S(1)}, bf16[128,512]{1,0:T(8,128)(2,1)S(1)}, u32[]{:S(2)}, u32[]{:S(2)}) collective-permute-start(bf16[128,512]{1,0:T(8,128)(2,1)S(1)} %get-tuple-element.52), channel_id=1, source_target_pairs={{0,2},{1,3},{2,0},{3,1},{4,6},{5,7},{6,4},{7,5},{8,10},{9,11},{10,... | collective-permute-start | bytes 393224 | tf_op jit(solution)/shard_map/ppermute | solution.py:200
  61.0 0.7 %copy-start.5 = (bf16[128,1024]{1,0:T(8,128)(2,1)}, bf16[128,1024]{1,0:T(8,128)(2,1)S(1)}, u32[]{:S(2)}) copy-start(bf16[128,1024]{1,0:T(8,128)(2,1)S(1)} %get-tuple-element.53) | copy-start | bytes 786436
  61.1 0.7 %copy-start.6 = (bf16[128,1024]{1,0:T(8,128)(2,1)}, bf16[128,1024]{1,0:T(8,128)(2,1)S(1)}, u32[]{:S(2)}) copy-start(bf16[128,1024]{1,0:T(8,128)(2,1)S(1)} %constant_dynamic-update-slice_fusion) | copy-start | bytes 786436

commit v6 on v5

--- a/solution.py
+++ b/solution.py
@@ -494,7 +494,7 @@
     dout_other = send(d_out, SWAP_PERM)
     nears = [send(pair, NEAR_PERM) for pair in pairs]
     fars = [send(pair, FAR_PERM) for pair in pairs]
-    corners = [send(near, FAR_PERM) for near in nears]
+    corners = [send(pairs[0], CORNER_PERM)] + [send(near, FAR_PERM) for near in nears[1:]]
     terms, dq_own, dq_got = [], [], []
     for chunk in range(len(CHUNKS)):
         dq_mine, dq_other, own_grads, near_grads, far_grads, corner_grads = attend(

time: 62.1 us -> 68.5 us (1.10)
  waiting for transfers between devices: 14.4 us -> 24.4 us
  starting transfers between devices: 21.2 us -> 17.6 us
    ppermute x20, waiting for transfers between devices: 14.4 us -> 24.4 us  [send(): return lax.ppermute(array, AXES, perm)]
    ppermute x20, starting transfers between devices: 21.2 us -> 17.6 us  [send(): return lax.ppermute(array, AXES, perm)]
  transfers between devices with their start and end apart: 20 -> 20, of which waited for: 7 -> 9; matrix products, arithmetic and copies ran while one was open for 1% -> 1% of each run, Pallas kernels for 33% -> 30%
where the time goes in v6:
time: 68.5 us; the launch traced here: 68.2 us
  waiting for transfers between devices  24.4 us (36%)
  Pallas kernels  22.2 us (32%)
  starting transfers between devices  17.6 us (26%)
  local copies, waits for them, and re-layouts  2.35 us (3%)
  between operations  0.85 us (1%)
  other arithmetic  0.74 us (1%)
    ppermute x20, waiting for transfers between devices, send(): return lax.ppermute(array, AXES, perm)  24.4 us
    pallas_call x2, Pallas kernels, attend(): pl.pallas_call(attend_kernel, out_shape=[OUT(dq_shape), OUT(dq_shape), wi...  17.8 us
    ppermute x20, starting transfers between devices, send(): return lax.ppermute(array, AXES, perm)  17.6 us
    pallas_call x1, Pallas kernels, place(): pl.pallas_call(partial(place_kernel, columns), out_shape=[jax.ShapeDtypeS...  2.86 us
    unnamed x19, local copies, waits for them, and re-layouts  2.27 us
    pallas_call x1, Pallas kernels, pack_pairs(): pl.pallas_call(pack_kernel, out_shape=[jax.ShapeDtypeStruct((PAIR, 2 * HE...  1.58 us
  transfers between devices with their start and end apart: 20, of which 9 were waited for; matrix products, arithmetic and copies ran while one was open for 1% of the time, Pallas kernels for 30%

profile of v6, /device:TPU:0, one launch (start us, length us, event | category | flops | bytes accessed | tf_op | source)
XLA Modules:
  0.0 68.2 jit_solution(9650319024746187225)
XLA Ops:
  0.6 0.0 copy-start.8
  0.6 0.5 collective-permute-start
  1.2 0.1 collective-permute-start.1
  1.2 0.1 pad_add_fusion.where_ref
  1.3 1.2 %collective-permute-done.ko_ref = bf16[128,1024]{1,0:T(8,128)(2,1)S(1)} collective-permute-done((bf16[128,1024]{1,0:T(8,128)(2,1)}, bf16[128,1024]{1,0:T(8,128)(2,1)S(1)}, u32[]{:S(2)}, u32[]{:S(2)}) %collective-permute-start) | collective-permute-done | bytes 262176 | tf_op jit(solution)/shard_map/ppermute | solution.py:200
  2.5 0.4 collective-permute-done.1.vo_ref
  2.9 1.6 %pack_pairs.1 = (bf16[256,512]{1,0:T(8,128)(2,1)S(1)}, bf16[256,512]{1,0:T(8,128)(2,1)S(1)}) custom-call(s32[2]{0:T(128)S(1)} %pad_add_fusion.where_ref, bf16[128,1024]{1,0:T(8,128)(2,1)} %k_ref.1, bf16[128,1024]{1,0:T(8,128)(2,1)} %v_ref.1, bf16[128,1024]{1,0:T(8,128)(2,1)S(1)} %collective-permute-done.ko_ref, ...), custom_call_target="tpu_custom_call" | custom-call | bytes 1048576 | tf_op jit(solution)/shard_map/pack_pairs/pallas_call | solution.py:233
  4.5 0.0 copy-start.7
  4.5 0.4 collective-permute-start.2
  5.0 0.1 collective-permute-start.3
  5.1 2.9 %collective-permute-start.8 = (bf16[256,512]{1,0:T(8,128)(2,1)S(1)}, bf16[256,512]{1,0:T(8,128)(2,1)S(1)}, u32[]{:S(2)}, u32[]{:S(2)}) collective-permute-start(bf16[256,512]{1,0:T(8,128)(2,1)S(1)} %get-tuple-element.33.pair_ref), channel_id=1, source_target_pairs={{0,4},{1,5},{2,3},{3,2},{4,0},{5,1},{6,7},{7,6},{8,12},{9,13},{10,... | collective-permute-start | bytes 786440 | tf_op jit(solution)/shard_map/ppermute | solution.py:200
  8.0 0.0 collective-permute-start.4
  8.0 2.0 %collective-permute-start.5 = (bf16[256,512]{1,0:T(8,128)(2,1)S(1)}, bf16[256,512]{1,0:T(8,128)(2,1)S(1)}, u32[]{:S(2)}, u32[]{:S(2)}) collective-permute-start(bf16[256,512]{1,0:T(8,128)(2,1)S(1)} %get-tuple-element.30.pair_ref), channel_id=1, source_target_pairs={{0,1},{1,0},{2,6},{3,7},{4,5},{5,4},{6,2},{7,3},{8,9},{9,8},{10,14... | collective-permute-start | bytes 786440 | tf_op jit(solution)/shard_map/ppermute | solution.py:200
  10.0 4.1 %collective-permute-done.8.near_ref = bf16[256,512]{1,0:T(8,128)(2,1)S(1)} collective-permute-done((bf16[256,512]{1,0:T(8,128)(2,1)S(1)}, bf16[256,512]{1,0:T(8,128)(2,1)S(1)}, u32[]{:S(2)}, u32[]{:S(2)}) %collective-permute-start.8) | collective-permute-done | bytes 262176 | tf_op jit(solution)/shard_map/ppermute | solution.py:200
  14.1 3.4 %collective-permute-start.6 = (bf16[256,512]{1,0:T(8,128)(2,1)S(1)}, bf16[256,512]{1,0:T(8,128)(2,1)S(1)}, u32[]{:S(2)}, u32[]{:S(2)}) collective-permute-start(bf16[256,512]{1,0:T(8,128)(2,1)S(1)} %get-tuple-element.30.pair_ref), channel_id=1, source_target_pairs={{0,5},{1,4},{2,7},{3,6},{4,1},{5,0},{6,3},{7,2},{8,13},{9,12},{10,... | collective-permute-start | bytes 786440 | tf_op jit(solution)/shard_map/ppermute | solution.py:200
  17.5 0.1 copy.9
  17.6 0.1 reshape.9.rand_ref
  17.7 2.1 %collective-permute-done.4.near_ref = bf16[256,512]{1,0:T(8,128)(2,1)S(1)} collective-permute-done((bf16[256,512]{1,0:T(8,128)(2,1)S(1)}, bf16[256,512]{1,0:T(8,128)(2,1)S(1)}, u32[]{:S(2)}, u32[]{:S(2)}) %collective-permute-start.4) | collective-permute-done | bytes 262176 | tf_op jit(solution)/shard_map/ppermute | solution.py:200
  19.8 2.4 %collective-permute-start.9 = (bf16[256,512]{1,0:T(8,128)(2,1)S(1)}, bf16[256,512]{1,0:T(8,128)(2,1)S(1)}, u32[]{:S(2)}, u32[]{:S(2)}) collective-permute-start(bf16[256,512]{1,0:T(8,128)(2,1)S(1)} %get-tuple-element.33.pair_ref), channel_id=1, source_target_pairs={{0,1},{1,0},{2,6},{3,7},{4,5},{5,4},{6,2},{7,3},{8,9},{9,8},{10,14... | collective-permute-start | bytes 786440 | tf_op jit(solution)/shard_map/ppermute | solution.py:200
  22.2 0.0 collective-permute-start.10
  22.2 5.0 %collective-permute-done.6.corner_ref = bf16[256,512]{1,0:T(8,128)(2,1)S(1)} collective-permute-done((bf16[256,512]{1,0:T(8,128)(2,1)S(1)}, bf16[256,512]{1,0:T(8,128)(2,1)S(1)}, u32[]{:S(2)}, u32[]{:S(2)}) %collective-permute-start.6) | collective-permute-done | bytes 262176 | tf_op jit(solution)/shard_map/ppermute | solution.py:200
  27.3 8.9 %attend.2 = (bf16[128,1024]{1,0:T(8,128)(2,1)S(1)}, bf16[128,1024]{1,0:T(8,128)(2,1)S(1)}, f32[256,512]{1,0:T(8,128)S(1)}, bf16[256,512]{1,0:T(8,128)(2,1)S(1)},...) custom-call(s32[2]{0:T(128)S(1)} %pad_add_fusion.where_ref, s32[24]{0:T(128)S(1)} %reshape.9.rand_ref, ...), custom_call_target="tpu_custom_call" | custom-call | flops 5368709120 | bytes 4194304 | tf_op jit(solution)/shard_map/attend/pallas_call | solution.py:406
  36.1 0.0 copy-start
  36.2 0.7 %copy-done = bf16[128,1024]{1,0:T(8,128)(2,1)} copy-done((bf16[128,1024]{1,0:T(8,128)(2,1)}, bf16[128,1024]{1,0:T(8,128)(2,1)S(1)}, u32[]{:S(2)}) %copy-start) | copy-done | bytes 262168
  36.9 1.4 %collective-permute-start.12 = (bf16[256,512]{1,0:T(8,128)(2,1)S(1)}, bf16[256,512]{1,0:T(8,128)(2,1)S(1)}, u32[]{:S(2)}, u32[]{:S(2)}) collective-permute-start(bf16[256,512]{1,0:T(8,128)(2,1)S(1)} %get-tuple-element.38), channel_id=1, source_target_pairs={{0,5},{1,4},{2,7},{3,6},{4,1},{5,0},{6,3},{7,2},{8,13},{9,12},{10,... | collective-permute-start | bytes 786440 | tf_op jit(solution)/shard_map/ppermute | solution.py:200
  38.3 0.1 collective-permute-start.13
  38.4 2.0 %collective-permute-start.14 = (bf16[256,512]{1,0:T(8,128)(2,1)S(1)}, bf16[256,512]{1,0:T(8,128)(2,1)S(1)}, u32[]{:S(2)}, u32[]{:S(2)}) collective-permute-start(bf16[256,512]{1,0:T(8,128)(2,1)S(1)} %get-tuple-element.40), channel_id=1, source_target_pairs={{0,1},{1,0},{2,6},{3,7},{4,5},{5,4},{6,2},{7,3},{8,9},{9,8},{10,14... | collective-permute-start | bytes 786440 | tf_op jit(solution)/shard_map/ppermute | solution.py:200
  40.4 8.9 %attend.3 = (bf16[128,1024]{1,0:T(8,128)(2,1)S(1)}, bf16[128,1024]{1,0:T(8,128)(2,1)S(1)}, f32[256,512]{1,0:T(8,128)S(1)}, f32[256,512]{1,0:T(8,128)S(1)}, bf16[...) custom-call(s32[2]{0:T(128)S(1)} %pad_add_fusion.where_ref, s32[24]{0:T(128)S(1)} %reshape.9.rand_ref, ...), custom_call_target="tpu_custom_call" | custom-call | flops 5368709120 | bytes 4194304 | tf_op jit(solution)/shard_map/attend/pallas_call | solution.py:406
  49.3 0.1 collective-permute-start.16
  49.4 0.0 collective-permute-start.11
  49.5 0.5 collective-permute-start.7
  50.0 0.1 add_convert_fusion.4
  50.1 0.1 collective-permute-start.15
  50.3 7.6 %collective-permute-done.16 = bf16[256,512]{1,0:T(8,128)(2,1)S(1)} collective-permute-done((bf16[256,512]{1,0:T(8,128)(2,1)S(1)}, bf16[256,512]{1,0:T(8,128)(2,1)S(1)}, u32[]{:S(2)}, u32[]{:S(2)}) %collective-permute-start.16) | collective-permute-done | bytes 262176 | tf_op jit(solution)/shard_map/ppermute | solution.py:200
  57.9 0.1 add_convert_fusion
  57.9 1.3 %collective-permute-start.17 = (bf16[256,512]{1,0:T(8,128)(2,1)S(1)}, bf16[256,512]{1,0:T(8,128)(2,1)S(1)}, u32[]{:S(2)}, u32[]{:S(2)}) collective-permute-start(bf16[256,512]{1,0:T(8,128)(2,1)S(1)} %add_convert_fusion), channel_id=1, source_target_pairs={{0,4},{1,5},{2,3},{3,2},{4,0},{5,1},{6,7},{7,6},{8,12},{9,13},{10,... | collective-permute-start | bytes 786440 | tf_op jit(solution)/shard_map/ppermute | solution.py:200
  59.3 0.0 copy-start.4
  59.3 0.7 copy-done.3
  60.0 0.1 copy-done.4
  60.0 2.9 %place_queries.1 = bf16[128,4096]{1,0:T(8,128)(2,1)} custom-call(s32[2]{0:T(128)} %copy-done.2, bf16[128,1024]{1,0:T(8,128)(2,1)} %copy-done, bf16[128,1024]{1,0:T(8,128)(2,1)} %copy-done.4, bf16[128,1024]{1,0:T(8,128)(2,1)} %copy-done.1, bf16[128,1024]{1,0:T(8,128)(2,1)} %copy-done.3), custom_call_target="tpu_custom_call" | custom-call | bytes 1048576 | tf_op jit(solution)/shard_map/place_queries/pallas_call | solution.py:450
  62.9 1.4 %collective-permute-done.17 = bf16[256,512]{1,0:T(8,128)(2,1)S(1)} collective-permute-done((bf16[256,512]{1,0:T(8,128)(2,1)S(1)}, bf16[256,512]{1,0:T(8,128)(2,1)S(1)}, u32[]{:S(2)}, u32[]{:S(2)}) %collective-permute-start.17) | collective-permute-done | bytes 262176 | tf_op jit(solution)/shard_map/ppermute | solution.py:200
  64.4 1.2 %collective-permute-done.18 = bf16[256,512]{1,0:T(8,128)(2,1)S(1)} collective-permute-done((bf16[256,512]{1,0:T(8,128)(2,1)S(1)}, bf16[256,512]{1,0:T(8,128)(2,1)S(1)}, u32[]{:S(2)}, u32[]{:S(2)}) %collective-permute-start.18) | collective-permute-done | bytes 262176 | tf_op jit(solution)/shard_map/ppermute | solution.py:200
  65.6 0.1 add_convert_fusion.2
  65.7 0.1 collective-permute-start.19
  65.8 1.3 %collective-permute-done.19 = bf16[128,512]{1,0:T(8,128)(2,1)S(1)} collective-permute-done((bf16[128,512]{1,0:T(8,128)(2,1)S(1)}, bf16[128,512]{1,0:T(8,128)(2,1)S(1)}, u32[]{:S(2)}, u32[]{:S(2)}) %collective-permute-start.19) | collective-permute-done | bytes 131104 | tf_op jit(solution)/shard_map/ppermute | solution.py:200
  67.4 0.0 copy-start.5
  67.5 0.6 copy-done.5
  68.1 0.1 copy-done.6
  (32 shorter events, 0.4 us)
Async XLA Ops:
  0.6 3.9 %copy-start.8 = (bf16[128,4096]{1,0:T(8,128)(2,1)S(1)}, bf16[128,4096]{1,0:T(8,128)(2,1)}, u32[]{:S(2)}) copy-start(bf16[128,4096]{1,0:T(8,128)(2,1)} %q_ref.1) | copy-start | bytes 3145732
  0.6 1.9 %collective-permute-start = (bf16[128,1024]{1,0:T(8,128)(2,1)}, bf16[128,1024]{1,0:T(8,128)(2,1)S(1)}, u32[]{:S(2)}, u32[]{:S(2)}) collective-permute-start(bf16[128,1024]{1,0:T(8,128)(2,1)} %k_ref.1), channel_id=1, source_target_pairs={{0,2},{1,3},{2,0},{3,1},{4,6},{5,7},{6,4},{7,5},{8,10},{9,11},{10,... | collective-permute-start | bytes 786440 | tf_op jit(solution)/shard_map/ppermute | solution.py:200
  1.2 1.7 %collective-permute-start.1 = (bf16[128,1024]{1,0:T(8,128)(2,1)}, bf16[128,1024]{1,0:T(8,128)(2,1)S(1)}, u32[]{:S(2)}, u32[]{:S(2)}) collective-permute-start(bf16[128,1024]{1,0:T(8,128)(2,1)} %v_ref.1), channel_id=1, source_target_pairs={{0,2},{1,3},{2,0},{3,1},{4,6},{5,7},{6,4},{7,5},{8,10},{9,11},{10,... | collective-permute-start | bytes 786440 | tf_op jit(solution)/shard_map/ppermute | solution.py:200
  1.3 39.0 %copy-start.2 = (s32[2]{0:T(128)}, s32[2]{0:T(128)S(1)}, u32[]{:S(2)}) copy-start(s32[2]{0:T(128)S(1)} %pad_add_fusion.where_ref) | copy-start | bytes 28
  4.5 13.0 %copy-start.7 = (s32[8,3]{0,1:T(4,128)S(1)}, s32[8,3]{0,1:T(4,128)}, u32[]{:S(2)}) copy-start(s32[8,3]{0,1:T(4,128)} %param.9) | copy-start | bytes 292
  4.5 22.7 %collective-permute-start.2 = (bf16[128,4096]{1,0:T(8,128)(2,1)S(1)}, bf16[128,4096]{1,0:T(8,128)(2,1)}, u32[]{:S(2)}, u32[]{:S(2)}) collective-permute-start(bf16[128,4096]{1,0:T(8,128)(2,1)S(1)} %copy-done.8), channel_id=1, source_target_pairs={{0,2},{1,3},{2,0},{3,1},{4,6},{5,7},{6,4},{7,5},{8,10},{9,11},{10,... | collective-permute-start | bytes 3145736 | tf_op jit(solution)/shard_map/ppermute | solution.py:200
  5.0 22.3 %collective-permute-start.3 = (bf16[128,4096]{1,0:T(8,128)(2,1)}, bf16[128,4096]{1,0:T(8,128)(2,1)}, u32[]{:S(2)}, u32[]{:S(2)}) collective-permute-start(bf16[128,4096]{1,0:T(8,128)(2,1)} %do_ref.1), channel_id=1, source_target_pairs={{0,2},{1,3},{2,0},{3,1},{4,6},{5,7},{6,4},{7,5},{8,10},{9,11},{10,... | collective-permute-start | bytes 3145736 | tf_op jit(solution)/shard_map/ppermute | solution.py:200
  5.1 9.1 %collective-permute-start.8 = (bf16[256,512]{1,0:T(8,128)(2,1)S(1)}, bf16[256,512]{1,0:T(8,128)(2,1)S(1)}, u32[]{:S(2)}, u32[]{:S(2)}) collective-permute-start(bf16[256,512]{1,0:T(8,128)(2,1)S(1)} %get-tuple-element.33.pair_ref), channel_id=1, source_target_pairs={{0,4},{1,5},{2,3},{3,2},{4,0},{5,1},{6,7},{7,6},{8,12},{9,13},{10,... | collective-permute-start | bytes 786440 | tf_op jit(solution)/shard_map/ppermute | solution.py:200
  8.0 11.8 %collective-permute-start.4 = (bf16[256,512]{1,0:T(8,128)(2,1)S(1)}, bf16[256,512]{1,0:T(8,128)(2,1)S(1)}, u32[]{:S(2)}, u32[]{:S(2)}) collective-permute-start(bf16[256,512]{1,0:T(8,128)(2,1)S(1)} %get-tuple-element.30.pair_ref), channel_id=1, source_target_pairs={{0,4},{1,5},{2,3},{3,2},{4,0},{5,1},{6,7},{7,6},{8,12},{9,13},{10,... | collective-permute-start | bytes 786440 | tf_op jit(solution)/shard_map/ppermute | solution.py:200
  8.0 14.2 %collective-permute-start.5 = (bf16[256,512]{1,0:T(8,128)(2,1)S(1)}, bf16[256,512]{1,0:T(8,128)(2,1)S(1)}, u32[]{:S(2)}, u32[]{:S(2)}) collective-permute-start(bf16[256,512]{1,0:T(8,128)(2,1)S(1)} %get-tuple-element.30.pair_ref), channel_id=1, source_target_pairs={{0,1},{1,0},{2,6},{3,7},{4,5},{5,4},{6,2},{7,3},{8,9},{9,8},{10,14... | collective-permute-start | bytes 786440 | tf_op jit(solution)/shard_map/ppermute | solution.py:200
  14.1 13.1 %collective-permute-start.6 = (bf16[256,512]{1,0:T(8,128)(2,1)S(1)}, bf16[256,512]{1,0:T(8,128)(2,1)S(1)}, u32[]{:S(2)}, u32[]{:S(2)}) collective-permute-start(bf16[256,512]{1,0:T(8,128)(2,1)S(1)} %get-tuple-element.30.pair_ref), channel_id=1, source_target_pairs={{0,5},{1,4},{2,7},{3,6},{4,1},{5,0},{6,3},{7,2},{8,13},{9,12},{10,... | collective-permute-start | bytes 786440 | tf_op jit(solution)/shard_map/ppermute | solution.py:200
  19.8 20.6 %collective-permute-start.9 = (bf16[256,512]{1,0:T(8,128)(2,1)S(1)}, bf16[256,512]{1,0:T(8,128)(2,1)S(1)}, u32[]{:S(2)}, u32[]{:S(2)}) collective-permute-start(bf16[256,512]{1,0:T(8,128)(2,1)S(1)} %get-tuple-element.33.pair_ref), channel_id=1, source_target_pairs={{0,1},{1,0},{2,6},{3,7},{4,5},{5,4},{6,2},{7,3},{8,9},{9,8},{10,14... | collective-permute-start | bytes 786440 | tf_op jit(solution)/shard_map/ppermute | solution.py:200
  22.2 18.1 %collective-permute-start.10 = (bf16[256,512]{1,0:T(8,128)(2,1)S(1)}, bf16[256,512]{1,0:T(8,128)(2,1)S(1)}, u32[]{:S(2)}, u32[]{:S(2)}) collective-permute-start(bf16[256,512]{1,0:T(8,128)(2,1)S(1)} %collective-permute-done.8.near_ref), channel_id=1, source_target_pairs={{0,1},{1,0},{2,6},{3,7},{4,5},{5,4},{6,2},{7,3},{8,9},{9,8},{10,14... | collective-permute-start | bytes 786440 | tf_op jit(solution)/shard_map/ppermute | solution.py:200
  36.1 0.7 %copy-start = (bf16[128,1024]{1,0:T(8,128)(2,1)}, bf16[128,1024]{1,0:T(8,128)(2,1)S(1)}, u32[]{:S(2)}) copy-start(bf16[128,1024]{1,0:T(8,128)(2,1)S(1)} %get-tuple-element.31.refs_0_) | copy-start | bytes 786436
  36.9 12.6 %collective-permute-start.12 = (bf16[256,512]{1,0:T(8,128)(2,1)S(1)}, bf16[256,512]{1,0:T(8,128)(2,1)S(1)}, u32[]{:S(2)}, u32[]{:S(2)}) collective-permute-start(bf16[256,512]{1,0:T(8,128)(2,1)S(1)} %get-tuple-element.38), channel_id=1, source_target_pairs={{0,5},{1,4},{2,7},{3,6},{4,1},{5,0},{6,3},{7,2},{8,13},{9,12},{10,... | collective-permute-start | bytes 786440 | tf_op jit(solution)/shard_map/ppermute | solution.py:200
  38.3 11.7 %collective-permute-start.13 = (bf16[256,512]{1,0:T(8,128)(2,1)S(1)}, bf16[256,512]{1,0:T(8,128)(2,1)S(1)}, u32[]{:S(2)}, u32[]{:S(2)}) collective-permute-start(bf16[256,512]{1,0:T(8,128)(2,1)S(1)} %get-tuple-element.39), channel_id=1, source_target_pairs={{0,4},{1,5},{2,3},{3,2},{4,0},{5,1},{6,7},{7,6},{8,12},{9,13},{10,... | collective-permute-start | bytes 786440 | tf_op jit(solution)/shard_map/ppermute | solution.py:200
  38.4 11.6 %collective-permute-start.14 = (bf16[256,512]{1,0:T(8,128)(2,1)S(1)}, bf16[256,512]{1,0:T(8,128)(2,1)S(1)}, u32[]{:S(2)}, u32[]{:S(2)}) collective-permute-start(bf16[256,512]{1,0:T(8,128)(2,1)S(1)} %get-tuple-element.40), channel_id=1, source_target_pairs={{0,1},{1,0},{2,6},{3,7},{4,5},{5,4},{6,2},{7,3},{8,9},{9,8},{10,14... | collective-permute-start | bytes 786440 | tf_op jit(solution)/shard_map/ppermute | solution.py:200
  49.3 0.8 %copy-start.1 = (bf16[128,1024]{1,0:T(8,128)(2,1)}, bf16[128,1024]{1,0:T(8,128)(2,1)S(1)}, u32[]{:S(2)}) copy-start(bf16[128,1024]{1,0:T(8,128)(2,1)S(1)} %get-tuple-element.34.refs_2_) | copy-start | bytes 786436
  49.3 8.6 %collective-permute-start.16 = (bf16[256,512]{1,0:T(8,128)(2,1)S(1)}, bf16[256,512]{1,0:T(8,128)(2,1)S(1)}, u32[]{:S(2)}, u32[]{:S(2)}) collective-permute-start(bf16[256,512]{1,0:T(8,128)(2,1)S(1)} %get-tuple-element.47), channel_id=1, source_target_pairs={{0,1},{1,0},{2,6},{3,7},{4,5},{5,4},{6,2},{7,3},{8,9},{9,8},{10,14... | collective-permute-start | bytes 786440 | tf_op jit(solution)/shard_map/ppermute | solution.py:200
  49.4 9.9 %collective-permute-start.11 = (bf16[128,1024]{1,0:T(8,128)(2,1)S(1)}, bf16[128,1024]{1,0:T(8,128)(2,1)S(1)}, u32[]{:S(2)}, u32[]{:S(2)}) collective-permute-start(bf16[128,1024]{1,0:T(8,128)(2,1)S(1)} %get-tuple-element.35), channel_id=1, source_target_pairs={{0,2},{1,3},{2,0},{3,1},{4,6},{5,7},{6,4},{7,5},{8,10},{9,11},{10,... | collective-permute-start | bytes 786440 | tf_op jit(solution)/shard_map/ppermute | solution.py:200
  49.5 9.8 %collective-permute-start.7 = (bf16[128,1024]{1,0:T(8,128)(2,1)S(1)}, bf16[128,1024]{1,0:T(8,128)(2,1)S(1)}, u32[]{:S(2)}, u32[]{:S(2)}) collective-permute-start(bf16[128,1024]{1,0:T(8,128)(2,1)S(1)} %get-tuple-element.32), channel_id=1, source_target_pairs={{0,2},{1,3},{2,0},{3,1},{4,6},{5,7},{6,4},{7,5},{8,10},{9,11},{10,... | collective-permute-start | bytes 786440 | tf_op jit(solution)/shard_map/ppermute | solution.py:200
  50.1 12.8 %collective-permute-start.15 = (bf16[128,512]{1,0:T(8,128)(2,1)S(1)}, bf16[128,512]{1,0:T(8,128)(2,1)S(1)}, u32[]{:S(2)}, u32[]{:S(2)}) collective-permute-start(bf16[128,512]{1,0:T(8,128)(2,1)S(1)} %get-tuple-element.50), channel_id=1, source_target_pairs={{0,2},{1,3},{2,0},{3,1},{4,6},{5,7},{6,4},{7,5},{8,10},{9,11},{10,... | collective-permute-start | bytes 393224 | tf_op jit(solution)/shard_map/ppermute | solution.py:200
  57.9 6.4 %collective-permute-start.17 = (bf16[256,512]{1,0:T(8,128)(2,1)S(1)}, bf16[256,512]{1,0:T(8,128)(2,1)S(1)}, u32[]{:S(2)}, u32[]{:S(2)}) collective-permute-start(bf16[256,512]{1,0:T(8,128)(2,1)S(1)} %add_convert_fusion), channel_id=1, source_target_pairs={{0,4},{1,5},{2,3},{3,2},{4,0},{5,1},{6,7},{7,6},{8,12},{9,13},{10,... | collective-permute-start | bytes 786440 | tf_op jit(solution)/shard_map/ppermute | solution.py:200
  59.2 6.4 %collective-permute-start.18 = (bf16[256,512]{1,0:T(8,128)(2,1)S(1)}, bf16[256,512]{1,0:T(8,128)(2,1)S(1)}, u32[]{:S(2)}, u32[]{:S(2)}) collective-permute-start(bf16[256,512]{1,0:T(8,128)(2,1)S(1)} %get-tuple-element.48), channel_id=1, source_target_pairs={{0,1},{1,0},{2,6},{3,7},{4,5},{5,4},{6,2},{7,3},{8,9},{9,8},{10,14... | collective-permute-start | bytes 786440 | tf_op jit(solution)/shard_map/ppermute | solution.py:200
  59.3 0.7 %copy-start.3 = (bf16[128,1024]{1,0:T(8,128)(2,1)}, bf16[128,1024]{1,0:T(8,128)(2,1)S(1)}, u32[]{:S(2)}) copy-start(bf16[128,1024]{1,0:T(8,128)(2,1)S(1)} %collective-permute-done.11.refs_3_) | copy-start | bytes 786436
  59.3 0.8 %copy-start.4 = (bf16[128,1024]{1,0:T(8,128)(2,1)}, bf16[128,1024]{1,0:T(8,128)(2,1)S(1)}, u32[]{:S(2)}) copy-start(bf16[128,1024]{1,0:T(8,128)(2,1)S(1)} %collective-permute-done.7.refs_1_) | copy-start | bytes 786436
  65.7 1.4 %collective-permute-start.19 = (bf16[128,512]{1,0:T(8,128)(2,1)S(1)}, bf16[128,512]{1,0:T(8,128)(2,1)S(1)}, u32[]{:S(2)}, u32[]{:S(2)}) collective-permute-start(bf16[128,512]{1,0:T(8,128)(2,1)S(1)} %get-tuple-element.52), channel_id=1, source_target_pairs={{0,2},{1,3},{2,0},{3,1},{4,6},{5,7},{6,4},{7,5},{8,10},{9,11},{10,... | collective-permute-start | bytes 393224 | tf_op jit(solution)/shard_map/ppermute | solution.py:200
  67.4 0.7 %copy-start.5 = (bf16[128,1024]{1,0:T(8,128)(2,1)}, bf16[128,1024]{1,0:T(8,128)(2,1)S(1)}, u32[]{:S(2)}) copy-start(bf16[128,1024]{1,0:T(8,128)(2,1)S(1)} %get-tuple-element.53) | copy-start | bytes 786436
  67.5 0.7 %copy-start.6 = (bf16[128,1024]{1,0:T(8,128)(2,1)}, bf16[128,1024]{1,0:T(8,128)(2,1)S(1)}, u32[]{:S(2)}) copy-start(bf16[128,1024]{1,0:T(8,128)(2,1)S(1)} %constant_dynamic-update-slice_fusion) | copy-start | bytes 786436
